TPU v7x, 32 devices: a whole 2x2x4 slice. The times are simulated.
32 devices in a mesh: groups: 2 (over y), wide: 4 (over z), narrow: 4 (over x, core).
Axes of the slice: x: 2, y: 2, z: 4, core: 2. Of those that a mesh axis runs over, the one named last changes fastest.
Arguments:
- populations: float32 [19, 96, 192, 128], P(None, ('groups', 'wide'), 'narrow'), parts along dimension 1, may hold values from 0.008 to 0.57, as said below
- flags: int32 [96, 192, 128], P(('groups', 'wide'), 'narrow'), parts along dimension 0, may hold values from 0 to 3, as said below
- potential: float32 [24, 48, 32], P(('groups', 'wide'), 'narrow'), parts along dimension 0, may hold values from -6 to 6
- conductivity: float32 [24, 48, 32], P(('groups', 'wide'), 'narrow'), parts along dimension 0, may hold values from 0.5 to 2
- coil_phase: int32 [24, 48, 32], P(('groups', 'wide'), 'narrow'), parts along dimension 0, may hold values from 0 to 2
- phase_table: float32 [3, 4], replicated, may hold values from -4 to 4
- magnetic: float32 [3, 24, 48, 32], P(None, ('groups', 'wide'), 'narrow'), parts along dimension 1, may hold values from -6 to 6
Outputs:
- populations_out: float32 [19, 96, 192, 128], P(None, ('groups', 'wide'), 'narrow'), parts along dimension 1
- potential_out: float32 [24, 48, 32], P(('groups', 'wide'), 'narrow'), parts along dimension 0
- lorentz: float32 [3, 24, 48, 32], P(None, ('groups', 'wide'), 'narrow'), parts along dimension 1
There are 2 independent parts, one for each index of `groups`. A program takes and returns all parts, laid end to end along the dimension named above; an argument that names none is the same for every part. Nothing has to cross between parts.
Inputs may be any that keep to these rules, and one draw needn't show every extreme that they name: flags: 0 fluid, 1 wall, 2 inlet, 3 outlet. `populations`: each population is its lattice weight times a positive factor.
All inputs are finite; a program needn't handle non-finite values.
Results may differ from a plain program's by a relative error of at most 0.00002.
Values sent between devices are 32-bit elements; how exact they have to be, the bound alone decides.
No kernel may reach another device: no remote copies, remote signals or barrier semaphores. Data moves between devices by JAX's collectives and lax.ppermute only.
A program may use at most 64 MiB of HBM per device.

v0:
```python
import jax
import jax.numpy as jnp
from jax import lax
from jax.sharding import PartitionSpec as P

SWEEPS = 2


lattice_dirs = [
    (0, 0, 0),
    (1, 0, 0),
    (-1, 0, 0),
    (0, 1, 0),
    (0, -1, 0),
    (0, 0, 1),
    (0, 0, -1),
    (1, 1, 0),
    (-1, -1, 0),
    (1, -1, 0),
    (-1, 1, 0),
    (1, 0, 1),
    (-1, 0, -1),
    (1, 0, -1),
    (-1, 0, 1),
    (0, 1, 1),
    (0, -1, -1),
    (0, 1, -1),
    (0, -1, 1),
]
opposite_dir = [0, 2, 1, 4, 3, 6, 5, 8, 7, 10, 9, 12, 11, 14, 13, 16, 15, 18, 17]
lattice_weights = [1.0 / 3.0] + [1.0 / 18.0] * 6 + [1.0 / 36.0] * 12
relax_time = 0.8
force_scale = 0.02
inlet_speed = 0.05


def extended(x, sides, width):
    for axis, dim in sides:
        size, length = (lax.axis_size(axis), x.shape[dim])
        up = [(i, (i + 1) % size) for i in range(size - 1)]
        down = [(j, i) for i, j in up]
        last = lax.slice_in_dim(x, length - width, length, axis=dim)
        first = lax.slice_in_dim(x, 0, width, axis=dim)
        before = lax.ppermute(last, axis, up)
        after = lax.ppermute(first, axis, down)
        x = jnp.concatenate([before, x, after], axis=dim)
    return x


def phase_lookup(coil_phase, phase_table, column):
    summed = jnp.zeros(coil_phase.shape, jnp.float32)
    for phase in range(3):
        summed = summed + jnp.where(
            coil_phase == phase, phase_table[phase, column], jnp.float32(0.0)
        )
    return summed


def jacobi_sweep(padded, source):
    beside_all = padded[2:, 1:-1, 1:-1] + padded[:-2, 1:-1, 1:-1]
    beside_all = beside_all + padded[1:-1, 2:, 1:-1] + padded[1:-1, :-2, 1:-1]
    beside_all = beside_all + padded[1:-1, 1:-1, 2:] + padded[1:-1, 1:-1, :-2]
    return (beside_all + source) / 6.0


def gradients(padded):
    grad_z = (padded[2:, 1:-1, 1:-1] - padded[:-2, 1:-1, 1:-1]) * 0.5
    grad_y = (padded[1:-1, 2:, 1:-1] - padded[1:-1, :-2, 1:-1]) * 0.5
    grad_x = (padded[1:-1, 1:-1, 2:] - padded[1:-1, 1:-1, :-2]) * 0.5
    return (grad_x, grad_y, grad_z)


def lorentz_from(grad_x, grad_y, grad_z, conductivity, coil_phase, phase_table, magnetic):
    cur_x = conductivity * (phase_lookup(coil_phase, phase_table, 1) - grad_x)
    cur_y = conductivity * (phase_lookup(coil_phase, phase_table, 2) - grad_y)
    cur_z = conductivity * (phase_lookup(coil_phase, phase_table, 3) - grad_z)
    field_x, field_y, field_z = (magnetic[0], magnetic[1], magnetic[2])
    return jnp.stack(
        [
            cur_y * field_z - cur_z * field_y,
            cur_z * field_x - cur_x * field_z,
            cur_x * field_y - cur_y * field_x,
        ]
    )


def upsample(lorentz):
    grown = jnp.repeat(jnp.repeat(jnp.repeat(lorentz, 4, axis=1), 4, axis=2), 4, axis=3)
    return grown * force_scale


def collide(popul, flags, force):
    density = jnp.sum(popul, axis=0)
    force_x, force_y, force_z = (force[0], force[1], force[2])
    mom_x = jnp.zeros_like(density)
    mom_y = jnp.zeros_like(density)
    mom_z = jnp.zeros_like(density)
    for number in range(19):
        step_x, step_y, step_z = lattice_dirs[number]
        if step_x != 0:
            mom_x = mom_x + step_x * popul[number]
        if step_y != 0:
            mom_y = mom_y + step_y * popul[number]
        if step_z != 0:
            mom_z = mom_z + step_z * popul[number]
    vel_x = (mom_x + 0.5 * force_x) / density
    vel_y = (mom_y + 0.5 * force_y) / density
    vel_z = (mom_z + 0.5 * force_z) / density
    speed_sq = vel_x * vel_x + vel_y * vel_y + vel_z * vel_z
    factor = 1.0 - 0.5 / relax_time
    merged = []
    for number in range(19):
        step_x, step_y, step_z = lattice_dirs[number]
        weight = lattice_weights[number]
        along_u = step_x * vel_x + step_y * vel_y + step_z * vel_z
        along_f = step_x * force_x + step_y * force_y + step_z * force_z
        shape_eq = 1.0 + 3.0 * along_u + 4.5 * along_u * along_u - 1.5 * speed_sq
        balanced = weight * density * shape_eq
        forcing = (
            factor
            * weight
            * (
                3.0
                * (
                    (step_x - vel_x) * force_x
                    + (step_y - vel_y) * force_y
                    + (step_z - vel_z) * force_z
                )
                + 9.0 * along_u * along_f
            )
        )
        relaxed = popul[number] - (popul[number] - balanced) / relax_time + forcing
        outflow = weight * shape_eq
        along_in = -step_z * inlet_speed
        inflow = jnp.full_like(
            density,
            weight
            * (1.0 + 3.0 * along_in + 4.5 * along_in * along_in - 1.5 * inlet_speed * inlet_speed),
        )
        chosen = jnp.where(
            flags == 0,
            relaxed,
            jnp.where(flags == 2, inflow, jnp.where(flags == 3, outflow, popul[number])),
        )
        merged.append(chosen)
    return jnp.stack(merged)


def bounce_back(post, pulled, open_pad, flags):
    size_z, size_y, size_x = flags.shape
    merged = []
    for number in range(19):
        step_x, step_y, step_z = lattice_dirs[number]
        open_src = open_pad[
            1 - step_z : 1 - step_z + size_z,
            1 - step_y : 1 - step_y + size_y,
            1 - step_x : 1 - step_x + size_x,
        ]
        read = jnp.where(open_src == 1, pulled[number], post[opposite_dir[number]])
        merged.append(jnp.where(flags == 1, post[number], read))
    return jnp.stack(merged)


def pull_padded(post_pad, shape):
    size_z, size_y, size_x = shape
    pulled = []
    for number in range(19):
        step_x, step_y, step_z = lattice_dirs[number]
        pulled.append(
            post_pad[
                number,
                1 - step_z : 1 - step_z + size_z,
                1 - step_y : 1 - step_y + size_y,
                1 - step_x : 1 - step_x + size_x,
            ]
        )
    return pulled


def rimmed_field(potential_now):
    padded = extended(potential_now, (("wide", 0), ("narrow", 1)), 1)
    return jnp.pad(padded, ((0, 0), (0, 0), (1, 1)))


def per_device(populations, flags, potential, conductivity, coil_phase, phase_table, magnetic):
    source = conductivity * phase_lookup(coil_phase, phase_table, 0)
    potential_now = potential
    for counter in range(SWEEPS):
        potential_now = jacobi_sweep(rimmed_field(potential_now), source)
    grad_x, grad_y, grad_z = gradients(rimmed_field(potential_now))
    lorentz = lorentz_from(grad_x, grad_y, grad_z, conductivity, coil_phase, phase_table, magnetic)
    force = upsample(lorentz)
    post = collide(populations, flags, force)
    open_cells = (flags != 1).astype(jnp.int32)
    open_rim = extended(open_cells, (("wide", 0), ("narrow", 1)), 1)
    open_pad = jnp.pad(open_rim, ((0, 0), (0, 0), (1, 1)))
    post_pad = extended(post, (("wide", 1), ("narrow", 2)), 1)
    post_pad = jnp.pad(post_pad, ((0, 0), (0, 0), (0, 0), (1, 1)))
    pulled = pull_padded(post_pad, flags.shape)
    result = bounce_back(post, pulled, open_pad, flags)
    return (result, potential_now, lorentz)


def solution(mesh):
    in_specs = (
        P(None, ("groups", "wide"), "narrow", None),
        P(("groups", "wide"), "narrow", None),
        P(("groups", "wide"), "narrow", None),
        P(("groups", "wide"), "narrow", None),
        P(("groups", "wide"), "narrow", None),
        P(),
        P(None, ("groups", "wide"), "narrow", None),
    )
    out_specs = (
        P(None, ("groups", "wide"), "narrow", None),
        P(("groups", "wide"), "narrow", None),
        P(None, ("groups", "wide"), "narrow", None),
    )
    return jax.shard_map(
        per_device, mesh=mesh, in_specs=in_specs, out_specs=out_specs, check_vma=False
    )
```

profile of v0, /device:TPU:1, one launch (start us, length us, event | category | flops | bytes accessed | tf_op | source)
XLA Modules:
  0.0 130.5 jit_solution(6515704023656254585)
XLA Ops:
  0.7 0.8 fusion.295
  1.4 4.0 %collective-permute-start.1 = (f32[1,12,32]{2,1,0:T(8,128)S(1)}, f32[1,12,32]{2,1,0:T(8,128)S(1)}, u32[]{:S(2)}, u32[]{:S(2)}) collective-permute-start(f32[1,12,32]{2,1,0:T(8,128)S(1)} %get-tuple-element.96), channel_id=1, source_target_pairs={{0,4},{4,8},{8,12},{1,5},{5,9},{9,13},{2,6},{6,10},{10,14},{3,7},{... | collective-permute-start | bytes 4616 | tf_op jit(solution)/shard_map/ppermute | solution.py:44
  5.4 1.3 collective-permute-start
  6.7 0.7 constant_dynamic-update-slice_fusion.1
  7.5 2.3 %collective-permute-done = f32[1,12,32]{2,1,0:T(8,128)S(1)} collective-permute-done((f32[1,12,32]{2,1,0:T(8,128)S(1)}, f32[1,12,32]{2,1,0:T(8,128)S(1)}, u32[]{:S(2)}, u32[]{:S(2)}) %collective-permute-start) | collective-permute-done | bytes 1568 | tf_op jit(solution)/shard_map/ppermute | solution.py:45
  9.8 4.0 %collective-permute-start.2 = (f32[5,1,32]{2,1,0:T(1,128)S(1)}, f32[5,1,32]{2,1,0:T(1,128)S(1)}, u32[]{:S(2)}, u32[]{:S(2)}) collective-permute-start(f32[5,1,32]{2,1,0:T(1,128)S(1)} %get-tuple-element.90), channel_id=1, source_target_pairs={{1,0},{2,1},{3,2},{5,4},{6,5},{7,6},{9,8},{10,9},{11,10},{13,12},{... | collective-permute-start | bytes 1928 | tf_op jit(solution)/shard_map/ppermute | solution.py:45
  13.9 3.0 %collective-permute-start.3 = (f32[5,1,32]{2,1,0:T(1,128)S(1)}, f32[5,1,32]{2,1,0:T(1,128)S(1)}, u32[]{:S(2)}, u32[]{:S(2)}) collective-permute-start(f32[5,1,32]{2,1,0:T(1,128)S(1)} %get-tuple-element.89), channel_id=1, source_target_pairs={{0,1},{1,2},{2,3},{4,5},{5,6},{6,7},{8,9},{9,10},{10,11},{12,13},{... | collective-permute-start | bytes 1928 | tf_op jit(solution)/shard_map/ppermute | solution.py:44
  16.9 1.8 %fusion.296 = (f32[1,1]{1,0:T(1,128)}, f32[1,1]{1,0:T(1,128)}, f32[1,1]{1,0:T(1,128)}, f32[1,1]{1,0:T(1,128)}, f32[1,1]{1,0:T(1,128)}, /*index=5*/f32[1,1]{1,0:T...) fusion(f32[3,4]{1,0:T(4,128)} %param.12), kind=kLoop, calls=%fused_computation.524 | loop fusion | bytes 96 | tf_op jit(solution)/shard_map/slice | solution.py:54
  18.8 2.8 %fusion.252 = (f32[3,12,32]{2,1,0:T(8,128)S(1)}, pred[3,12,32]{2,1,0:T(8,128)(4,1)S(1)}, pred[3,12,32]{2,1,0:T(8,128)(4,1)S(1)}, pred[3,12,32]{2,1,0:T(8,128)(4,1)S(1)}) fusion(f32[5,14,34]{2,1,0:T(8,128)S(1)} %select_maximum_fusion.12, f32[5,12,32]{2,1,0:T(8,128)S(1)} %constant_dynamic-update-slice_fusion, f32[5,1,32]{2,1,0:T(1,128)S(1)} %collective-permute-done.3, ...), kind=kLoop, calls=%fused_computation.484 | loop fusion | flops 23040 | bytes 43148 | tf_op jit(solution)/shard_map/div | solution.py:63
  21.6 1.3 collective-permute-start.4
  22.9 4.0 %collective-permute-start.5 = (f32[1,12,32]{2,1,0:T(8,128)S(1)}, f32[1,12,32]{2,1,0:T(8,128)S(1)}, u32[]{:S(2)}, u32[]{:S(2)}) collective-permute-start(f32[1,12,32]{2,1,0:T(8,128)S(1)} %get-tuple-element.93), channel_id=1, source_target_pairs={{0,4},{4,8},{8,12},{1,5},{5,9},{9,13},{2,6},{6,10},{10,14},{3,7},{... | collective-permute-start | bytes 4616 | tf_op jit(solution)/shard_map/ppermute | solution.py:44
  26.9 0.8 collective-permute-done.5
  27.7 2.4 %collective-permute-start.6 = (f32[5,1,32]{2,1,0:T(1,128)S(1)}, f32[5,1,32]{2,1,0:T(1,128)S(1)}, u32[]{:S(2)}, u32[]{:S(2)}) collective-permute-start(f32[5,1,32]{2,1,0:T(1,128)S(1)} %get-tuple-element.88), channel_id=1, source_target_pairs={{1,0},{2,1},{3,2},{5,4},{6,5},{7,6},{9,8},{10,9},{11,10},{13,12},{... | collective-permute-start | bytes 1928 | tf_op jit(solution)/shard_map/ppermute | solution.py:45
  30.1 3.7 %collective-permute-start.7 = (f32[5,1,32]{2,1,0:T(1,128)S(1)}, f32[5,1,32]{2,1,0:T(1,128)S(1)}, u32[]{:S(2)}, u32[]{:S(2)}) collective-permute-start(f32[5,1,32]{2,1,0:T(1,128)S(1)} %get-tuple-element.87), channel_id=1, source_target_pairs={{0,1},{1,2},{2,3},{4,5},{5,6},{6,7},{8,9},{9,10},{10,11},{12,13},{... | collective-permute-start | bytes 1928 | tf_op jit(solution)/shard_map/ppermute | solution.py:44
  33.8 0.7 collective-permute-done.7
  34.6 2.7 %fusion.247 = f32[3,12,32]{2,1,0:T(8,128)S(1)} fusion(f32[5,14,34]{2,1,0:T(8,128)S(1)} %select_maximum_fusion.8, f32[5,1,32]{2,1,0:T(1,128)S(1)} %collective-permute-done.7, f32[1,12,32]{2,1,0:T(8,128)S(1)} %collective-permute-done.4, f32[3,12,32]{2,1,0:T(8,128)S(1)} %get-tuple-element.68, f32[1,12,32]{2,1,0:T(8,128)S(1)} %collective-permute-done.5, ...), kind=kLoop, calls=%fused_computation.469 | loop fusion | flops 24192 | bytes 30860 | tf_op jit(solution)/shard_map/div | solution.py:63
  37.4 3.9 %collective-permute-start.8 = (f32[1,12,32]{2,1,0:T(8,128)S(1)}, f32[1,12,32]{2,1,0:T(8,128)S(1)}, u32[]{:S(2)}, u32[]{:S(2)}) collective-permute-start(f32[1,12,32]{2,1,0:T(8,128)S(1)} %get-tuple-element.92), channel_id=1, source_target_pairs={{0,4},{4,8},{8,12},{1,5},{5,9},{9,13},{2,6},{6,10},{10,14},{3,7},{... | collective-permute-start | bytes 4616 | tf_op jit(solution)/shard_map/ppermute | solution.py:44
  41.3 1.3 collective-permute-start.9
  42.6 3.1 %collective-permute-done.9 = f32[1,12,32]{2,1,0:T(8,128)S(1)} collective-permute-done((f32[1,12,32]{2,1,0:T(8,128)S(1)}, f32[1,12,32]{2,1,0:T(8,128)S(1)}, u32[]{:S(2)}, u32[]{:S(2)}) %collective-permute-start.9) | collective-permute-done | bytes 1568 | tf_op jit(solution)/shard_map/ppermute | solution.py:45
  45.7 2.2 %collective-permute-start.10 = (f32[5,1,32]{2,1,0:T(1,128)S(1)}, f32[5,1,32]{2,1,0:T(1,128)S(1)}, u32[]{:S(2)}, u32[]{:S(2)}) collective-permute-start(f32[5,1,32]{2,1,0:T(1,128)S(1)} %get-tuple-element.85), channel_id=1, source_target_pairs={{1,0},{2,1},{3,2},{5,4},{6,5},{7,6},{9,8},{10,9},{11,10},{13,12},{... | collective-permute-start | bytes 1928 | tf_op jit(solution)/shard_map/ppermute | solution.py:45
  47.9 5.4 %collective-permute-start.11 = (f32[5,1,32]{2,1,0:T(1,128)S(1)}, f32[5,1,32]{2,1,0:T(1,128)S(1)}, u32[]{:S(2)}, u32[]{:S(2)}) collective-permute-start(f32[5,1,32]{2,1,0:T(1,128)S(1)} %get-tuple-element.86), channel_id=1, source_target_pairs={{0,1},{1,2},{2,3},{4,5},{5,6},{6,7},{8,9},{9,10},{10,11},{12,13},{... | collective-permute-start | bytes 1928 | tf_op jit(solution)/shard_map/ppermute | solution.py:44
  53.3 2.9 %reduce_sum.9 = f32[12,48,128]{2,1,0:T(8,128)S(1)} reduce(f32[19,12,48,128]{3,2,1,0:T(8,128)} %param.7, f32[]{:T(128)} %constant.29.clone.1), dimensions={0}, to_apply=%region_0.1 | reduce | flops 1327104 | bytes 5898244 | tf_op jit(solution)/shard_map/reduce_sum | solution.py:93
  56.3 3.8 %fusion.261 = (f32[1,3,12,32]{3,2,1,0:T(8,128)S(1)}, f32[3,12,32]{2,1,0:T(8,128)S(1)}, f32[3,12,32]{2,1,0:T(8,128)S(1)}) fusion(f32[3,3,12,32]{3,2,1,0:T(8,128)S(1)} %copy-done.4, f32[3,12,32]{2,1,0:T(8,128)S(1)} %copy-done.3, f32[3,12,32]{2,1,0:T(8,128)S(1)} %fusion.247, f32[1,12,32]{2,1,0:T(8,128)S(1)} %collective-permute-done.8, ...), kind=kLoop, calls=%fused_computation.502 | loop fusion | flops 33408 | bytes 40088 | tf_op jit(solution)/shard_map/stack | solution.py:78
  60.1 2.0 %fusion.257 = (f32[1,3,12,32]{3,2,1,0:T(8,128)S(1)}, f32[3,12,32]{2,1,0:T(8,128)S(1)}) fusion(f32[3,12,32]{2,1,0:T(8,128)S(1)} %get-tuple-element.64, f32[3,3,12,32]{3,2,1,0:T(8,128)S(1)} %copy-done.4, f32[3,12,32]{2,1,0:T(8,128)S(1)} %copy-done.3, f32[5,14,34]{2,1,0:T(8,128)S(1)} %select_maximum_fusion.4, pred[3,12,32]{2,1,0:T(8,128)(4,1)S(1)} %get-tuple-element.71, ...), kind=kLoop, calls=%fused_computation.496 | loop fusion | flops 13824 | bytes 40332 | tf_op jit(solution)/shard_map/stack | solution.py:78
  62.1 0.6 broadcast_multiply_fusion.1
  64.6 3.6 %fusion.228 = (f32[12,48,128]{2,1,0:T(8,128)S(1)}, f32[12,48,128]{2,1,0:T(8,128)S(1)}, f32[12,48,128]{2,1,0:T(8,128)S(1)}, f32[12,48,128]{2,1,0:T(8,128)S(1)}, f...) fusion(f32[12,48,128]{2,1,0:T(8,128)S(1)} %reduce_sum.9, ...), kind=kLoop, calls=%fused_computation.391 | loop fusion | flops 7077888 | bytes 9363456 | tf_op jit(solution)/shard_map/jit(_where)/select_n | solution.py:140
  68.2 0.5 copy.118
  68.8 1.6 %slice-done = s8[4194304]{0:T(1024)(128)(4,1)S(1)} async-done(((s8[5603328]{0:T(1024)(128)(4,1)}), s8[4194304]{0:T(1024)(128)(4,1)S(1)}, s32[]{:S(2)}) %slice-start) | async-done | bytes 4194328
  71.2 0.5 bitcast_dynamic-update-slice_fusion.16
  72.2 0.5 bitcast_dynamic-update-slice_fusion.14
  72.6 0.4 bitcast_dynamic-update-slice_fusion.13
  73.1 0.5 bitcast_dynamic-update-slice_fusion.12
  74.0 0.5 bitcast_dynamic-update-slice_fusion.10
  74.4 0.5 bitcast_dynamic-update-slice_fusion.9
  74.9 0.5 bitcast_dynamic-update-slice_fusion.8
  78.8 3.2 %collective-permute-start.16 = (f32[19,1,48,128]{3,2,1,0:T(8,128)S(1)}, f32[19,1,48,128]{3,2,1,0:T(8,128)S(1)}, u32[]{:S(2)}, u32[]{:S(2)}) collective-permute-start(f32[19,1,48,128]{3,2,1,0:T(8,128)S(1)} %get-tuple-element.74), channel_id=1, source_target_pairs={{0,4},{4,8},{8,12},{1,5},{5,9},{9,13},{2,6},{6,10},{10,14},{3,7},{... | collective-permute-start | bytes 1400840 | tf_op jit(solution)/shard_map/ppermute | solution.py:44
  82.0 1.3 collective-permute-start.17
  83.4 4.0 %collective-permute-start.12 = (s32[1,48,128]{2,1,0:T(8,128)S(1)}, s32[1,48,128]{2,1,0:T(8,128)S(1)}, u32[]{:S(2)}, u32[]{:S(2)}) collective-permute-start(s32[1,48,128]{2,1,0:T(8,128)S(1)} %get-tuple-element.80), channel_id=1, source_target_pairs={{0,4},{4,8},{8,12},{1,5},{5,9},{9,13},{2,6},{6,10},{10,14},{3,7},{... | collective-permute-start | bytes 73736 | tf_op jit(solution)/shard_map/ppermute | solution.py:44
  87.4 1.3 collective-permute-start.13
  88.7 1.9 %collective-permute-done.12 = s32[1,48,128]{2,1,0:T(8,128)S(1)} collective-permute-done((s32[1,48,128]{2,1,0:T(8,128)S(1)}, s32[1,48,128]{2,1,0:T(8,128)S(1)}, u32[]{:S(2)}, u32[]{:S(2)}) %collective-permute-start.12) | collective-permute-done | bytes 24608 | tf_op jit(solution)/shard_map/ppermute | solution.py:44
  90.5 4.1 %collective-permute-done.13 = s32[1,48,128]{2,1,0:T(8,128)S(1)} collective-permute-done((s32[1,48,128]{2,1,0:T(8,128)S(1)}, s32[1,48,128]{2,1,0:T(8,128)S(1)}, u32[]{:S(2)}, u32[]{:S(2)}) %collective-permute-start.13) | collective-permute-done | bytes 24608 | tf_op jit(solution)/shard_map/ppermute | solution.py:45
  94.7 4.2 %collective-permute-start.14 = (s32[14,1,128]{2,1,0:T(1,128)S(1)}, s32[14,1,128]{2,1,0:T(1,128)S(1)}, u32[]{:S(2)}, u32[]{:S(2)}) collective-permute-start(s32[14,1,128]{2,1,0:T(1,128)S(1)} %get-tuple-element.78), channel_id=1, source_target_pairs={{0,1},{1,2},{2,3},{4,5},{5,6},{6,7},{8,9},{9,10},{10,11},{12,13},{... | collective-permute-start | bytes 21512 | tf_op jit(solution)/shard_map/ppermute | solution.py:44
  98.9 1.9 %collective-permute-start.15 = (s32[14,1,128]{2,1,0:T(1,128)S(1)}, s32[14,1,128]{2,1,0:T(1,128)S(1)}, u32[]{:S(2)}, u32[]{:S(2)}) collective-permute-start(s32[14,1,128]{2,1,0:T(1,128)S(1)} %get-tuple-element.79), channel_id=1, source_target_pairs={{1,0},{2,1},{3,2},{5,4},{6,5},{7,6},{9,8},{10,9},{11,10},{13,12},{... | collective-permute-start | bytes 21512 | tf_op jit(solution)/shard_map/ppermute | solution.py:45
  101.0 3.6 %collective-permute-start.18 = (f32[19,14,1,128]{3,2,1,0:T(1,128)S(1)}, f32[19,14,1,128]{3,2,1,0:T(1,128)S(1)}, u32[]{:S(2)}, u32[]{:S(2)}) collective-permute-start(f32[19,14,1,128]{3,2,1,0:T(1,128)S(1)} %get-tuple-element.72), channel_id=1, source_target_pairs={{0,1},{1,2},{2,3},{4,5},{5,6},{6,7},{8,9},{9,10},{10,11},{12,13},{... | collective-permute-start | bytes 408584 | tf_op jit(solution)/shard_map/ppermute | solution.py:44
  104.7 2.1 %collective-permute-start.19 = (f32[19,14,1,128]{3,2,1,0:T(1,128)S(1)}, f32[19,14,1,128]{3,2,1,0:T(1,128)S(1)}, u32[]{:S(2)}, u32[]{:S(2)}) collective-permute-start(f32[19,14,1,128]{3,2,1,0:T(1,128)S(1)} %get-tuple-element.73), channel_id=1, source_target_pairs={{1,0},{2,1},{3,2},{5,4},{6,5},{7,6},{9,8},{10,9},{11,10},{13,12},{... | collective-permute-start | bytes 408584 | tf_op jit(solution)/shard_map/ppermute | solution.py:45
  106.9 4.1 %collective-permute-done.19 = f32[19,14,1,128]{3,2,1,0:T(1,128)S(1)} collective-permute-done((f32[19,14,1,128]{3,2,1,0:T(1,128)S(1)}, f32[19,14,1,128]{3,2,1,0:T(1,128)S(1)}, u32[]{:S(2)}, u32[]{:S(2)}) %collective-permute-start.19) | collective-permute-done | bytes 136224 | tf_op jit(solution)/shard_map/ppermute | solution.py:45
  111.0 14.2 %select_maximum_fusion = f32[19,14,50,130]{3,2,1,0:T(8,128)S(1)} fusion(f32[19,14,1,128]{3,2,1,0:T(1,128)S(1)} %collective-permute-done.19, f32[19,14,1,128]{3,2,1,0:T(1,128)S(1)} %collective-permute-done.18, f32[19,1,48,128]{3,2,1,0:T(8,128)S(1)} %collective-permute-done.17, f32[19,12,48,128]{3,2,1,0:T(8,128)S(1)} %get-tuple-element.11, ...), kind=kLoop, calls=%fused_computation.2 | loop fusion | flops 20748000 | bytes 13725600 | tf_op jit(solution)/shard_map/concatenate | solution.py:46
  128.0 2.5 %copy-done = f32[19,12,48,128]{3,2,1,0:T(8,128)} copy-done((f32[19,12,48,128]{3,2,1,0:T(8,128)}, f32[19,12,48,128]{3,2,1,0:T(8,128)S(1)}, u32[]{:S(2)}) %copy-start) | copy-done | bytes 5603352
  (90 shorter events, 10.3 us)
Async XLA Ops:
  0.6 55.7 %copy-start.3 = (f32[3,12,32]{2,1,0:T(8,128)S(1)}, f32[3,12,32]{2,1,0:T(8,128)}, u32[]{:S(2)}) copy-start(f32[3,12,32]{2,1,0:T(8,128)} %param.10) | copy-start | bytes 13828
  0.6 55.7 %copy-start.4 = (f32[3,3,12,32]{3,2,1,0:T(8,128)S(1)}, f32[3,3,12,32]{3,2,1,0:T(8,128)}, u32[]{:S(2)}) copy-start(f32[3,3,12,32]{3,2,1,0:T(8,128)} %param.13) | copy-start | bytes 41476
  1.4 5.3 %collective-permute-start.1 = (f32[1,12,32]{2,1,0:T(8,128)S(1)}, f32[1,12,32]{2,1,0:T(8,128)S(1)}, u32[]{:S(2)}, u32[]{:S(2)}) collective-permute-start(f32[1,12,32]{2,1,0:T(8,128)S(1)} %get-tuple-element.96), channel_id=1, source_target_pairs={{0,4},{4,8},{8,12},{1,5},{5,9},{9,13},{2,6},{6,10},{10,14},{3,7},{... | collective-permute-start | bytes 4616 | tf_op jit(solution)/shard_map/ppermute | solution.py:44
  5.4 4.4 %collective-permute-start = (f32[1,12,32]{2,1,0:T(8,128)S(1)}, f32[1,12,32]{2,1,0:T(8,128)S(1)}, u32[]{:S(2)}, u32[]{:S(2)}) collective-permute-start(f32[1,12,32]{2,1,0:T(8,128)S(1)} %get-tuple-element.95), channel_id=1, source_target_pairs={{4,0},{8,4},{12,8},{5,1},{9,5},{13,9},{6,2},{10,6},{14,10},{7,3},{... | collective-permute-start | bytes 4616 | tf_op jit(solution)/shard_map/ppermute | solution.py:45
  9.8 8.9 %collective-permute-start.2 = (f32[5,1,32]{2,1,0:T(1,128)S(1)}, f32[5,1,32]{2,1,0:T(1,128)S(1)}, u32[]{:S(2)}, u32[]{:S(2)}) collective-permute-start(f32[5,1,32]{2,1,0:T(1,128)S(1)} %get-tuple-element.90), channel_id=1, source_target_pairs={{1,0},{2,1},{3,2},{5,4},{6,5},{7,6},{9,8},{10,9},{11,10},{13,12},{... | collective-permute-start | bytes 1928 | tf_op jit(solution)/shard_map/ppermute | solution.py:45
  13.9 4.9 %collective-permute-start.3 = (f32[5,1,32]{2,1,0:T(1,128)S(1)}, f32[5,1,32]{2,1,0:T(1,128)S(1)}, u32[]{:S(2)}, u32[]{:S(2)}) collective-permute-start(f32[5,1,32]{2,1,0:T(1,128)S(1)} %get-tuple-element.89), channel_id=1, source_target_pairs={{0,1},{1,2},{2,3},{4,5},{5,6},{6,7},{8,9},{9,10},{10,11},{12,13},{... | collective-permute-start | bytes 1928 | tf_op jit(solution)/shard_map/ppermute | solution.py:44
  21.6 5.3 %collective-permute-start.4 = (f32[1,12,32]{2,1,0:T(8,128)S(1)}, f32[1,12,32]{2,1,0:T(8,128)S(1)}, u32[]{:S(2)}, u32[]{:S(2)}) collective-permute-start(f32[1,12,32]{2,1,0:T(8,128)S(1)} %get-tuple-element.94), channel_id=1, source_target_pairs={{4,0},{8,4},{12,8},{5,1},{9,5},{13,9},{6,2},{10,6},{14,10},{7,3},{... | collective-permute-start | bytes 4616 | tf_op jit(solution)/shard_map/ppermute | solution.py:45
  22.9 4.8 %collective-permute-start.5 = (f32[1,12,32]{2,1,0:T(8,128)S(1)}, f32[1,12,32]{2,1,0:T(8,128)S(1)}, u32[]{:S(2)}, u32[]{:S(2)}) collective-permute-start(f32[1,12,32]{2,1,0:T(8,128)S(1)} %get-tuple-element.93), channel_id=1, source_target_pairs={{0,4},{4,8},{8,12},{1,5},{5,9},{9,13},{2,6},{6,10},{10,14},{3,7},{... | collective-permute-start | bytes 4616 | tf_op jit(solution)/shard_map/ppermute | solution.py:44
  27.7 6.1 %collective-permute-start.6 = (f32[5,1,32]{2,1,0:T(1,128)S(1)}, f32[5,1,32]{2,1,0:T(1,128)S(1)}, u32[]{:S(2)}, u32[]{:S(2)}) collective-permute-start(f32[5,1,32]{2,1,0:T(1,128)S(1)} %get-tuple-element.88), channel_id=1, source_target_pairs={{1,0},{2,1},{3,2},{5,4},{6,5},{7,6},{9,8},{10,9},{11,10},{13,12},{... | collective-permute-start | bytes 1928 | tf_op jit(solution)/shard_map/ppermute | solution.py:45
  30.1 4.4 %collective-permute-start.7 = (f32[5,1,32]{2,1,0:T(1,128)S(1)}, f32[5,1,32]{2,1,0:T(1,128)S(1)}, u32[]{:S(2)}, u32[]{:S(2)}) collective-permute-start(f32[5,1,32]{2,1,0:T(1,128)S(1)} %get-tuple-element.87), channel_id=1, source_target_pairs={{0,1},{1,2},{2,3},{4,5},{5,6},{6,7},{8,9},{9,10},{10,11},{12,13},{... | collective-permute-start | bytes 1928 | tf_op jit(solution)/shard_map/ppermute | solution.py:44
  37.4 26.4 %copy-start.2 = (f32[3,12,32]{2,1,0:T(8,128)}, f32[3,12,32]{2,1,0:T(8,128)S(1)}, u32[]{:S(2)}) copy-start(f32[3,12,32]{2,1,0:T(8,128)S(1)} %fusion.247) | copy-start | bytes 13828
  37.4 5.2 %collective-permute-start.8 = (f32[1,12,32]{2,1,0:T(8,128)S(1)}, f32[1,12,32]{2,1,0:T(8,128)S(1)}, u32[]{:S(2)}, u32[]{:S(2)}) collective-permute-start(f32[1,12,32]{2,1,0:T(8,128)S(1)} %get-tuple-element.92), channel_id=1, source_target_pairs={{0,4},{4,8},{8,12},{1,5},{5,9},{9,13},{2,6},{6,10},{10,14},{3,7},{... | collective-permute-start | bytes 4616 | tf_op jit(solution)/shard_map/ppermute | solution.py:44
  41.3 4.4 %collective-permute-start.9 = (f32[1,12,32]{2,1,0:T(8,128)S(1)}, f32[1,12,32]{2,1,0:T(8,128)S(1)}, u32[]{:S(2)}, u32[]{:S(2)}) collective-permute-start(f32[1,12,32]{2,1,0:T(8,128)S(1)} %get-tuple-element.91), channel_id=1, source_target_pairs={{4,0},{8,4},{12,8},{5,1},{9,5},{13,9},{6,2},{10,6},{14,10},{7,3},{... | collective-permute-start | bytes 4616 | tf_op jit(solution)/shard_map/ppermute | solution.py:45
  45.7 10.5 %collective-permute-start.10 = (f32[5,1,32]{2,1,0:T(1,128)S(1)}, f32[5,1,32]{2,1,0:T(1,128)S(1)}, u32[]{:S(2)}, u32[]{:S(2)}) collective-permute-start(f32[5,1,32]{2,1,0:T(1,128)S(1)} %get-tuple-element.85), channel_id=1, source_target_pairs={{1,0},{2,1},{3,2},{5,4},{6,5},{7,6},{9,8},{10,9},{11,10},{13,12},{... | collective-permute-start | bytes 1928 | tf_op jit(solution)/shard_map/ppermute | solution.py:45
  47.9 8.3 %collective-permute-start.11 = (f32[5,1,32]{2,1,0:T(1,128)S(1)}, f32[5,1,32]{2,1,0:T(1,128)S(1)}, u32[]{:S(2)}, u32[]{:S(2)}) collective-permute-start(f32[5,1,32]{2,1,0:T(1,128)S(1)} %get-tuple-element.86), channel_id=1, source_target_pairs={{0,1},{1,2},{2,3},{4,5},{5,6},{6,7},{8,9},{9,10},{10,11},{12,13},{... | collective-permute-start | bytes 1928 | tf_op jit(solution)/shard_map/ppermute | solution.py:44
  56.2 8.4 %copy-start.1 = (s32[12,48,128]{2,1,0:T(8,128)S(1)}, s32[12,48,128]{2,1,0:T(8,128)}, u32[]{:S(2)}) copy-start(s32[12,48,128]{2,1,0:T(8,128)} %param.8) | copy-start | bytes 884740
  68.2 2.2 %slice-start = ((s8[5603328]{0:T(1024)(128)(4,1)}), s8[4194304]{0:T(1024)(128)(4,1)S(1)}, s32[]{:S(2)}) async-start(s8[5603328]{0:T(1024)(128)(4,1)} %bitcast.820), calls=%async_computation | async-start | bytes 8388608
  68.2 2.6 %slice-start.1 = ((s8[5603328]{0:T(1024)(128)(4,1)}), s8[1409024]{0:T(1024)(128)(4,1)S(1)}, s32[]{:S(2)}) async-start(s8[5603328]{0:T(1024)(128)(4,1)} %bitcast.820), calls=%async_computation.1 | async-start | bytes 2818048
  78.8 22.0 %collective-permute-start.16 = (f32[19,1,48,128]{3,2,1,0:T(8,128)S(1)}, f32[19,1,48,128]{3,2,1,0:T(8,128)S(1)}, u32[]{:S(2)}, u32[]{:S(2)}) collective-permute-start(f32[19,1,48,128]{3,2,1,0:T(8,128)S(1)} %get-tuple-element.74), channel_id=1, source_target_pairs={{0,4},{4,8},{8,12},{1,5},{5,9},{9,13},{2,6},{6,10},{10,14},{3,7},{... | collective-permute-start | bytes 1400840 | tf_op jit(solution)/shard_map/ppermute | solution.py:44
  82.0 18.8 %collective-permute-start.17 = (f32[19,1,48,128]{3,2,1,0:T(8,128)S(1)}, f32[19,1,48,128]{3,2,1,0:T(8,128)S(1)}, u32[]{:S(2)}, u32[]{:S(2)}) collective-permute-start(f32[19,1,48,128]{3,2,1,0:T(8,128)S(1)} %get-tuple-element.75), channel_id=1, source_target_pairs={{4,0},{8,4},{12,8},{5,1},{9,5},{13,9},{6,2},{10,6},{14,10},{7,3},{... | collective-permute-start | bytes 1400840 | tf_op jit(solution)/shard_map/ppermute | solution.py:45
  83.4 7.1 %collective-permute-start.12 = (s32[1,48,128]{2,1,0:T(8,128)S(1)}, s32[1,48,128]{2,1,0:T(8,128)S(1)}, u32[]{:S(2)}, u32[]{:S(2)}) collective-permute-start(s32[1,48,128]{2,1,0:T(8,128)S(1)} %get-tuple-element.80), channel_id=1, source_target_pairs={{0,4},{4,8},{8,12},{1,5},{5,9},{9,13},{2,6},{6,10},{10,14},{3,7},{... | collective-permute-start | bytes 73736 | tf_op jit(solution)/shard_map/ppermute | solution.py:44
  87.4 7.3 %collective-permute-start.13 = (s32[1,48,128]{2,1,0:T(8,128)S(1)}, s32[1,48,128]{2,1,0:T(8,128)S(1)}, u32[]{:S(2)}, u32[]{:S(2)}) collective-permute-start(s32[1,48,128]{2,1,0:T(8,128)S(1)} %get-tuple-element.81), channel_id=1, source_target_pairs={{4,0},{8,4},{12,8},{5,1},{9,5},{13,9},{6,2},{10,6},{14,10},{7,3},{... | collective-permute-start | bytes 73736 | tf_op jit(solution)/shard_map/ppermute | solution.py:45
  94.7 12.1 %collective-permute-start.14 = (s32[14,1,128]{2,1,0:T(1,128)S(1)}, s32[14,1,128]{2,1,0:T(1,128)S(1)}, u32[]{:S(2)}, u32[]{:S(2)}) collective-permute-start(s32[14,1,128]{2,1,0:T(1,128)S(1)} %get-tuple-element.78), channel_id=1, source_target_pairs={{0,1},{1,2},{2,3},{4,5},{5,6},{6,7},{8,9},{9,10},{10,11},{12,13},{... | collective-permute-start | bytes 21512 | tf_op jit(solution)/shard_map/ppermute | solution.py:44
  98.9 7.9 %collective-permute-start.15 = (s32[14,1,128]{2,1,0:T(1,128)S(1)}, s32[14,1,128]{2,1,0:T(1,128)S(1)}, u32[]{:S(2)}, u32[]{:S(2)}) collective-permute-start(s32[14,1,128]{2,1,0:T(1,128)S(1)} %get-tuple-element.79), channel_id=1, source_target_pairs={{1,0},{2,1},{3,2},{5,4},{6,5},{7,6},{9,8},{10,9},{11,10},{13,12},{... | collective-permute-start | bytes 21512 | tf_op jit(solution)/shard_map/ppermute | solution.py:45
  101.0 5.9 %collective-permute-start.18 = (f32[19,14,1,128]{3,2,1,0:T(1,128)S(1)}, f32[19,14,1,128]{3,2,1,0:T(1,128)S(1)}, u32[]{:S(2)}, u32[]{:S(2)}) collective-permute-start(f32[19,14,1,128]{3,2,1,0:T(1,128)S(1)} %get-tuple-element.72), channel_id=1, source_target_pairs={{0,1},{1,2},{2,3},{4,5},{5,6},{6,7},{8,9},{9,10},{10,11},{12,13},{... | collective-permute-start | bytes 408584 | tf_op jit(solution)/shard_map/ppermute | solution.py:44
  104.7 6.3 %collective-permute-start.19 = (f32[19,14,1,128]{3,2,1,0:T(1,128)S(1)}, f32[19,14,1,128]{3,2,1,0:T(1,128)S(1)}, u32[]{:S(2)}, u32[]{:S(2)}) collective-permute-start(f32[19,14,1,128]{3,2,1,0:T(1,128)S(1)} %get-tuple-element.73), channel_id=1, source_target_pairs={{1,0},{2,1},{3,2},{5,4},{6,5},{7,6},{9,8},{10,9},{11,10},{13,12},{... | collective-permute-start | bytes 408584 | tf_op jit(solution)/shard_map/ppermute | solution.py:45
  128.0 2.5 %copy-start = (f32[19,12,48,128]{3,2,1,0:T(8,128)}, f32[19,12,48,128]{3,2,1,0:T(8,128)S(1)}, u32[]{:S(2)}) copy-start(f32[19,12,48,128]{3,2,1,0:T(8,128)S(1)} %fusion.53) | copy-start | bytes 16809988
where the time goes:
time: 132 us; the launch traced here: 130 us
  starting transfers between devices  58.1 us (44%)
  other arithmetic  43.8 us (33%)
  waiting for transfers between devices  17 us (13%)
  local copies, waits for them, and re-layouts  10.2 us (8%)
  between operations  1.35 us (1%)
    ppermute x10, starting transfers between devices, extended(): before = lax.ppermute(last, axis, up)  39 us
    ppermute x10, starting transfers between devices, extended(): after = lax.ppermute(first, axis, down)  19.1 us
    concatenate x7, other arithmetic, extended(): x = jnp.concatenate([before, x, after], axis=dim)  14.5 us
    ppermute x10, waiting for transfers between devices, extended(): after = lax.ppermute(first, axis, down)  13.6 us
    unnamed x35, other arithmetic  10.1 us
    unnamed x18, local copies, waits for them, and re-layouts  5.83 us
    another operation x3, other arithmetic, lorentz_from(): jnp.stack([cur_y * field_z - cur_z * field_y, cur_z * field_x - cur_x * f...  5.79 us
    div x2, other arithmetic, jacobi_sweep(): return (beside_all + source) / 6.0  5.51 us
  transfers between devices with their start and end apart: 20, of which 7 were waited for; matrix products, arithmetic and copies ran while one was open for 4% of the time, Pallas kernels for 0%

commit v1 on v0

v1 whole, which is shorter than its diff:
```python
import jax
import jax.numpy as jnp
from jax import lax
from jax.experimental import pallas as pl
from jax.experimental.pallas import tpu as pltpu
from jax.sharding import PartitionSpec as P

lattice_dirs = [
    (0, 0, 0),
    (1, 0, 0),
    (-1, 0, 0),
    (0, 1, 0),
    (0, -1, 0),
    (0, 0, 1),
    (0, 0, -1),
    (1, 1, 0),
    (-1, -1, 0),
    (1, -1, 0),
    (-1, 1, 0),
    (1, 0, 1),
    (-1, 0, -1),
    (1, 0, -1),
    (-1, 0, 1),
    (0, 1, 1),
    (0, -1, -1),
    (0, 1, -1),
    (0, -1, 1),
]
opposite_dir = [0, 2, 1, 4, 3, 6, 5, 8, 7, 10, 9, 12, 11, 14, 13, 16, 15, 18, 17]
pairs = [(i, opposite_dir[i]) for i in range(1, 19) if i < opposite_dir[i]]
relax_time = 0.8
force_scale = 0.02
inlet_speed = 0.05
force_factor = 1.0 - 0.5 / relax_time

leave_yp = [3, 7, 10, 15, 17]
leave_ym = [4, 8, 9, 16, 18]
leave_zp = [5, 11, 14, 15, 18]
leave_zm = [6, 12, 13, 16, 17]

FACE = 10
GROUPS = 7
POT, SRC, COND, PH, MX, MY, MZ = range(GROUPS)
RIM = 4
CLOSED = -1e30
OPEN_ABOVE = -1e29
VMEM_LIMIT = 48 * 1024 * 1024

any_spec = pl.BlockSpec(memory_space=pl.ANY)
hbm_spec = pl.BlockSpec(memory_space=pltpu.HBM)
vmem_spec = pl.BlockSpec(memory_space=pltpu.VMEM)


def moments(f):
    d = {}
    rho = f[0]
    for i, j in pairs:
        rho = rho + (f[i] + f[j])
        d[i] = f[i] - f[j]
    mx = d[1] + d[7] + d[9] + d[11] + d[13]
    my = d[3] + d[7] - d[9] + d[15] + d[17]
    mz = d[5] + d[11] - d[13] + d[15] - d[17]
    return rho, mx, my, mz


def coefficients(rho, mom, force, fluid, inlet):
    inv = 1.0 / rho
    u = [(m + 0.5 * f) * inv for m, f in zip(mom, force)]
    u = [jnp.where(inlet, c, v) for c, v in zip((0.0, 0.0, -inlet_speed), u)]
    r = jnp.where(fluid, rho * (1.0 / (36.0 * relax_time)), 1.0 / 36.0)
    f = [jnp.where(fluid, v * (force_factor / 36.0), 0.0) for v in force]
    sq = u[0] * u[0] + u[1] * u[1] + u[2] * u[2]
    uf = u[0] * f[0] + u[1] * f[1] + u[2] * f[2]
    base = r * (1.0 - 1.5 * sq) - 3.0 * uf
    ru = [r * v for v in u]
    g = [4.5 * a + 9.0 * b for a, b in zip(ru, f)]
    h = [3.0 * (a + b) for a, b in zip(ru, f)]
    keep = jnp.where(fluid, 1.0 - 1.0 / relax_time, 0.0)
    return keep, base, u, g, h


def along(c, v):
    total = None
    for s, x in zip(c, v):
        if s == 0:
            continue
        if total is None:
            total = x if s > 0 else -x
        else:
            total = total + x if s > 0 else total - x
    return total


def post_pair(i, co):
    keep, base, u, g, h = co
    c = lattice_dirs[i]
    sym = base + along(c, u) * along(c, g)
    anti = along(c, h)
    if sum(abs(s) for s in c) == 1:
        return 2.0 * sym, 2.0 * anti
    return sym, anti


def post_one(i, f, co):
    keep = co[0]
    if i < opposite_dir[i]:
        sym, anti = post_pair(i, co)
        return keep * f + (sym + anti)
    sym, anti = post_pair(opposite_dir[i], co)
    return keep * f + (sym - anti)


def pick(cond, a, b):
    return jnp.where(cond, a, b)


def lanes_to(x, shift):
    shift = shift % 128
    return x if shift == 0 else pltpu.roll(x, shift, 1)


def pack_faces(
    pops,
    flags,
    pot_hbm,
    cond_hbm,
    ph_hbm,
    mag_hbm,
    tab_hbm,
    o_z1,
    o_z2,
    o_y1,
    o_y2,
    o_g,
    pbuf,
    ybuf,
    fpbuf,
    fybuf,
    zsc,
    ysc,
    pot,
    cond,
    ph,
    mag,
    tab,
    sems,
):
    nz, ny = pops.shape[1], pops.shape[2]
    kz, ky, kx = pot.shape
    coarse = [
        pltpu.make_async_copy(a, b, sems.at[8 + k])
        for k, (a, b) in enumerate(
            ((tab_hbm, tab), (ph_hbm, ph), (cond_hbm, cond), (pot_hbm, pot), (mag_hbm, mag))
        )
    ]
    copies = []
    for side, row in ((0, 0), (1, ny - 8)):
        copies.append(
            pltpu.make_async_copy(pops.at[:, :, pl.ds(row, 8), :], ybuf.at[side], sems.at[side])
        )
        copies.append(
            pltpu.make_async_copy(flags.at[:, pl.ds(row, 8), :], fybuf.at[side], sems.at[2 + side])
        )
    for side, plane in ((0, 0), (1, nz - 1)):
        copies.append(pltpu.make_async_copy(pops.at[:, plane], pbuf.at[side], sems.at[4 + side]))
        copies.append(pltpu.make_async_copy(flags.at[plane], fpbuf.at[side], sems.at[6 + side]))
    for c in coarse + copies:
        c.start()
    for c in coarse:
        c.wait()
    phase = ph[...]
    conductivity = cond[...]
    source = conductivity * jnp.where(
        phase == 0, tab[0, 0], jnp.where(phase == 1, tab[1, 0], tab[2, 0])
    )
    fields = [pot[...], source, conductivity, phase.astype(jnp.float32), mag[0], mag[1], mag[2]]
    blank = jnp.zeros((ky, 128 - kz * kx), jnp.float32)
    for g, field in enumerate(fields):
        row = jnp.concatenate([field[l] for l in range(kz)] + [blank], axis=1)
        o_g[g, 0:ky, :] = row
        at = FACE * nz + RIM * g
        ysc[0, at : at + RIM, :] = row[0:RIM]
        ysc[1, at : at + RIM, :] = row[ky - RIM : ky]
    for c in copies[:4]:
        c.wait()
    for side, leave, row in ((0, leave_ym, 0), (1, leave_yp, 7)):
        for z in range(nz):
            f = [ybuf[side, i, z] for i in range(19)]
            values = [f[i] for i in leave] + list(moments(f))
            values.append(fybuf[side, z].astype(jnp.float32))
            for k, v in enumerate(values):
                ysc[side, k * nz + z : k * nz + z + 1, :] = v[row : row + 1]
    for c in copies[4:]:
        c.wait()
    for side, leave in ((0, leave_zm), (1, leave_zp)):
        for b in range(ny // 8):
            rows = slice(8 * b, 8 * b + 8)
            f = [pbuf[side, i, rows] for i in range(19)]
            values = [f[i] for i in leave] + list(moments(f))
            values.append(fpbuf[side, rows].astype(jnp.float32))
            for k, v in enumerate(values):
                zsc[side, k, rows, :] = v
    up_z = 1 - lax.axis_index("wide") % 2
    up_y = 1 - lax.axis_index("narrow") % 2
    o_y1[...] = ysc[up_y]
    o_y2[...] = ysc[1 - up_y]
    o_z1[...] = zsc[up_z]
    o_z2[...] = zsc[1 - up_z]


def pack_layers(kz, ky, kx, nz, yr1, yr2, own, o_c1, o_c2, o_p, o_e, zsc):
    even = lax.axis_index("narrow") % 2 == 0
    low = pick(even, yr2[...], yr1[...])
    high = pick(even, yr1[...], yr2[...])
    lane = lax.broadcasted_iota(jnp.int32, (24, 128), 1)
    tail = jnp.zeros((24 - ky - 2 * RIM, 128), jnp.float32)
    for g in range(GROUPS):
        at = FACE * nz + RIM * g
        o_e[g, 0:RIM, :] = low[at : at + RIM]
        o_e[g, RIM : RIM + ky, :] = own[g, 0:ky, :]
        o_e[g, RIM + ky : 2 * RIM + ky, :] = high[at : at + RIM]
        o_e[g, 2 * RIM + ky : 24, :] = tail
    o_p[...] = o_e[POT]
    for side, layer, plane in ((0, 0, 0), (1, kz - 1, nz - 1)):
        zsc[side, 0:24, :] = o_e[POT]
        zsc[side, 24:48, :] = o_e[SRC]
        parts = [lanes_to(o_e[g], kx * (s - layer)) for s, g in enumerate((COND, PH, MX, MY))]
        face = pick(lane < kx, parts[0], parts[1])
        face = pick(lane < 2 * kx, face, parts[2])
        face = pick(lane < 3 * kx, face, parts[3])
        zsc[side, 48:72, :] = face
        zsc[side, 72:96, :] = o_e[MZ]
        for k in range(FACE):
            at = k * nz + plane
            zsc[side, 96 + k : 97 + k, :] = low[at : at + 1]
            zsc[side, 106 + k : 107 + k, :] = high[at : at + 1]
        zsc[side, 116:120, :] = jnp.zeros((4, 128), jnp.float32)
    up_z = 1 - lax.axis_index("wide") % 2
    o_c1[...] = zsc[up_z]
    o_c2[...] = zsc[1 - up_z]


def step_kernel(
    W,
    N,
    pops,
    flags,
    tab_hbm,
    fz1,
    fz2,
    yr1,
    yr2,
    zr1,
    zr2,
    pr_up,
    pr_dn,
    ext,
    o_pops,
    o_pot,
    o_lor,
    buf,
    fbuf,
    post,
    fc,
    fu,
    tab,
    sem_in,
    sem_out,
):
    nz, ny, nx = buf.shape[1:]
    kz, ky, kx = o_pot.shape
    wi, ni = lax.axis_index("wide"), lax.axis_index("narrow")
    tcopy = pltpu.make_async_copy(tab_hbm, tab, sem_in.at[nz + 1])
    tcopy.start()
    fcopy = pltpu.make_async_copy(flags, fbuf, sem_in.at[nz])
    fcopy.start()
    for z in range(nz):
        pltpu.make_async_copy(pops.at[:, z], buf.at[:, z], sem_in.at[z]).start()

    even_z = wi % 2 == 0
    even_y = ni % 2 == 0
    has_low_z, has_high_z = wi > 0, wi < W - 1
    has_low_y, has_high_y = ni > 0, ni < N - 1

    def z_low(rows):
        return pick(even_z, zr2[rows, :], zr1[rows, :])

    def z_high(rows):
        return pick(even_z, zr1[rows, :], zr2[rows, :])

    shape = (24, 128)
    lane = lax.broadcasted_iota(jnp.int32, shape, 1)
    row = lax.broadcasted_iota(jnp.int32, shape, 0)
    y_at = ni * ky + row - RIM
    y_in = (y_at >= 0) & (y_at < ky * N)
    layer = lane // kx
    x_at = lane - layer * kx

    def inside(first):
        z_at = wi * kz + first + layer
        return y_in & (z_at >= 0) & (z_at < kz * W) & (layer < kz)

    inner = [inside(-kz), inside(0), inside(kz)]
    beyond = [inside(-2 * kz), inside(2 * kz)]

    def group(at):
        rows = slice(24 * at, 24 * at + 24)
        return z_low(rows), z_high(rows)

    def three(g, at):
        a, b = group(at)
        return [a, ext[g], b]

    zero = jnp.zeros(shape, jnp.float32)
    field = [pick(m, v, 0.0) for m, v in zip(inner, three(POT, 0))]
    far_low = pick(beyond[0], pr_dn[...], 0.0)
    far_high = pick(beyond[1], pr_up[...], 0.0)
    source = three(SRC, 1)
    last = (kz - 1) * kx

    def next_z(here, above):
        return pick(lane < last, lanes_to(here, -kx), lanes_to(above, last))

    def prev_z(here, below):
        return pick(lane >= kx, lanes_to(here, kx), lanes_to(below, -last))

    def next_x(v):
        return pick(x_at == kx - 1, 0.0, lanes_to(v, -1))

    def prev_x(v):
        return pick(x_at == 0, 0.0, lanes_to(v, 1))

    def next_y(v):
        return pltpu.roll(v, 23, 0)

    def prev_y(v):
        return pltpu.roll(v, 1, 0)

    def sweep(values, lower, upper):
        chain = [lower] + values + [upper]
        new = []
        for k in range(3):
            v = values[k]
            total = next_z(v, chain[k + 2]) + prev_z(v, chain[k])
            total = total + next_y(v) + prev_y(v)
            total = total + next_x(v) + prev_x(v)
            new.append(pick(inner[k], (total + source[k]) / 6.0, 0.0))
        return new

    field = sweep(field, far_low, far_high)
    field = sweep(field, zero, zero)

    tcopy.wait()
    face = group(2)
    mz = three(MZ, 3)

    def face_fields(slot, g):
        k = slot
        a = lanes_to(face[0], kx * (kz - 1 - k))
        b = lanes_to(face[1], -kx * k)
        return [a, ext[g], b]

    cond = face_fields(0, COND)
    phase = face_fields(1, PH)
    mx = face_fields(2, MX)
    my = face_fields(3, MY)
    chain = [zero] + field + [zero]
    lorentz = []
    for k in range(3):
        v = field[k]
        grad = (
            (next_x(v) - prev_x(v)) * 0.5,
            (next_y(v) - prev_y(v)) * 0.5,
            (next_z(v, chain[k + 2]) - prev_z(v, chain[k])) * 0.5,
        )
        cur = []
        for a in range(3):
            applied = pick(
                phase[k] < 0.5, tab[0, 1 + a], pick(phase[k] < 1.5, tab[1, 1 + a], tab[2, 1 + a])
            )
            cur.append(cond[k] * (applied - grad[a]))
        lorentz.append(
            [
                cur[1] * mz[k] - cur[2] * my[k],
                cur[2] * mx[k] - cur[0] * mz[k],
                cur[0] * my[k] - cur[1] * mx[k],
            ]
        )
    for l in range(kz):
        o_pot[l] = lanes_to(field[1], -kx * l)[RIM : RIM + ky, 0:kx]
        for a in range(3):
            o_lor[a, l] = lanes_to(lorentz[1][a], -kx * l)[RIM : RIM + ky, 0:kx]

    src = lax.broadcasted_iota(jnp.int32, (128, 128), 0)
    dst = lax.broadcasted_iota(jnp.int32, (128, 128), 1) // (nx // kx)

    def widened(stack, l):
        choose = jnp.where(src == kx * l + dst, 1.0, 0.0)
        return lax.dot_general(
            stack,
            choose,
            (((1,), (0,)), ((), ())),
            precision=lax.Precision.HIGHEST,
            preferred_element_type=jnp.float32,
        )

    stacks = [
        jnp.concatenate([lorentz[k][a] * force_scale for a in range(3)], axis=0) for k in range(3)
    ]
    wide = [widened(stacks[0], kz - 1)]
    wide += [widened(stacks[1], l) for l in range(kz)]
    wide += [widened(stacks[2], 0)]
    sub = lax.broadcasted_iota(jnp.int32, (8, 128), 0)
    for l in range(kz + 2):
        for a in range(3):
            fc[l, a] = wide[l][24 * a : 24 * a + 24]
    for l in range(kz + 2):
        for a in range(3):
            for b in range(ny // 8):
                first = jnp.broadcast_to(fc[l, a, pl.ds(RIM + 2 * b, 1), :], (8, 128))
                second = jnp.broadcast_to(fc[l, a, pl.ds(RIM + 2 * b + 1, 1), :], (8, 128))
                fu[l, a, 8 * b : 8 * b + 8, :] = pick(sub < 4, first, second)

    def beyond_face(values, leave, force, there):
        flag = values[9]
        co = coefficients(values[5], values[6:9], force, flag < 0.5, (flag > 1.5) & (flag < 2.5))
        shut = (flag > 0.5) & (flag < 1.5)
        shut = shut | jnp.logical_not(there)
        return [(i, pick(shut, CLOSED, post_one(i, values[k], co))) for k, i in leave]

    zrow = lax.broadcasted_iota(jnp.int32, (nz, 128), 0)
    for low, leave, frow, at, there in (
        (True, leave_yp, RIM - 1, 7, has_low_y),
        (False, leave_ym, RIM + ky, 8 + ny, has_high_y),
    ):
        first, second = (yr2, yr1) if low else (yr1, yr2)
        values = [
            pick(even_y, first[nz * k : nz * k + nz, :], second[nz * k : nz * k + nz, :])
            for k in range(FACE)
        ]
        force = []
        for a in range(3):
            rows = [jnp.broadcast_to(fc[1 + l, a, frow : frow + 1, :], (nz, 128)) for l in range(kz)]
            v = rows[kz - 1]
            for l in range(kz - 2, -1, -1):
                v = pick(zrow < 4 * (l + 1), rows[l], v)
            force.append(v)
        there_b = jnp.broadcast_to(there, (nz, 128))
        for i, v in beyond_face(values, list(enumerate(leave)), force, there_b):
            for z in range(nz):
                post[i, 1 + z, at : at + 1, :] = v[z : z + 1]

    for low, leave, l, at, there in (
        (True, leave_zp, 0, 0, has_low_z),
        (False, leave_zm, kz + 1, nz + 1, has_high_z),
    ):
        first, second = (fz2, fz1) if low else (fz1, fz2)
        there_b = jnp.broadcast_to(there, (8, 128))
        for b in range(ny // 8):
            rows = slice(8 * b, 8 * b + 8)
            values = [pick(even_z, first[k, rows, :], second[k, rows, :]) for k in range(FACE)]
            force = [fu[l, a, rows, :] for a in range(3)]
            for i, v in beyond_face(values, list(enumerate(leave)), force, there_b):
                post[i, at, 8 + 8 * b : 16 + 8 * b, :] = v

    for z_side, y_side, i, k, there in (
        (0, 0, 15, 3, has_low_z & has_low_y),
        (0, 1, 18, 4, has_low_z & has_high_y),
        (1, 0, 17, 4, has_high_z & has_low_y),
        (1, 1, 16, 3, has_high_z & has_high_y),
    ):
        at = 96 + FACE * y_side
        rows = (z_high if z_side else z_low)(slice(at, at + FACE))
        values = [rows[j : j + 1] for j in range(FACE)]
        frow = RIM + ky if y_side else RIM - 1
        force = [fc[(kz + 1) * z_side, a, frow : frow + 1, :] for a in range(3)]
        there_b = jnp.broadcast_to(there, (1, 128))
        for i, v in beyond_face(values, [(k, i)], force, there_b):
            yrow = 8 + ny if y_side else 7
            post[i, (nz + 1) * z_side, yrow : yrow + 1, :] = v

    fcopy.wait()

    def collide(z, carry):
        pltpu.make_async_copy(pops.at[:, z], buf.at[:, z], sem_in.at[z]).wait()
        l = 1 + z // 4
        for b in range(ny // 8):
            rows = slice(8 * b, 8 * b + 8)
            out = slice(8 + 8 * b, 16 + 8 * b)
            f = [buf[i, z, rows, :] for i in range(19)]
            flag = fbuf[z, rows, :]
            force = [fu[l, a, rows, :] for a in range(3)]
            rho, mom_x, mom_y, mom_z = moments(f)
            wall = flag == 1
            co = coefficients(rho, (mom_x, mom_y, mom_z), force, flag == 0, flag == 2)
            keep = co[0]
            post[0, 1 + z, out, :] = pick(wall, CLOSED, keep * f[0] + 12.0 * co[1])
            for i, j in pairs:
                sym, anti = post_pair(i, co)
                post[i, 1 + z, out, :] = pick(wall, CLOSED, keep * f[i] + (sym + anti))
                post[j, 1 + z, out, :] = pick(wall, CLOSED, keep * f[j] + (sym - anti))
        return carry

    lax.fori_loop(0, nz, collide, 0)

    lane8 = lax.broadcasted_iota(jnp.int32, (8, 128), 1)
    not_first = lane8 > 0
    not_last = lane8 < nx - 1

    def passing(z, carry):
        for b in range(ny // 8):
            rows = slice(8 * b, 8 * b + 8)
            out = slice(8 + 8 * b, 16 + 8 * b)
            wall = fbuf[z, rows, :] == 1
            for i in range(19):
                cx, cy, cz = lattice_dirs[i]
                own = post[opposite_dir[i], 1 + z, out, :]
                if i > 0:
                    v = post[i, 1 + z - cz, 8 + 8 * b - cy : 16 + 8 * b - cy, :]
                    if cx != 0:
                        v = pltpu.roll(v, cx % nx, 1)
                    ok = v > OPEN_ABOVE
                    if cx == 1:
                        ok = ok & not_first
                    if cx == -1:
                        ok = ok & not_last
                    own = pick(ok, v, own)
                buf[i, z, rows, :] = pick(wall, buf[i, z, rows, :], own)
        pltpu.make_async_copy(buf.at[:, z], o_pops.at[:, z], sem_out.at[z]).start()
        return carry

    lax.fori_loop(0, nz, passing, 0)

    def drain(z, carry):
        pltpu.make_async_copy(buf.at[:, z], o_pops.at[:, z], sem_out.at[z]).wait()
        return carry

    lax.fori_loop(0, nz, drain, 0)


def pair_first(size):
    return [(i, i ^ 1) for i in range(size)]


def pair_second(size, wrap):
    found = []
    for i in range(1, size, 2):
        j = (i + 1) % size
        if j > i or wrap:
            found += [(i, j), (j, i)]
    return found


def solution(mesh):
    W, N = mesh.shape["wide"], mesh.shape["narrow"]

    def per_device(populations, flags, potential, conductivity, coil_phase, phase_table, magnetic):
        f32 = jnp.float32
        nz, ny, nx = flags.shape
        kz, ky, kx = potential.shape
        yrows = FACE * nz + RIM * GROUPS
        yrows += -yrows % 8
        params = pltpu.CompilerParams(vmem_limit_bytes=VMEM_LIMIT)
        shape = jax.ShapeDtypeStruct
        z1, z2, y1, y2, own = pl.pallas_call(
            pack_faces,
            name="pack_faces",
            out_shape=(
                shape((FACE, ny, nx), f32),
                shape((FACE, ny, nx), f32),
                shape((yrows, nx), f32),
                shape((yrows, nx), f32),
                shape((GROUPS, 16, nx), f32),
            ),
            in_specs=[hbm_spec] * 7,
            out_specs=[vmem_spec] * 5,
            scratch_shapes=[
                pltpu.VMEM((2, 19, ny, nx), f32),
                pltpu.VMEM((2, 19, nz, 8, nx), f32),
                pltpu.VMEM((2, ny, nx), jnp.int32),
                pltpu.VMEM((2, nz, 8, nx), jnp.int32),
                pltpu.VMEM((2, FACE, ny, nx), f32),
                pltpu.VMEM((2, yrows, nx), f32),
                pltpu.VMEM(potential.shape, f32),
                pltpu.VMEM(conductivity.shape, f32),
                pltpu.VMEM(coil_phase.shape, jnp.int32),
                pltpu.VMEM(magnetic.shape, f32),
                pltpu.SMEM(phase_table.shape, f32),
                pltpu.SemaphoreType.DMA((13,)),
            ],
            compiler_params=params,
        )(
            *[
                pltpu.with_memory_space_constraint(x, pltpu.HBM)
                for x in (populations, flags, potential, conductivity, coil_phase, magnetic, phase_table)
            ]
        )
        yr1 = lax.ppermute(y1, "narrow", pair_first(N))
        yr2 = lax.ppermute(y2, "narrow", pair_second(N, True))
        fz1 = lax.ppermute(z1, "wide", pair_first(W))
        fz2 = lax.ppermute(z2, "wide", pair_second(W, False))
        c1, c2, pot_rows, ext = pl.pallas_call(
            lambda *refs: pack_layers(kz, ky, kx, nz, *refs),
            name="pack_layers",
            out_shape=(
                shape((120, nx), f32),
                shape((120, nx), f32),
                shape((24, nx), f32),
                shape((GROUPS, 24, nx), f32),
            ),
            in_specs=[vmem_spec] * 3,
            out_specs=[vmem_spec] * 4,
            scratch_shapes=[pltpu.VMEM((2, 120, nx), f32)],
            compiler_params=params,
        )(yr1, yr2, own)
        zr1 = lax.ppermute(c1, "wide", pair_first(W))
        zr2 = lax.ppermute(c2, "wide", pair_second(W, False))
        if W == 4:
            pr_up = lax.ppermute(pot_rows, "wide", [(i, i ^ 2) for i in range(W)])
            pr_dn = pr_up
        else:
            pr_up = lax.ppermute(pot_rows, "wide", [(i, i - 2) for i in range(2, W)])
            pr_dn = lax.ppermute(pot_rows, "wide", [(i, i + 2) for i in range(W - 2)])
        return pl.pallas_call(
            lambda *refs: step_kernel(W, N, *refs),
            name="mold_step",
            out_shape=(
                shape(populations.shape, f32),
                shape(potential.shape, f32),
                shape(magnetic.shape, f32),
            ),
            in_specs=[any_spec] * 3 + [vmem_spec] * 9,
            out_specs=[any_spec, vmem_spec, vmem_spec],
            scratch_shapes=[
                pltpu.VMEM(populations.shape, f32),
                pltpu.VMEM(flags.shape, jnp.int32),
                pltpu.VMEM((19, nz + 2, ny + 16, nx), f32),
                pltpu.VMEM((kz + 2, 3, 24, nx), f32),
                pltpu.VMEM((kz + 2, 3, ny, nx), f32),
                pltpu.SMEM(phase_table.shape, f32),
                pltpu.SemaphoreType.DMA((nz + 2,)),
                pltpu.SemaphoreType.DMA((nz,)),
            ],
            compiler_params=params,
        )(
            populations,
            flags,
            phase_table,
            fz1,
            fz2,
            yr1,
            yr2,
            zr1,
            zr2,
            pr_up,
            pr_dn,
            ext,
        )

    in_specs = (
        P(None, ("groups", "wide"), "narrow", None),
        P(("groups", "wide"), "narrow", None),
        P(("groups", "wide"), "narrow", None),
        P(("groups", "wide"), "narrow", None),
        P(("groups", "wide"), "narrow", None),
        P(),
        P(None, ("groups", "wide"), "narrow", None),
    )
    out_specs = (
        P(None, ("groups", "wide"), "narrow", None),
        P(("groups", "wide"), "narrow", None),
        P(None, ("groups", "wide"), "narrow", None),
    )
    return jax.shard_map(
        per_device, mesh=mesh, in_specs=in_specs, out_specs=out_specs, check_vma=False
    )
```

time: 132 us -> 29.2 us (0.22)
  the two profiles are of different devices: /device:TPU:1 before, /device:TPU:0 now
where the time goes in v1:
time: 29.2 us; the launch traced here: 29 us
  starting transfers between devices  13.3 us (46%)
  Pallas kernels  9.4 us (32%)
  waiting for transfers between devices  5.56 us (19%)
  between operations  0.71 us (2%)
    pallas_call x1, Pallas kernels, per_device(): pl.pallas_call(lambda *refs: step_kernel(W, N, *refs), name='mold_step',...  7.14 us
    ppermute x1, starting transfers between devices, per_device(): zr1 = lax.ppermute(c1, 'wide', pair_first(W))  4.45 us
    ppermute x1, starting transfers between devices, per_device(): fz1 = lax.ppermute(z1, 'wide', pair_first(W))  3.09 us
    ppermute x1, waiting for transfers between devices, per_device(): pr_up = lax.ppermute(pot_rows, 'wide', [(i, i ^ 2) for i in range(W)])  3.01 us
    ppermute x1, starting transfers between devices, per_device(): pr_up = lax.ppermute(pot_rows, 'wide', [(i, i ^ 2) for i in range(W)])  2.8 us
    ppermute x1, waiting for transfers between devices, per_device(): yr2 = lax.ppermute(y2, 'narrow', pair_second(N, True))  2.54 us
    pallas_call x1, Pallas kernels, per_device(): pl.pallas_call(pack_faces, name='pack_faces', out_shape=(shape((FACE, ny,...  2.16 us
    ppermute x1, starting transfers between devices, per_device(): yr2 = lax.ppermute(y2, 'narrow', pair_second(N, True))  1.61 us
  transfers between devices with their start and end apart: 7, of which 2 were waited for; matrix products, arithmetic and copies ran while one was open for 0% of the time, Pallas kernels for 0%

profile of v1, /device:TPU:0, one launch (start us, length us, event | category | flops | bytes accessed | tf_op | source)
XLA Modules:
  0.0 29.0 jit_solution(1587888039209672180)
XLA Ops:
  0.6 0.0 copy-start.1
  0.6 0.0 copy-start
  0.7 2.2 %pack_faces.1 = (f32[10,48,128]{2,1,0:T(8,128)S(1)}, f32[10,48,128]{2,1,0:T(8,128)S(1)}, f32[152,128]{1,0:T(8,128)S(1)}, f32[152,128]{1,0:T(8,128)S(1)}, f32[7,16,128]{2,1,0:T(8,128)S(1)}) custom-call(f32[19,12,48,128]{3,2,1,0:T(8,128)} %refs_0_.1, s32[12,48,128]{2,1,0:T(8,128)} %refs_1_.1, f32[3,12,32]{2,1,0:T(8,128)} %pot_hbm.1, f32[3,12,32]{2,1,0:T(8,128)} %cond_hbm.1, ...), custom_call_target="tpu_custom_call" | custom-call | tf_op jit(solution)/shard_map/pack_faces/pallas_call | solution.py:565
  2.8 3.1 %collective-permute-start = (f32[10,48,128]{2,1,0:T(8,128)S(1)}, f32[10,48,128]{2,1,0:T(8,128)S(1)}, u32[]{:S(2)}, u32[]{:S(2)}) collective-permute-start(f32[10,48,128]{2,1,0:T(8,128)S(1)} %get-tuple-element.12), channel_id=1, source_target_pairs={{0,4},{4,0},{8,12},{12,8},{1,5},{5,1},{9,13},{13,9},{2,6},{6,2},{1... | collective-permute-start | bytes 737288 | tf_op jit(solution)/shard_map/ppermute | solution.py:600
  5.9 0.7 %collective-permute-start.1 = (f32[10,48,128]{2,1,0:T(8,128)S(1)}, f32[10,48,128]{2,1,0:T(8,128)S(1)}, u32[]{:S(2)}, u32[]{:S(2)}) collective-permute-start(f32[10,48,128]{2,1,0:T(8,128)S(1)} %get-tuple-element.13), channel_id=1, source_target_pairs={{4,8},{8,4},{5,9},{9,5},{6,10},{10,6},{7,11},{11,7},{20,24},{24,20... | collective-permute-start | bytes 737288 | tf_op jit(solution)/shard_map/ppermute | solution.py:601
  6.6 0.1 collective-permute-start.2
  6.7 1.6 %collective-permute-start.3 = (f32[152,128]{1,0:T(8,128)S(1)}, f32[152,128]{1,0:T(8,128)S(1)}, u32[]{:S(2)}, u32[]{:S(2)}) collective-permute-start(f32[152,128]{1,0:T(8,128)S(1)} %get-tuple-element.15), channel_id=1, source_target_pairs={{1,2},{2,1},{3,0},{0,3},{5,6},{6,5},{7,4},{4,7},{9,10},{10,9},{11,... | collective-permute-start | bytes 233480 | tf_op jit(solution)/shard_map/ppermute | solution.py:599
  8.3 0.0 collective-permute-done.2.refs_0_.refs_5_
  8.3 2.5 %collective-permute-done.3.refs_1_.refs_6_ = f32[152,128]{1,0:T(8,128)S(1)} collective-permute-done((f32[152,128]{1,0:T(8,128)S(1)}, f32[152,128]{1,0:T(8,128)S(1)}, u32[]{:S(2)}, u32[]{:S(2)}) %collective-permute-start.3) | collective-permute-done | bytes 77856 | tf_op jit(solution)/shard_map/ppermute | solution.py:599
  10.8 0.1 pack_layers.1
  10.9 4.5 %collective-permute-start.4 = (f32[120,128]{1,0:T(8,128)S(1)}, f32[120,128]{1,0:T(8,128)S(1)}, u32[]{:S(2)}, u32[]{:S(2)}) collective-permute-start(f32[120,128]{1,0:T(8,128)S(1)} %get-tuple-element.17), channel_id=1, source_target_pairs={{0,4},{4,0},{8,12},{12,8},{1,5},{5,1},{9,13},{13,9},{2,6},{6,2},{1... | collective-permute-start | bytes 184328 | tf_op jit(solution)/shard_map/ppermute | solution.py:616
  15.4 0.7 %collective-permute-start.5 = (f32[120,128]{1,0:T(8,128)S(1)}, f32[120,128]{1,0:T(8,128)S(1)}, u32[]{:S(2)}, u32[]{:S(2)}) collective-permute-start(f32[120,128]{1,0:T(8,128)S(1)} %get-tuple-element.18), channel_id=1, source_target_pairs={{4,8},{8,4},{5,9},{9,5},{6,10},{10,6},{7,11},{11,7},{20,24},{24,20... | collective-permute-start | bytes 184328 | tf_op jit(solution)/shard_map/ppermute | solution.py:617
  16.0 2.8 %collective-permute-start.6 = (f32[24,128]{1,0:T(8,128)S(1)}, f32[24,128]{1,0:T(8,128)S(1)}, u32[]{:S(2)}, u32[]{:S(2)}) collective-permute-start(f32[24,128]{1,0:T(8,128)S(1)} %get-tuple-element.19), channel_id=1, source_target_pairs={{0,8},{4,12},{8,0},{12,4},{1,9},{5,13},{9,1},{13,5},{2,10},{6,14},... | collective-permute-start | bytes 36872 | tf_op jit(solution)/shard_map/ppermute | solution.py:619
  18.8 3.0 %collective-permute-done.6.refs_9_.refs_10_ = f32[24,128]{1,0:T(8,128)S(1)} collective-permute-done((f32[24,128]{1,0:T(8,128)S(1)}, f32[24,128]{1,0:T(8,128)S(1)}, u32[]{:S(2)}, u32[]{:S(2)}) %collective-permute-start.6) | collective-permute-done | bytes 12320 | tf_op jit(solution)/shard_map/ppermute | solution.py:619
  21.8 0.0 collective-permute-done.4.refs_7_
  21.8 0.0 collective-permute-done.5.refs_8_
  21.8 0.0 collective-permute-done.refs_3_
  21.8 0.0 collective-permute-done.1.refs_4_
  21.9 0.0 copy-done.1
  21.9 0.0 copy-done
  21.9 7.1 %mold_step.1 = (f32[19,12,48,128]{3,2,1,0:T(8,128)}, f32[3,12,32]{2,1,0:T(8,128)}, f32[3,3,12,32]{3,2,1,0:T(8,128)}) custom-call(f32[19,12,48,128]{3,2,1,0:T(8,128)} %refs_0_.1, s32[12,48,128]{2,1,0:T(8,128)S(1)} %copy-done, f32[3,4]{1,0:T(4,128)S(1)} %copy-done.1, f32[10,48,128]{2,1,0:T(8,128)S(1)} %collective-permute-done.refs_3_, ...), custom_call_target="tpu_custom_call" | custom-call | tf_op jit(solution)/shard_map/mold_step/pallas_call | solution.py:624
Async XLA Ops:
  0.6 21.2 %copy-start.1 = (f32[3,4]{1,0:T(4,128)S(1)}, f32[3,4]{1,0:T(4,128)}, u32[]{:S(2)}) copy-start(f32[3,4]{1,0:T(4,128)} %refs_2_.1) | copy-start | bytes 148
  0.6 21.2 %copy-start = (s32[12,48,128]{2,1,0:T(8,128)S(1)}, s32[12,48,128]{2,1,0:T(8,128)}, u32[]{:S(2)}) copy-start(s32[12,48,128]{2,1,0:T(8,128)} %refs_1_.1) | copy-start | bytes 884740
  2.8 19.0 %collective-permute-start = (f32[10,48,128]{2,1,0:T(8,128)S(1)}, f32[10,48,128]{2,1,0:T(8,128)S(1)}, u32[]{:S(2)}, u32[]{:S(2)}) collective-permute-start(f32[10,48,128]{2,1,0:T(8,128)S(1)} %get-tuple-element.12), channel_id=1, source_target_pairs={{0,4},{4,0},{8,12},{12,8},{1,5},{5,1},{9,13},{13,9},{2,6},{6,2},{1... | collective-permute-start | bytes 737288 | tf_op jit(solution)/shard_map/ppermute | solution.py:600
  5.9 15.9 %collective-permute-start.1 = (f32[10,48,128]{2,1,0:T(8,128)S(1)}, f32[10,48,128]{2,1,0:T(8,128)S(1)}, u32[]{:S(2)}, u32[]{:S(2)}) collective-permute-start(f32[10,48,128]{2,1,0:T(8,128)S(1)} %get-tuple-element.13), channel_id=1, source_target_pairs={{4,8},{8,4},{5,9},{9,5},{6,10},{10,6},{7,11},{11,7},{20,24},{24,20... | collective-permute-start | bytes 737288 | tf_op jit(solution)/shard_map/ppermute | solution.py:601
  6.6 1.7 %collective-permute-start.2 = (f32[152,128]{1,0:T(8,128)S(1)}, f32[152,128]{1,0:T(8,128)S(1)}, u32[]{:S(2)}, u32[]{:S(2)}) collective-permute-start(f32[152,128]{1,0:T(8,128)S(1)} %get-tuple-element.14), channel_id=1, source_target_pairs={{0,1},{1,0},{2,3},{3,2},{4,5},{5,4},{6,7},{7,6},{8,9},{9,8},{10,11... | collective-permute-start | bytes 233480 | tf_op jit(solution)/shard_map/ppermute | solution.py:598
  6.7 4.2 %collective-permute-start.3 = (f32[152,128]{1,0:T(8,128)S(1)}, f32[152,128]{1,0:T(8,128)S(1)}, u32[]{:S(2)}, u32[]{:S(2)}) collective-permute-start(f32[152,128]{1,0:T(8,128)S(1)} %get-tuple-element.15), channel_id=1, source_target_pairs={{1,2},{2,1},{3,0},{0,3},{5,6},{6,5},{7,4},{4,7},{9,10},{10,9},{11,... | collective-permute-start | bytes 233480 | tf_op jit(solution)/shard_map/ppermute | solution.py:599
  10.9 10.9 %collective-permute-start.4 = (f32[120,128]{1,0:T(8,128)S(1)}, f32[120,128]{1,0:T(8,128)S(1)}, u32[]{:S(2)}, u32[]{:S(2)}) collective-permute-start(f32[120,128]{1,0:T(8,128)S(1)} %get-tuple-element.17), channel_id=1, source_target_pairs={{0,4},{4,0},{8,12},{12,8},{1,5},{5,1},{9,13},{13,9},{2,6},{6,2},{1... | collective-permute-start | bytes 184328 | tf_op jit(solution)/shard_map/ppermute | solution.py:616
  15.4 6.5 %collective-permute-start.5 = (f32[120,128]{1,0:T(8,128)S(1)}, f32[120,128]{1,0:T(8,128)S(1)}, u32[]{:S(2)}, u32[]{:S(2)}) collective-permute-start(f32[120,128]{1,0:T(8,128)S(1)} %get-tuple-element.18), channel_id=1, source_target_pairs={{4,8},{8,4},{5,9},{9,5},{6,10},{10,6},{7,11},{11,7},{20,24},{24,20... | collective-permute-start | bytes 184328 | tf_op jit(solution)/shard_map/ppermute | solution.py:617
  16.0 5.8 %collective-permute-start.6 = (f32[24,128]{1,0:T(8,128)S(1)}, f32[24,128]{1,0:T(8,128)S(1)}, u32[]{:S(2)}, u32[]{:S(2)}) collective-permute-start(f32[24,128]{1,0:T(8,128)S(1)} %get-tuple-element.19), channel_id=1, source_target_pairs={{0,8},{4,12},{8,0},{12,4},{1,9},{5,13},{9,1},{13,5},{2,10},{6,14},... | collective-permute-start | bytes 36872 | tf_op jit(solution)/shard_map/ppermute | solution.py:619

commit v2 on v1

--- a/solution.py
+++ b/solution.py
@@ -44,7 +44,8 @@
 RIM = 4
 CLOSED = -1e30
 OPEN_ABOVE = -1e29
-VMEM_LIMIT = 48 * 1024 * 1024
+WRAP_COARSE = True
+VMEM_LIMIT = 32 * 1024 * 1024
 
 any_spec = pl.BlockSpec(memory_space=pl.ANY)
 hbm_spec = pl.BlockSpec(memory_space=pltpu.HBM)
@@ -119,7 +120,21 @@
     return x if shift == 0 else pltpu.roll(x, shift, 1)
 
 
-def pack_faces(
+def z_sections(ky):
+    return [ky * g for g in range(4)] + [4 * ky]
+
+
+def y_sections(nz):
+    found, at = [], FACE * nz
+    own = [RIM, RIM, 1, 1, 1, 1, 1]
+    side = [RIM, RIM, 1, 1]
+    for rows in own + side + side + [1, 1, FACE, FACE]:
+        found.append((at, rows))
+        at += rows
+    return found, at + -at % 8
+
+
+def pack_coarse(
     pops,
     flags,
     pot_hbm,
@@ -127,17 +142,13 @@
     ph_hbm,
     mag_hbm,
     tab_hbm,
-    o_z1,
-    o_z2,
-    o_y1,
-    o_y2,
+    o_c1,
+    o_c2,
     o_g,
-    pbuf,
-    ybuf,
-    fpbuf,
-    fybuf,
+    o_p,
+    ebuf,
+    febuf,
     zsc,
-    ysc,
     pot,
     cond,
     ph,
@@ -154,16 +165,10 @@
         )
     ]
     copies = []
-    for side, row in ((0, 0), (1, ny - 8)):
-        copies.append(
-            pltpu.make_async_copy(pops.at[:, :, pl.ds(row, 8), :], ybuf.at[side], sems.at[side])
-        )
-        copies.append(
-            pltpu.make_async_copy(flags.at[:, pl.ds(row, 8), :], fybuf.at[side], sems.at[2 + side])
-        )
-    for side, plane in ((0, 0), (1, nz - 1)):
-        copies.append(pltpu.make_async_copy(pops.at[:, plane], pbuf.at[side], sems.at[4 + side]))
-        copies.append(pltpu.make_async_copy(flags.at[plane], fpbuf.at[side], sems.at[6 + side]))
+    for k, (plane, row) in enumerate(((0, 0), (0, ny - 8), (nz - 1, 0), (nz - 1, ny - 8))):
+        rows = pl.ds(row, 8)
+        copies.append(pltpu.make_async_copy(pops.at[:, plane, rows, :], ebuf.at[k], sems.at[k]))
+        copies.append(pltpu.make_async_copy(flags.at[plane, rows, :], febuf.at[k], sems.at[4 + k]))
     for c in coarse + copies:
         c.start()
     for c in coarse:
@@ -175,22 +180,49 @@
     )
     fields = [pot[...], source, conductivity, phase.astype(jnp.float32), mag[0], mag[1], mag[2]]
     blank = jnp.zeros((ky, 128 - kz * kx), jnp.float32)
+    rows = []
     for g, field in enumerate(fields):
-        row = jnp.concatenate([field[l] for l in range(kz)] + [blank], axis=1)
-        o_g[g, 0:ky, :] = row
-        at = FACE * nz + RIM * g
-        ysc[0, at : at + RIM, :] = row[0:RIM]
-        ysc[1, at : at + RIM, :] = row[ky - RIM : ky]
+        rows.append(jnp.concatenate([field[l] for l in range(kz)] + [blank], axis=1))
+        o_g[g, 0:ky, :] = rows[g]
+    o_p[0:ky, :] = rows[POT]
+    o_p[ky:16, :] = jnp.zeros((16 - ky, 128), jnp.float32)
+    at = z_sections(ky)
+    for side, layer in ((0, 0), (1, kz - 1)):
+        face = [fields[g][layer] for g in (COND, PH, MX, MY)]
+        face = jnp.concatenate(face, axis=1)
+        for k, v in enumerate((rows[POT], rows[SRC], face, rows[MZ])):
+            zsc[side, at[k] : at[k] + ky, :] = v
+    for c in copies:
+        c.wait()
+    for side, leave in ((0, leave_zm), (1, leave_zp)):
+        for y_side, row in ((0, 0), (1, 7)):
+            f = [ebuf[2 * side + y_side, i] for i in range(19)]
+            values = [f[i] for i in leave] + list(moments(f))
+            values.append(febuf[2 * side + y_side].astype(jnp.float32))
+            for k, v in enumerate(values):
+                to = at[4] + FACE * y_side + k
+                zsc[side, to : to + 1, :] = v[row : row + 1]
+        zsc[side, at[4] + 2 * FACE :, :] = jnp.zeros(
+            (zsc.shape[1] - at[4] - 2 * FACE, 128), jnp.float32
+        )
+    up_z = 1 - lax.axis_index("wide") % 2
+    o_c1[...] = zsc[up_z]
+    o_c2[...] = zsc[1 - up_z]
+
+
+def pack_faces(pops, flags, after, o_z1, o_z2, o_y, pbuf, ybuf, fpbuf, fybuf, zsc, sems):
+    nz, ny = pops.shape[1], pops.shape[2]
+    copies = []
+    for side, plane in ((0, 0), (1, nz - 1)):
+        copies.append(pltpu.make_async_copy(pops.at[:, plane], pbuf.at[side], sems.at[side]))
+        copies.append(pltpu.make_async_copy(flags.at[plane], fpbuf.at[side], sems.at[2 + side]))
+    for side, row in ((0, 0), (1, ny - 8)):
+        rows = pl.ds(row, 8)
+        copies.append(pltpu.make_async_copy(pops.at[:, :, rows, :], ybuf.at[side], sems.at[4 + side]))
+        copies.append(pltpu.make_async_copy(flags.at[:, rows, :], fybuf.at[side], sems.at[6 + side]))
+    for c in copies:
+        c.start()
     for c in copies[:4]:
-        c.wait()
-    for side, leave, row in ((0, leave_ym, 0), (1, leave_yp, 7)):
-        for z in range(nz):
-            f = [ybuf[side, i, z] for i in range(19)]
-            values = [f[i] for i in leave] + list(moments(f))
-            values.append(fybuf[side, z].astype(jnp.float32))
-            for k, v in enumerate(values):
-                ysc[side, k * nz + z : k * nz + z + 1, :] = v[row : row + 1]
-    for c in copies[4:]:
         c.wait()
     for side, leave in ((0, leave_zm), (1, leave_zp)):
         for b in range(ny // 8):
@@ -201,43 +233,42 @@
             for k, v in enumerate(values):
                 zsc[side, k, rows, :] = v
     up_z = 1 - lax.axis_index("wide") % 2
+    o_z1[...] = zsc[up_z]
+    o_z2[...] = zsc[1 - up_z]
+    for c in copies[4:]:
+        c.wait()
+    for side, leave, row in ((0, leave_ym, 0), (1, leave_yp, 7)):
+        for z in range(nz):
+            f = [ybuf[side, i, z] for i in range(19)]
+            values = [f[i] for i in leave] + list(moments(f))
+            values.append(fybuf[side, z].astype(jnp.float32))
+            for k, v in enumerate(values):
+                o_y[side, k * nz + z : k * nz + z + 1, :] = v[row : row + 1]
+
+
+def pack_rows(kz, ky, nz, zr1, zr2, pr_up, pr_dn, own, fine, o_y1, o_y2, ysc):
+    even = lax.axis_index("wide") % 2 == 0
+    low = pick(even, zr2[...], zr1[...])
+    high = pick(even, zr1[...], zr2[...])
+    zat = z_sections(ky)
+    sections, total = y_sections(nz)
+    blocks = [own[g, 0:ky, :] for g in range(GROUPS)]
+    blocks += [low[a : a + ky] for a in zat[:4]]
+    blocks += [high[a : a + ky] for a in zat[:4]]
+    blocks += [pr_dn[0:ky, :], pr_up[0:ky, :]]
+    for side in range(2):
+        ysc[side, 0 : FACE * nz, :] = fine[side]
+        for (at, rows), v in zip(sections, blocks):
+            ysc[side, at : at + rows, :] = v[ky - rows : ky] if side else v[0:rows]
+        for (at, rows), v in zip(sections[len(blocks) :], (low, high)):
+            first = zat[4] + FACE * side
+            ysc[side, at : at + rows, :] = v[first : first + FACE]
+        used = sections[-1][0] + FACE
+        if used < total:
+            ysc[side, used:total, :] = jnp.zeros((total - used, 128), jnp.float32)
     up_y = 1 - lax.axis_index("narrow") % 2
     o_y1[...] = ysc[up_y]
     o_y2[...] = ysc[1 - up_y]
-    o_z1[...] = zsc[up_z]
-    o_z2[...] = zsc[1 - up_z]
-
-
-def pack_layers(kz, ky, kx, nz, yr1, yr2, own, o_c1, o_c2, o_p, o_e, zsc):
-    even = lax.axis_index("narrow") % 2 == 0
-    low = pick(even, yr2[...], yr1[...])
-    high = pick(even, yr1[...], yr2[...])
-    lane = lax.broadcasted_iota(jnp.int32, (24, 128), 1)
-    tail = jnp.zeros((24 - ky - 2 * RIM, 128), jnp.float32)
-    for g in range(GROUPS):
-        at = FACE * nz + RIM * g
-        o_e[g, 0:RIM, :] = low[at : at + RIM]
-        o_e[g, RIM : RIM + ky, :] = own[g, 0:ky, :]
-        o_e[g, RIM + ky : 2 * RIM + ky, :] = high[at : at + RIM]
-        o_e[g, 2 * RIM + ky : 24, :] = tail
-    o_p[...] = o_e[POT]
-    for side, layer, plane in ((0, 0, 0), (1, kz - 1, nz - 1)):
-        zsc[side, 0:24, :] = o_e[POT]
-        zsc[side, 24:48, :] = o_e[SRC]
-        parts = [lanes_to(o_e[g], kx * (s - layer)) for s, g in enumerate((COND, PH, MX, MY))]
-        face = pick(lane < kx, parts[0], parts[1])
-        face = pick(lane < 2 * kx, face, parts[2])
-        face = pick(lane < 3 * kx, face, parts[3])
-        zsc[side, 48:72, :] = face
-        zsc[side, 72:96, :] = o_e[MZ]
-        for k in range(FACE):
-            at = k * nz + plane
-            zsc[side, 96 + k : 97 + k, :] = low[at : at + 1]
-            zsc[side, 106 + k : 107 + k, :] = high[at : at + 1]
-        zsc[side, 116:120, :] = jnp.zeros((4, 128), jnp.float32)
-    up_z = 1 - lax.axis_index("wide") % 2
-    o_c1[...] = zsc[up_z]
-    o_c2[...] = zsc[1 - up_z]
 
 
 def step_kernel(
@@ -254,39 +285,49 @@
     zr2,
     pr_up,
     pr_dn,
-    ext,
+    own,
     o_pops,
     o_pot,
     o_lor,
-    buf,
-    fbuf,
+    obuf,
+    ext,
     post,
     fc,
     fu,
     tab,
-    sem_in,
+    sem_tab,
     sem_out,
 ):
-    nz, ny, nx = buf.shape[1:]
+    nz, ny, nx = obuf.shape[1:]
     kz, ky, kx = o_pot.shape
     wi, ni = lax.axis_index("wide"), lax.axis_index("narrow")
-    tcopy = pltpu.make_async_copy(tab_hbm, tab, sem_in.at[nz + 1])
+    tcopy = pltpu.make_async_copy(tab_hbm, tab, sem_tab)
     tcopy.start()
-    fcopy = pltpu.make_async_copy(flags, fbuf, sem_in.at[nz])
-    fcopy.start()
-    for z in range(nz):
-        pltpu.make_async_copy(pops.at[:, z], buf.at[:, z], sem_in.at[z]).start()
-
     even_z = wi % 2 == 0
     even_y = ni % 2 == 0
     has_low_z, has_high_z = wi > 0, wi < W - 1
     has_low_y, has_high_y = ni > 0, ni < N - 1
 
-    def z_low(rows):
-        return pick(even_z, zr2[rows, :], zr1[rows, :])
-
-    def z_high(rows):
-        return pick(even_z, zr1[rows, :], zr2[rows, :])
+    z_lo = pick(even_z, zr2[...], zr1[...])
+    z_hi = pick(even_z, zr1[...], zr2[...])
+    y_lo = pick(even_y, yr2[...], yr1[...])
+    y_hi = pick(even_y, yr1[...], yr2[...])
+    zat = z_sections(ky)
+    sections, _ = y_sections(nz)
+    blocks = [own[g, 0:ky, :] for g in range(GROUPS)]
+    blocks += [z_lo[a : a + ky] for a in zat[:4]]
+    blocks += [z_hi[a : a + ky] for a in zat[:4]]
+    blocks += [pr_dn[0:ky, :], pr_up[0:ky, :]]
+    blank = jnp.zeros((RIM, 128), jnp.float32)
+    for k, ((at, rows), v) in enumerate(zip(sections, blocks)):
+        if rows < RIM:
+            ext[k, 0:RIM, :] = blank
+            ext[k, RIM + ky : 2 * RIM + ky, :] = blank
+        ext[k, RIM - rows : RIM, :] = y_lo[at : at + rows]
+        ext[k, RIM : RIM + ky, :] = v
+        ext[k, RIM + ky : RIM + ky + rows, :] = y_hi[at : at + rows]
+        ext[k, 2 * RIM + ky : 24, :] = jnp.zeros((24 - 2 * RIM - ky, 128), jnp.float32)
+    below, above, far = GROUPS, GROUPS + 4, GROUPS + 8
 
     shape = (24, 128)
     lane = lax.broadcasted_iota(jnp.int32, shape, 1)
@@ -303,18 +344,13 @@
     inner = [inside(-kz), inside(0), inside(kz)]
     beyond = [inside(-2 * kz), inside(2 * kz)]
 
-    def group(at):
-        rows = slice(24 * at, 24 * at + 24)
-        return z_low(rows), z_high(rows)
-
     def three(g, at):
-        a, b = group(at)
-        return [a, ext[g], b]
+        return [ext[below + at], ext[g], ext[above + at]]
 
     zero = jnp.zeros(shape, jnp.float32)
     field = [pick(m, v, 0.0) for m, v in zip(inner, three(POT, 0))]
-    far_low = pick(beyond[0], pr_dn[...], 0.0)
-    far_high = pick(beyond[1], pr_up[...], 0.0)
+    far_low = pick(beyond[0], ext[far], 0.0)
+    far_high = pick(beyond[1], ext[far + 1], 0.0)
     source = three(SRC, 1)
     last = (kz - 1) * kx
 
@@ -351,7 +387,7 @@
     field = sweep(field, zero, zero)
 
     tcopy.wait()
-    face = group(2)
+    face = ext[below + 2], ext[above + 2]
     mz = three(MZ, 3)
 
     def face_fields(slot, g):
@@ -433,11 +469,8 @@
         (True, leave_yp, RIM - 1, 7, has_low_y),
         (False, leave_ym, RIM + ky, 8 + ny, has_high_y),
     ):
-        first, second = (yr2, yr1) if low else (yr1, yr2)
-        values = [
-            pick(even_y, first[nz * k : nz * k + nz, :], second[nz * k : nz * k + nz, :])
-            for k in range(FACE)
-        ]
+        side = y_lo if low else y_hi
+        values = [side[nz * k : nz * k + nz] for k in range(FACE)]
         force = []
         for a in range(3):
             rows = [jnp.broadcast_to(fc[1 + l, a, frow : frow + 1, :], (nz, 128)) for l in range(kz)]
@@ -469,8 +502,8 @@
         (1, 0, 17, 4, has_high_z & has_low_y),
         (1, 1, 16, 3, has_high_z & has_high_y),
     ):
-        at = 96 + FACE * y_side
-        rows = (z_high if z_side else z_low)(slice(at, at + FACE))
+        at = sections[GROUPS + 10 + z_side][0]
+        rows = (y_hi if y_side else y_lo)[at : at + FACE]
         values = [rows[j : j + 1] for j in range(FACE)]
         frow = RIM + ky if y_side else RIM - 1
         force = [fc[(kz + 1) * z_side, a, frow : frow + 1, :] for a in range(3)]
@@ -479,16 +512,17 @@
             yrow = 8 + ny if y_side else 7
             post[i, (nz + 1) * z_side, yrow : yrow + 1, :] = v
 
-    fcopy.wait()
-
-    def collide(z, carry):
-        pltpu.make_async_copy(pops.at[:, z], buf.at[:, z], sem_in.at[z]).wait()
+    lane8 = lax.broadcasted_iota(jnp.int32, (8, 128), 1)
+    not_first = lane8 > 0
+    not_last = lane8 < nx - 1
+
+    def collide(z):
         l = 1 + z // 4
         for b in range(ny // 8):
             rows = slice(8 * b, 8 * b + 8)
             out = slice(8 + 8 * b, 16 + 8 * b)
-            f = [buf[i, z, rows, :] for i in range(19)]
-            flag = fbuf[z, rows, :]
+            f = [pops[i, z, rows, :] for i in range(19)]
+            flag = flags[z, rows, :]
             force = [fu[l, a, rows, :] for a in range(3)]
             rho, mom_x, mom_y, mom_z = moments(f)
             wall = flag == 1
@@ -499,19 +533,12 @@
                 sym, anti = post_pair(i, co)
                 post[i, 1 + z, out, :] = pick(wall, CLOSED, keep * f[i] + (sym + anti))
                 post[j, 1 + z, out, :] = pick(wall, CLOSED, keep * f[j] + (sym - anti))
-        return carry
-
-    lax.fori_loop(0, nz, collide, 0)
-
-    lane8 = lax.broadcasted_iota(jnp.int32, (8, 128), 1)
-    not_first = lane8 > 0
-    not_last = lane8 < nx - 1
-
-    def passing(z, carry):
+
+    def passing(z):
         for b in range(ny // 8):
             rows = slice(8 * b, 8 * b + 8)
             out = slice(8 + 8 * b, 16 + 8 * b)
-            wall = fbuf[z, rows, :] == 1
+            wall = flags[z, rows, :] == 1
             for i in range(19):
                 cx, cy, cz = lattice_dirs[i]
                 own = post[opposite_dir[i], 1 + z, out, :]
@@ -525,14 +552,21 @@
                     if cx == -1:
                         ok = ok & not_last
                     own = pick(ok, v, own)
-                buf[i, z, rows, :] = pick(wall, buf[i, z, rows, :], own)
-        pltpu.make_async_copy(buf.at[:, z], o_pops.at[:, z], sem_out.at[z]).start()
+                obuf[i, z, rows, :] = pick(wall, pops[i, z, rows, :], own)
+        pltpu.make_async_copy(obuf.at[:, z], o_pops.at[:, z], sem_out.at[z]).start()
+
+    collide(0)
+
+    def plane(z, carry):
+        collide(z + 1)
+        passing(z)
         return carry
 
-    lax.fori_loop(0, nz, passing, 0)
+    lax.fori_loop(0, nz - 1, plane, 0)
+    passing(nz - 1)
 
     def drain(z, carry):
-        pltpu.make_async_copy(buf.at[:, z], o_pops.at[:, z], sem_out.at[z]).wait()
+        pltpu.make_async_copy(obuf.at[:, z], o_pops.at[:, z], sem_out.at[z]).wait()
         return carry
 
     lax.fori_loop(0, nz, drain, 0)
@@ -558,29 +592,30 @@
         f32 = jnp.float32
         nz, ny, nx = flags.shape
         kz, ky, kx = potential.shape
-        yrows = FACE * nz + RIM * GROUPS
-        yrows += -yrows % 8
+        zrows = z_sections(ky)[4] + 2 * FACE
+        zrows += -zrows % 8
+        yrows = y_sections(nz)[1]
         params = pltpu.CompilerParams(vmem_limit_bytes=VMEM_LIMIT)
         shape = jax.ShapeDtypeStruct
-        z1, z2, y1, y2, own = pl.pallas_call(
-            pack_faces,
-            name="pack_faces",
+
+        def in_hbm(*xs):
+            return [pltpu.with_memory_space_constraint(x, pltpu.HBM) for x in xs]
+
+        c1, c2, own, pot_rows = pl.pallas_call(
+            pack_coarse,
+            name="pack_coarse",
             out_shape=(
-                shape((FACE, ny, nx), f32),
-                shape((FACE, ny, nx), f32),
-                shape((yrows, nx), f32),
-                shape((yrows, nx), f32),
+                shape((zrows, nx), f32),
+                shape((zrows, nx), f32),
                 shape((GROUPS, 16, nx), f32),
+                shape((16, nx), f32),
             ),
             in_specs=[hbm_spec] * 7,
-            out_specs=[vmem_spec] * 5,
+            out_specs=[vmem_spec] * 4,
             scratch_shapes=[
-                pltpu.VMEM((2, 19, ny, nx), f32),
-                pltpu.VMEM((2, 19, nz, 8, nx), f32),
-                pltpu.VMEM((2, ny, nx), jnp.int32),
-                pltpu.VMEM((2, nz, 8, nx), jnp.int32),
-                pltpu.VMEM((2, FACE, ny, nx), f32),
-                pltpu.VMEM((2, yrows, nx), f32),
+                pltpu.VMEM((4, 19, 8, nx), f32),
+                pltpu.VMEM((4, 8, nx), jnp.int32),
+                pltpu.VMEM((2, zrows, nx), f32),
                 pltpu.VMEM(potential.shape, f32),
                 pltpu.VMEM(conductivity.shape, f32),
                 pltpu.VMEM(coil_phase.shape, jnp.int32),
@@ -590,37 +625,52 @@
             ],
             compiler_params=params,
         )(
-            *[
-                pltpu.with_memory_space_constraint(x, pltpu.HBM)
-                for x in (populations, flags, potential, conductivity, coil_phase, magnetic, phase_table)
-            ]
+            *in_hbm(populations, flags, potential, conductivity, coil_phase, magnetic, phase_table)
         )
-        yr1 = lax.ppermute(y1, "narrow", pair_first(N))
-        yr2 = lax.ppermute(y2, "narrow", pair_second(N, True))
-        fz1 = lax.ppermute(z1, "wide", pair_first(W))
-        fz2 = lax.ppermute(z2, "wide", pair_second(W, False))
-        c1, c2, pot_rows, ext = pl.pallas_call(
-            lambda *refs: pack_layers(kz, ky, kx, nz, *refs),
-            name="pack_layers",
-            out_shape=(
-                shape((120, nx), f32),
-                shape((120, nx), f32),
-                shape((24, nx), f32),
-                shape((GROUPS, 24, nx), f32),
-            ),
-            in_specs=[vmem_spec] * 3,
-            out_specs=[vmem_spec] * 4,
-            scratch_shapes=[pltpu.VMEM((2, 120, nx), f32)],
-            compiler_params=params,
-        )(yr1, yr2, own)
         zr1 = lax.ppermute(c1, "wide", pair_first(W))
-        zr2 = lax.ppermute(c2, "wide", pair_second(W, False))
+        zr2 = lax.ppermute(c2, "wide", pair_second(W, WRAP_COARSE))
         if W == 4:
             pr_up = lax.ppermute(pot_rows, "wide", [(i, i ^ 2) for i in range(W)])
             pr_dn = pr_up
         else:
             pr_up = lax.ppermute(pot_rows, "wide", [(i, i - 2) for i in range(2, W)])
             pr_dn = lax.ppermute(pot_rows, "wide", [(i, i + 2) for i in range(W - 2)])
+        z1, z2, fine = pl.pallas_call(
+            pack_faces,
+            name="pack_faces",
+            out_shape=(
+                shape((FACE, ny, nx), f32),
+                shape((FACE, ny, nx), f32),
+                shape((2, FACE * nz, nx), f32),
+            ),
+            in_specs=[hbm_spec] * 2 + [any_spec],
+            out_specs=[vmem_spec] * 3,
+            scratch_shapes=[
+                pltpu.VMEM((2, 19, ny, nx), f32),
+                pltpu.VMEM((2, 19, nz, 8, nx), f32),
+                pltpu.VMEM((2, ny, nx), jnp.int32),
+                pltpu.VMEM((2, nz, 8, nx), jnp.int32),
+                pltpu.VMEM((2, FACE, ny, nx), f32),
+                pltpu.SemaphoreType.DMA((8,)),
+            ],
+            compiler_params=params,
+        )(*in_hbm(populations, flags), own)
+        z1, z2, fine, zr1, zr2, pr_up, pr_dn = lax.optimization_barrier(
+            (z1, z2, fine, zr1, zr2, pr_up, pr_dn)
+        )
+        fz1 = lax.ppermute(z1, "wide", pair_first(W))
+        fz2 = lax.ppermute(z2, "wide", pair_second(W, False))
+        y1, y2 = pl.pallas_call(
+            lambda *refs: pack_rows(kz, ky, nz, *refs),
+            name="pack_rows",
+            out_shape=(shape((yrows, nx), f32), shape((yrows, nx), f32)),
+            in_specs=[vmem_spec] * 6,
+            out_specs=[vmem_spec] * 2,
+            scratch_shapes=[pltpu.VMEM((2, yrows, nx), f32)],
+            compiler_params=params,
+        )(zr1, zr2, pr_up, pr_dn, own, fine)
+        yr1 = lax.ppermute(y1, "narrow", pair_first(N))
+        yr2 = lax.ppermute(y2, "narrow", pair_second(N, True))
         return pl.pallas_call(
             lambda *refs: step_kernel(W, N, *refs),
             name="mold_step",
@@ -629,22 +679,22 @@
                 shape(potential.shape, f32),
                 shape(magnetic.shape, f32),
             ),
-            in_specs=[any_spec] * 3 + [vmem_spec] * 9,
+            in_specs=[vmem_spec] * 2 + [any_spec] + [vmem_spec] * 9,
             out_specs=[any_spec, vmem_spec, vmem_spec],
             scratch_shapes=[
                 pltpu.VMEM(populations.shape, f32),
-                pltpu.VMEM(flags.shape, jnp.int32),
+                pltpu.VMEM((GROUPS + 10, 24, nx), f32),
                 pltpu.VMEM((19, nz + 2, ny + 16, nx), f32),
                 pltpu.VMEM((kz + 2, 3, 24, nx), f32),
                 pltpu.VMEM((kz + 2, 3, ny, nx), f32),
                 pltpu.SMEM(phase_table.shape, f32),
-                pltpu.SemaphoreType.DMA((nz + 2,)),
+                pltpu.SemaphoreType.DMA,
                 pltpu.SemaphoreType.DMA((nz,)),
             ],
             compiler_params=params,
         )(
-            populations,
-            flags,
+            pltpu.with_memory_space_constraint(populations, pltpu.VMEM),
+            pltpu.with_memory_space_constraint(flags, pltpu.VMEM),
             phase_table,
             fz1,
             fz2,
@@ -654,7 +704,7 @@
             zr2,
             pr_up,
             pr_dn,
-            ext,
+            own,
         )
 
     in_specs = (

time: 29.2 us -> 26.2 us (0.90)
  the two profiles are of different devices: /device:TPU:0 before, /device:TPU:8 now
where the time goes in v2:
time: 26.2 us; the launch traced here: 26.1 us
  Pallas kernels  10.2 us (39%)
  starting transfers between devices  9.85 us (38%)
  waiting for transfers between devices  5.24 us (20%)
  between operations  0.71 us (3%)
    pallas_call x1, Pallas kernels, per_device(): pl.pallas_call(lambda *refs: step_kernel(W, N, *refs), name='mold_step',...  6.79 us
    ppermute x1, starting transfers between devices, per_device(): zr2 = lax.ppermute(c2, 'wide', pair_second(W, WRAP_COARSE))  3.14 us
    ppermute x1, waiting for transfers between devices, per_device(): yr2 = lax.ppermute(y2, 'narrow', pair_second(N, True))  2.8 us
    ppermute x1, starting transfers between devices, per_device(): fz2 = lax.ppermute(z2, 'wide', pair_second(W, False))  2.38 us
    pallas_call x1, Pallas kernels, per_device(): pl.pallas_call(pack_faces, name='pack_faces', out_shape=(shape((FACE, ny,...  2.03 us
    ppermute x1, starting transfers between devices, per_device(): yr2 = lax.ppermute(y2, 'narrow', pair_second(N, True))  1.61 us
    pallas_call x1, Pallas kernels, per_device(): pl.pallas_call(pack_coarse, name='pack_coarse', out_shape=(shape((zrows,...  1.39 us
    ppermute x1, starting transfers between devices, per_device(): fz1 = lax.ppermute(z1, 'wide', pair_first(W))  1.35 us
  transfers between devices with their start and end apart: 7, of which 3 were waited for; matrix products, arithmetic and copies ran while one was open for 0% of the time, Pallas kernels for 8%

profile of v2, /device:TPU:8, one launch (start us, length us, event | category | flops | bytes accessed | tf_op | source)
XLA Modules:
  0.0 26.1 jit_solution(13743476402592624949)
XLA Ops:
  0.6 0.0 copy-start.1
  0.6 0.0 copy-start
  0.7 0.0 copy-start.2
  0.7 1.4 %pack_coarse.1 = (f32[72,128]{1,0:T(8,128)S(1)}, f32[72,128]{1,0:T(8,128)S(1)}, f32[7,16,128]{2,1,0:T(8,128)S(1)}, f32[16,128]{1,0:T(8,128)S(1)}) custom-call(f32[19,12,48,128]{3,2,1,0:T(8,128)} %refs_0_.1, s32[12,48,128]{2,1,0:T(8,128)} %refs_1_.1, f32[3,12,32]{2,1,0:T(8,128)} %pot_hbm.1, f32[3,12,32]{2,1,0:T(8,128)} %cond_hbm.1, s32[3,12,32]{2,1,0:T(8,128)} %ph_hbm.1, ...), custom_call_target="tpu_custom_call" | custom-call | tf_op jit(solution)/shard_map/pack_coarse/pallas_call | solution.py:604
  2.1 0.1 collective-permute-start
  2.1 3.1 %collective-permute-start.1 = (f32[72,128]{1,0:T(8,128)S(1)}, f32[72,128]{1,0:T(8,128)S(1)}, u32[]{:S(2)}, u32[]{:S(2)}) collective-permute-start(f32[72,128]{1,0:T(8,128)S(1)} %get-tuple-element.24), channel_id=1, source_target_pairs={{4,8},{8,4},{12,0},{0,12},{5,9},{9,5},{13,1},{1,13},{6,10},{10,6},... | collective-permute-start | bytes 110600 | tf_op jit(solution)/shard_map/ppermute | solution.py:631
  5.3 1.2 %collective-permute-start.2 = (f32[16,128]{1,0:T(8,128)S(1)}, f32[16,128]{1,0:T(8,128)S(1)}, u32[]{:S(2)}, u32[]{:S(2)}) collective-permute-start(f32[16,128]{1,0:T(8,128)S(1)} %get-tuple-element.25), channel_id=1, source_target_pairs={{0,8},{4,12},{8,0},{12,4},{1,9},{5,13},{9,1},{13,5},{2,10},{6,14},... | collective-permute-start | bytes 24584 | tf_op jit(solution)/shard_map/ppermute | solution.py:633
  6.5 2.0 %pack_faces.1 = (f32[10,48,128]{2,1,0:T(8,128)S(1)}, f32[10,48,128]{2,1,0:T(8,128)S(1)}, f32[2,120,128]{2,1,0:T(8,128)S(1)}) custom-call(f32[19,12,48,128]{3,2,1,0:T(8,128)} %refs_0_.1, s32[12,48,128]{2,1,0:T(8,128)} %refs_1_.1, f32[7,16,128]{2,1,0:T(8,128)S(1)} %get-tuple-element.19.after.refs_4_.refs_11_), custom_call_target="tpu_custom_call" | custom-call | tf_op jit(solution)/shard_map/pack_faces/pallas_call | solution.py:638
  8.6 1.3 %collective-permute-done.2.refs_2_.refs_3_.refs_9_.refs_10_ = f32[16,128]{1,0:T(8,128)S(1)} collective-permute-done((f32[16,128]{1,0:T(8,128)S(1)}, f32[16,128]{1,0:T(8,128)S(1)}, u32[]{:S(2)}, u32[]{:S(2)}) %collective-permute-start.2) | collective-permute-done | bytes 8224 | tf_op jit(solution)/shard_map/ppermute | solution.py:633
  9.8 0.0 collective-permute-done.refs_0_.refs_7_
  9.8 0.0 collective-permute-done.1.refs_1_.refs_8_
  9.8 1.4 %collective-permute-start.3 = (f32[10,48,128]{2,1,0:T(8,128)S(1)}, f32[10,48,128]{2,1,0:T(8,128)S(1)}, u32[]{:S(2)}, u32[]{:S(2)}) collective-permute-start(f32[10,48,128]{2,1,0:T(8,128)S(1)} %get-tuple-element.26), channel_id=1, source_target_pairs={{0,4},{4,0},{8,12},{12,8},{1,5},{5,1},{9,13},{13,9},{2,6},{6,2},{1... | collective-permute-start | bytes 737288 | tf_op jit(solution)/shard_map/ppermute | solution.py:661
  11.2 2.4 %collective-permute-start.4 = (f32[10,48,128]{2,1,0:T(8,128)S(1)}, f32[10,48,128]{2,1,0:T(8,128)S(1)}, u32[]{:S(2)}, u32[]{:S(2)}) collective-permute-start(f32[10,48,128]{2,1,0:T(8,128)S(1)} %get-tuple-element.27), channel_id=1, source_target_pairs={{4,8},{8,4},{5,9},{9,5},{6,10},{10,6},{7,11},{11,7},{20,24},{24,20... | collective-permute-start | bytes 737288 | tf_op jit(solution)/shard_map/ppermute | solution.py:662
  13.6 0.1 collective-permute-start.5
  13.7 1.6 %collective-permute-start.6 = (f32[176,128]{1,0:T(8,128)S(1)}, f32[176,128]{1,0:T(8,128)S(1)}, u32[]{:S(2)}, u32[]{:S(2)}) collective-permute-start(f32[176,128]{1,0:T(8,128)S(1)} %get-tuple-element.34), channel_id=1, source_target_pairs={{1,2},{2,1},{3,0},{0,3},{5,6},{6,5},{7,4},{4,7},{9,10},{10,9},{11,... | collective-permute-start | bytes 270344 | tf_op jit(solution)/shard_map/ppermute | solution.py:673
  15.3 0.0 collective-permute-done.5.refs_5_
  15.3 2.8 %collective-permute-done.6.refs_6_ = f32[176,128]{1,0:T(8,128)S(1)} collective-permute-done((f32[176,128]{1,0:T(8,128)S(1)}, f32[176,128]{1,0:T(8,128)S(1)}, u32[]{:S(2)}, u32[]{:S(2)}) %collective-permute-start.6) | collective-permute-done | bytes 90144 | tf_op jit(solution)/shard_map/ppermute | solution.py:673
  18.1 0.0 collective-permute-done.3.refs_3_
  18.1 1.1 %collective-permute-done.4.refs_4_ = f32[10,48,128]{2,1,0:T(8,128)S(1)} collective-permute-done((f32[10,48,128]{2,1,0:T(8,128)S(1)}, f32[10,48,128]{2,1,0:T(8,128)S(1)}, u32[]{:S(2)}, u32[]{:S(2)}) %collective-permute-start.4) | collective-permute-done | bytes 245792 | tf_op jit(solution)/shard_map/ppermute | solution.py:662
  19.3 0.0 copy-done.1
  19.3 0.0 copy-done
  19.3 0.0 copy-done.2
  19.3 6.8 %mold_step.1 = (f32[19,12,48,128]{3,2,1,0:T(8,128)}, f32[3,12,32]{2,1,0:T(8,128)}, f32[3,3,12,32]{3,2,1,0:T(8,128)}) custom-call(f32[19,12,48,128]{3,2,1,0:T(8,128)S(1)} %copy-done, s32[12,48,128]{2,1,0:T(8,128)S(1)} %copy-done.1, f32[3,4]{1,0:T(4,128)S(1)} %copy-done.2, f32[10,48,128]{2,1,0:T(8,128)S(1)} %collective-permute-done.3.refs_3_, ...), custom_call_target="tpu_custom_call" | custom-call | tf_op jit(solution)/shard_map/mold_step/pallas_call | solution.py:674
  (1 shorter events, 0.0 us)
Async XLA Ops:
  0.6 18.6 %copy-start.1 = (s32[12,48,128]{2,1,0:T(8,128)S(1)}, s32[12,48,128]{2,1,0:T(8,128)}, u32[]{:S(2)}) copy-start(s32[12,48,128]{2,1,0:T(8,128)} %refs_1_.1) | copy-start | bytes 884740
  0.6 18.6 %copy-start = (f32[19,12,48,128]{3,2,1,0:T(8,128)S(1)}, f32[19,12,48,128]{3,2,1,0:T(8,128)}, u32[]{:S(2)}) copy-start(f32[19,12,48,128]{3,2,1,0:T(8,128)} %refs_0_.1) | copy-start | bytes 16809988
  0.7 18.6 %copy-start.2 = (f32[3,4]{1,0:T(4,128)S(1)}, f32[3,4]{1,0:T(4,128)}, u32[]{:S(2)}) copy-start(f32[3,4]{1,0:T(4,128)} %refs_2_.1) | copy-start | bytes 148
  2.1 7.8 %collective-permute-start = (f32[72,128]{1,0:T(8,128)S(1)}, f32[72,128]{1,0:T(8,128)S(1)}, u32[]{:S(2)}, u32[]{:S(2)}) collective-permute-start(f32[72,128]{1,0:T(8,128)S(1)} %get-tuple-element.23), channel_id=1, source_target_pairs={{0,4},{4,0},{8,12},{12,8},{1,5},{5,1},{9,13},{13,9},{2,6},{6,2},{1... | collective-permute-start | bytes 110600 | tf_op jit(solution)/shard_map/ppermute | solution.py:630
  2.1 7.7 %collective-permute-start.1 = (f32[72,128]{1,0:T(8,128)S(1)}, f32[72,128]{1,0:T(8,128)S(1)}, u32[]{:S(2)}, u32[]{:S(2)}) collective-permute-start(f32[72,128]{1,0:T(8,128)S(1)} %get-tuple-element.24), channel_id=1, source_target_pairs={{4,8},{8,4},{12,0},{0,12},{5,9},{9,5},{13,1},{1,13},{6,10},{10,6},... | collective-permute-start | bytes 110600 | tf_op jit(solution)/shard_map/ppermute | solution.py:631
  5.3 4.5 %collective-permute-start.2 = (f32[16,128]{1,0:T(8,128)S(1)}, f32[16,128]{1,0:T(8,128)S(1)}, u32[]{:S(2)}, u32[]{:S(2)}) collective-permute-start(f32[16,128]{1,0:T(8,128)S(1)} %get-tuple-element.25), channel_id=1, source_target_pairs={{0,8},{4,12},{8,0},{12,4},{1,9},{5,13},{9,1},{13,5},{2,10},{6,14},... | collective-permute-start | bytes 24584 | tf_op jit(solution)/shard_map/ppermute | solution.py:633
  9.8 8.3 %collective-permute-start.3 = (f32[10,48,128]{2,1,0:T(8,128)S(1)}, f32[10,48,128]{2,1,0:T(8,128)S(1)}, u32[]{:S(2)}, u32[]{:S(2)}) collective-permute-start(f32[10,48,128]{2,1,0:T(8,128)S(1)} %get-tuple-element.26), channel_id=1, source_target_pairs={{0,4},{4,0},{8,12},{12,8},{1,5},{5,1},{9,13},{13,9},{2,6},{6,2},{1... | collective-permute-start | bytes 737288 | tf_op jit(solution)/shard_map/ppermute | solution.py:661
  11.2 8.1 %collective-permute-start.4 = (f32[10,48,128]{2,1,0:T(8,128)S(1)}, f32[10,48,128]{2,1,0:T(8,128)S(1)}, u32[]{:S(2)}, u32[]{:S(2)}) collective-permute-start(f32[10,48,128]{2,1,0:T(8,128)S(1)} %get-tuple-element.27), channel_id=1, source_target_pairs={{4,8},{8,4},{5,9},{9,5},{6,10},{10,6},{7,11},{11,7},{20,24},{24,20... | collective-permute-start | bytes 737288 | tf_op jit(solution)/shard_map/ppermute | solution.py:662
  13.6 1.7 %collective-permute-start.5 = (f32[176,128]{1,0:T(8,128)S(1)}, f32[176,128]{1,0:T(8,128)S(1)}, u32[]{:S(2)}, u32[]{:S(2)}) collective-permute-start(f32[176,128]{1,0:T(8,128)S(1)} %get-tuple-element.33), channel_id=1, source_target_pairs={{0,1},{1,0},{2,3},{3,2},{4,5},{5,4},{6,7},{7,6},{8,9},{9,8},{10,11... | collective-permute-start | bytes 270344 | tf_op jit(solution)/shard_map/ppermute | solution.py:672
  13.7 4.4 %collective-permute-start.6 = (f32[176,128]{1,0:T(8,128)S(1)}, f32[176,128]{1,0:T(8,128)S(1)}, u32[]{:S(2)}, u32[]{:S(2)}) collective-permute-start(f32[176,128]{1,0:T(8,128)S(1)} %get-tuple-element.34), channel_id=1, source_target_pairs={{1,2},{2,1},{3,0},{0,3},{5,6},{6,5},{7,4},{4,7},{9,10},{10,9},{11,... | collective-permute-start | bytes 270344 | tf_op jit(solution)/shard_map/ppermute | solution.py:673

commit v3 on v2

v3 whole, which is shorter than its diff:
```python
import jax
import jax.numpy as jnp
from jax import lax
from jax.experimental import pallas as pl
from jax.experimental.pallas import tpu as pltpu
from jax.sharding import PartitionSpec as P

lattice_dirs = [
    (0, 0, 0),
    (1, 0, 0),
    (-1, 0, 0),
    (0, 1, 0),
    (0, -1, 0),
    (0, 0, 1),
    (0, 0, -1),
    (1, 1, 0),
    (-1, -1, 0),
    (1, -1, 0),
    (-1, 1, 0),
    (1, 0, 1),
    (-1, 0, -1),
    (1, 0, -1),
    (-1, 0, 1),
    (0, 1, 1),
    (0, -1, -1),
    (0, 1, -1),
    (0, -1, 1),
]
opposite_dir = [0, 2, 1, 4, 3, 6, 5, 8, 7, 10, 9, 12, 11, 14, 13, 16, 15, 18, 17]
pairs = [(i, opposite_dir[i]) for i in range(1, 19) if i < opposite_dir[i]]
relax_time = 0.8
force_scale = 0.02
inlet_speed = 0.05
force_factor = 1.0 - 0.5 / relax_time

leave_yp = [3, 7, 10, 15, 17]
leave_ym = [4, 8, 9, 16, 18]
leave_zp = [5, 11, 14, 15, 18]
leave_zm = [6, 12, 13, 16, 17]

FACE = 10
GROUPS = 7
POT, SRC, COND, PH, MX, MY, MZ = range(GROUPS)
RIM = 4
CLOSED = -1e30
OPEN_ABOVE = -1e29
INNER_COST = pl.CostEstimate(flops=20000000000, bytes_accessed=12000000, transcendentals=0)
VMEM_LIMIT = 24 * 1024 * 1024

any_spec = pl.BlockSpec(memory_space=pl.ANY)
hbm_spec = pl.BlockSpec(memory_space=pltpu.HBM)
vmem_spec = pl.BlockSpec(memory_space=pltpu.VMEM)


def moments(f):
    d = {}
    rho = f[0]
    for i, j in pairs:
        rho = rho + (f[i] + f[j])
        d[i] = f[i] - f[j]
    mx = d[1] + d[7] + d[9] + d[11] + d[13]
    my = d[3] + d[7] - d[9] + d[15] + d[17]
    mz = d[5] + d[11] - d[13] + d[15] - d[17]
    return rho, mx, my, mz


def coefficients(rho, mom, force, fluid, inlet):
    inv = 1.0 / rho
    u = [(m + 0.5 * f) * inv for m, f in zip(mom, force)]
    u = [jnp.where(inlet, c, v) for c, v in zip((0.0, 0.0, -inlet_speed), u)]
    r = jnp.where(fluid, rho * (1.0 / (36.0 * relax_time)), 1.0 / 36.0)
    f = [jnp.where(fluid, v * (force_factor / 36.0), 0.0) for v in force]
    sq = u[0] * u[0] + u[1] * u[1] + u[2] * u[2]
    uf = u[0] * f[0] + u[1] * f[1] + u[2] * f[2]
    base = r * (1.0 - 1.5 * sq) - 3.0 * uf
    ru = [r * v for v in u]
    g = [4.5 * a + 9.0 * b for a, b in zip(ru, f)]
    h = [3.0 * (a + b) for a, b in zip(ru, f)]
    keep = jnp.where(fluid, 1.0 - 1.0 / relax_time, 0.0)
    return keep, base, u, g, h


def along(c, v):
    total = None
    for s, x in zip(c, v):
        if s == 0:
            continue
        if total is None:
            total = x if s > 0 else -x
        else:
            total = total + x if s > 0 else total - x
    return total


def post_pair(i, co):
    keep, base, u, g, h = co
    c = lattice_dirs[i]
    sym = base + along(c, u) * along(c, g)
    anti = along(c, h)
    if sum(abs(s) for s in c) == 1:
        return 2.0 * sym, 2.0 * anti
    return sym, anti


def post_one(i, f, co):
    keep = co[0]
    if i < opposite_dir[i]:
        sym, anti = post_pair(i, co)
        return keep * f + (sym + anti)
    sym, anti = post_pair(opposite_dir[i], co)
    return keep * f + (sym - anti)


def pick(cond, a, b):
    return jnp.where(cond, a, b)


def beyond_face(values, leave, force, there):
    flag = values[9]
    co = coefficients(values[5], values[6:9], force, flag < 0.5, (flag > 1.5) & (flag < 2.5))
    shut = (flag > 0.5) & (flag < 1.5)
    shut = shut | jnp.logical_not(there)
    return [(i, pick(shut, CLOSED, post_one(i, values[k], co))) for k, i in leave]


def lanes_to(x, shift):
    shift = shift % 128
    return x if shift == 0 else pltpu.roll(x, shift, 1)


def y_sections(nz):
    found, at = [], FACE * nz
    for rows in [RIM, RIM, 1, 1, 1, 1, 1] + [RIM] * 4:
        found.append((at, rows))
        at += rows
    return found, at, at + -at % 8


def pack_coarse(
    flags,
    pot_hbm,
    cond_hbm,
    ph_hbm,
    mag_hbm,
    tab_hbm,
    o_c1,
    o_c2,
    o_g,
    fbuf,
    zsc,
    pot,
    cond,
    ph,
    mag,
    tab,
    sems,
):
    nz, ny = flags.shape[0], flags.shape[1]
    kz, ky, kx = pot.shape
    coarse = [
        pltpu.make_async_copy(a, b, sems.at[2 + k])
        for k, (a, b) in enumerate(
            ((tab_hbm, tab), (ph_hbm, ph), (cond_hbm, cond), (pot_hbm, pot), (mag_hbm, mag))
        )
    ]
    copies = [
        pltpu.make_async_copy(flags.at[plane], fbuf.at[k], sems.at[k])
        for k, plane in enumerate((0, nz - 1))
    ]
    for c in coarse + copies:
        c.start()
    for c in coarse:
        c.wait()
    phase = ph[...]
    conductivity = cond[...]
    source = conductivity * jnp.where(
        phase == 0, tab[0, 0], jnp.where(phase == 1, tab[1, 0], tab[2, 0])
    )
    fields = [pot[...], source, conductivity, phase.astype(jnp.float32), mag[0], mag[1], mag[2]]
    blank = jnp.zeros((ky, 128 - kz * kx), jnp.float32)
    for g, field in enumerate(fields):
        row = jnp.concatenate([field[l] for l in range(kz)] + [blank], axis=1)
        o_g[g, 0:ky, :] = row
        if g <= SRC:
            for side in range(2):
                zsc[side, ny + ky * g : ny + ky * g + ky, :] = row
    for c in copies:
        c.wait()
    for side in range(2):
        zsc[side, 0:ny, :] = fbuf[side].astype(jnp.float32)
    up_z = 1 - lax.axis_index("wide") % 2
    o_c1[...] = zsc[up_z]
    o_c2[...] = zsc[1 - up_z]


def pack_y_faces(pops, flags, after, o_y, ybuf, fybuf, sems):
    nz, ny = pops.shape[1], pops.shape[2]
    copies = []
    for side, row in ((0, 0), (1, ny - 8)):
        rows = pl.ds(row, 8)
        copies.append(pltpu.make_async_copy(pops.at[:, :, rows, :], ybuf.at[side], sems.at[side]))
        copies.append(pltpu.make_async_copy(flags.at[:, rows, :], fybuf.at[side], sems.at[2 + side]))
    for c in copies:
        c.start()
    for c in copies:
        c.wait()
    for side, leave, row in ((0, leave_ym, 0), (1, leave_yp, 7)):
        for z in range(nz):
            f = [ybuf[side, i, z] for i in range(19)]
            values = [f[i] for i in leave] + list(moments(f))
            values.append(fybuf[side, z].astype(jnp.float32))
            for k, v in enumerate(values):
                o_y[side, k * nz + z : k * nz + z + 1, :] = v[row : row + 1]


def coarse_blocks(ny, ky, low, high, own):
    blocks = [own[g, 0:ky, :] for g in range(GROUPS)]
    for side in (low, high):
        blocks += [side[ny + ky * g : ny + ky * g + ky] for g in (POT, SRC)]
    return blocks


def pack_rows(ny, ky, nz, zr1, zr2, own, fine, o_y1, o_y2, ysc):
    even = lax.axis_index("wide") % 2 == 0
    low = pick(even, zr2[...], zr1[...])
    high = pick(even, zr1[...], zr2[...])
    sections, used, total = y_sections(nz)
    blocks = coarse_blocks(ny, ky, low, high, own)
    for side in range(2):
        ysc[side, 0 : FACE * nz, :] = fine[side]
        for (at, rows), v in zip(sections, blocks):
            ysc[side, at : at + rows, :] = v[ky - rows : ky] if side else v[0:rows]
        if used < total:
            ysc[side, used:total, :] = jnp.zeros((total - used, 128), jnp.float32)
    up_y = 1 - lax.axis_index("narrow") % 2
    o_y1[...] = ysc[up_y]
    o_y2[...] = ysc[1 - up_y]


def collide_plane(z, to, pops, flags, fu, post):
    ny = flags.shape[1]
    l = z // 4
    for b in range(ny // 8):
        rows = slice(8 * b, 8 * b + 8)
        out = slice(8 + 8 * b, 16 + 8 * b)
        f = [pops[i, z, rows, :] for i in range(19)]
        flag = flags[z, rows, :]
        force = [fu[l, a, rows, :] for a in range(3)]
        rho, mom_x, mom_y, mom_z = moments(f)
        wall = flag == 1
        co = coefficients(rho, (mom_x, mom_y, mom_z), force, flag == 0, flag == 2)
        keep = co[0]
        post[0, to, out, :] = pick(wall, CLOSED, keep * f[0] + 12.0 * co[1])
        for i, j in pairs:
            sym, anti = post_pair(i, co)
            post[i, to, out, :] = pick(wall, CLOSED, keep * f[i] + (sym + anti))
            post[j, to, out, :] = pick(wall, CLOSED, keep * f[j] + (sym - anti))


def pass_plane(z, pops, flags, here, source, put):
    ny, nx = flags.shape[1:]
    lane8 = lax.broadcasted_iota(jnp.int32, (8, 128), 1)
    not_first = lane8 > 0
    not_last = lane8 < nx - 1
    for b in range(ny // 8):
        rows = slice(8 * b, 8 * b + 8)
        out = slice(8 + 8 * b, 16 + 8 * b)
        wall = flags[z, rows, :] == 1
        for i in range(19):
            cx, cy, cz = lattice_dirs[i]
            own = here(opposite_dir[i], out)
            if i > 0:
                v = source(i, cz, slice(8 + 8 * b - cy, 16 + 8 * b - cy))
                if cx != 0:
                    v = pltpu.roll(v, cx % nx, 1)
                ok = v > OPEN_ABOVE
                if cx == 1:
                    ok = ok & not_first
                if cx == -1:
                    ok = ok & not_last
                own = pick(ok, v, own)
            put(i, rows, pick(wall, pops[i, z, rows, :], own))


def face_kernel(
    W,
    N,
    pops,
    flags,
    tab_hbm,
    yr1,
    yr2,
    zr1,
    zr2,
    own,
    o_pot,
    o_lor,
    o_f1,
    o_f2,
    post,
    o_yh,
    fu,
    ext,
    fc,
    zsc,
    tab,
    sem_tab,
):
    nz, ny, nx = flags.shape
    kz, ky, kx = o_pot.shape
    wi, ni = lax.axis_index("wide"), lax.axis_index("narrow")
    tcopy = pltpu.make_async_copy(tab_hbm, tab, sem_tab)
    tcopy.start()
    even_z = wi % 2 == 0
    even_y = ni % 2 == 0
    has_low_y, has_high_y = ni > 0, ni < N - 1

    z_lo = pick(even_z, zr2[...], zr1[...])
    z_hi = pick(even_z, zr1[...], zr2[...])
    y_lo = pick(even_y, yr2[...], yr1[...])
    y_hi = pick(even_y, yr1[...], yr2[...])
    sections = y_sections(nz)[0]
    blocks = coarse_blocks(ny, ky, z_lo, z_hi, own)
    blank = jnp.zeros((RIM, 128), jnp.float32)
    for k, ((at, rows), v) in enumerate(zip(sections, blocks)):
        if rows < RIM:
            ext[k, 0:RIM, :] = blank
            ext[k, RIM + ky : 2 * RIM + ky, :] = blank
        ext[k, RIM - rows : RIM, :] = y_lo[at : at + rows]
        ext[k, RIM : RIM + ky, :] = v
        ext[k, RIM + ky : RIM + ky + rows, :] = y_hi[at : at + rows]
        ext[k, 2 * RIM + ky : 24, :] = jnp.zeros((24 - 2 * RIM - ky, 128), jnp.float32)
    below, above = GROUPS, GROUPS + 2

    shape = (24, 128)
    lane = lax.broadcasted_iota(jnp.int32, shape, 1)
    row = lax.broadcasted_iota(jnp.int32, shape, 0)
    y_at = ni * ky + row - RIM
    y_in = (y_at >= 0) & (y_at < ky * N)
    layer = lane // kx
    x_at = lane - layer * kx

    def inside(first):
        z_at = wi * kz + first + layer
        return y_in & (z_at >= 0) & (z_at < kz * W) & (layer < kz)

    inner = [inside(-kz), inside(0), inside(kz)]

    def three(g):
        return [ext[below + g], ext[g], ext[above + g]]

    zero = jnp.zeros(shape, jnp.float32)
    field = [pick(m, v, 0.0) for m, v in zip(inner, three(POT))]
    source = three(SRC)
    last = (kz - 1) * kx

    def next_z(here, above):
        return pick(lane < last, lanes_to(here, -kx), lanes_to(above, last))

    def prev_z(here, below):
        return pick(lane >= kx, lanes_to(here, kx), lanes_to(below, -last))

    def next_x(v):
        return pick(x_at == kx - 1, 0.0, lanes_to(v, -1))

    def prev_x(v):
        return pick(x_at == 0, 0.0, lanes_to(v, 1))

    def next_y(v):
        return pltpu.roll(v, 23, 0)

    def prev_y(v):
        return pltpu.roll(v, 1, 0)

    def sweep(values, lower, upper):
        chain = [lower] + values + [upper]
        new = []
        for k in range(3):
            v = values[k]
            total = next_z(v, chain[k + 2]) + prev_z(v, chain[k])
            total = total + next_y(v) + prev_y(v)
            total = total + next_x(v) + prev_x(v)
            new.append(pick(inner[k], (total + source[k]) / 6.0, 0.0))
        return new

    field = sweep(field, zero, zero)
    field = sweep(field, zero, zero)

    tcopy.wait()
    v = field[1]
    grad = (
        (next_x(v) - prev_x(v)) * 0.5,
        (next_y(v) - prev_y(v)) * 0.5,
        (next_z(v, field[2]) - prev_z(v, field[0])) * 0.5,
    )
    phase = ext[PH]
    cur = []
    for a in range(3):
        applied = pick(phase < 0.5, tab[0, 1 + a], pick(phase < 1.5, tab[1, 1 + a], tab[2, 1 + a]))
        cur.append(ext[COND] * (applied - grad[a]))
    lorentz = [
        cur[1] * ext[MZ] - cur[2] * ext[MY],
        cur[2] * ext[MX] - cur[0] * ext[MZ],
        cur[0] * ext[MY] - cur[1] * ext[MX],
    ]
    for l in range(kz):
        o_pot[l] = lanes_to(field[1], -kx * l)[RIM : RIM + ky, 0:kx]
        for a in range(3):
            o_lor[a, l] = lanes_to(lorentz[a], -kx * l)[RIM : RIM + ky, 0:kx]

    src = lax.broadcasted_iota(jnp.int32, (128, 128), 0)
    dst = lax.broadcasted_iota(jnp.int32, (128, 128), 1) // (nx // kx)

    def widened(stack, l):
        choose = jnp.where(src == kx * l + dst, 1.0, 0.0)
        return lax.dot_general(
            stack,
            choose,
            (((1,), (0,)), ((), ())),
            precision=lax.Precision.HIGHEST,
            preferred_element_type=jnp.float32,
        )

    stack = jnp.concatenate([v * force_scale for v in lorentz], axis=0)
    wide = [widened(stack, l) for l in range(kz)]
    sub = lax.broadcasted_iota(jnp.int32, (8, 128), 0)
    for l in range(kz):
        for a in range(3):
            fc[l, a] = wide[l][24 * a : 24 * a + 24]
    for l in range(kz):
        for a in range(3):
            for b in range(ny // 8):
                first = jnp.broadcast_to(fc[l, a, pl.ds(RIM + 2 * b, 1), :], (8, 128))
                second = jnp.broadcast_to(fc[l, a, pl.ds(RIM + 2 * b + 1, 1), :], (8, 128))
                fu[l, a, 8 * b : 8 * b + 8, :] = pick(sub < 4, first, second)

    zrow = lax.broadcasted_iota(jnp.int32, (nz, 128), 0)
    for low, leave, frow, at, there in (
        (True, leave_yp, RIM - 1, 7, has_low_y),
        (False, leave_ym, RIM + ky, 8 + ny, has_high_y),
    ):
        side = y_lo if low else y_hi
        values = [side[nz * k : nz * k + nz] for k in range(FACE)]
        force = []
        for a in range(3):
            rows = [jnp.broadcast_to(fc[l, a, frow : frow + 1, :], (nz, 128)) for l in range(kz)]
            v = rows[kz - 1]
            for l in range(kz - 2, -1, -1):
                v = pick(zrow < 4 * (l + 1), rows[l], v)
            force.append(v)
        there_b = jnp.broadcast_to(there, (nz, 128))
        for k, (i, v) in enumerate(beyond_face(values, list(enumerate(leave)), force, there_b)):
            o_yh[0 if low else 1, k, 0:nz, :] = v
            for to, z in enumerate((0, nz - 1)):
                post[i, to, at : at + 1, :] = v[z : z + 1]

    collide_plane(0, 0, pops, flags, fu, post)
    collide_plane(nz - 1, 1, pops, flags, fu, post)
    for side, leave, edges in ((0, leave_zm, (17, 16)), (1, leave_zp, (15, 18))):
        for k, i in enumerate(leave):
            zsc[side, ny * k : ny * k + ny, :] = post[i, side, 8 : 8 + ny, :]
        at = 5 * ny
        z = side * (nz - 1)
        for y_side, (i, rows) in enumerate(zip(edges, (y_lo, y_hi))):
            yrow = 8 + ny if y_side else 7
            zsc[side, at + y_side : at + y_side + 1, :] = post[i, side, yrow : yrow + 1, :]
            row = 9 * nz + z
            zsc[side, at + 2 + y_side : at + 3 + y_side, :] = rows[row : row + 1]
        zsc[side, at + 4 : at + 8, :] = jnp.zeros((4, 128), jnp.float32)
    up_z = 1 - wi % 2
    o_f1[...] = zsc[up_z]
    o_f2[...] = zsc[1 - up_z]


def inner_kernel(pops, flags, faces, yh, fu, o_pops, o_near, obuf, post, sem_out):
    nz, ny, nx = flags.shape
    for i in range(19):
        post[i, 0] = faces[i, 0]
        post[i, nz - 1] = faces[i, 1]
    for side, leave, at in ((0, leave_yp, 7), (1, leave_ym, 8 + ny)):
        for k, i in enumerate(leave):
            rows = yh[side, k]
            for z in range(1, nz - 1):
                post[i, z, at : at + 1, :] = rows[z : z + 1]

    def passing(z):
        def put(i, rows, v):
            obuf[i, z, rows, :] = v

        pass_plane(
            z,
            pops,
            flags,
            lambda i, rows: post[i, z, rows, :],
            lambda i, cz, rows: post[i, z - cz, rows, :],
            put,
        )
        pltpu.make_async_copy(obuf.at[:, z], o_pops.at[:, z], sem_out.at[z]).start()

    collide_plane(1, 1, pops, flags, fu, post)

    def plane(z, carry):
        collide_plane(z + 1, z + 1, pops, flags, fu, post)
        passing(z)
        return carry

    lax.fori_loop(1, nz - 2, plane, 0)
    passing(nz - 2)
    for i in range(19):
        o_near[i, 0] = post[i, 1]
        o_near[i, 1] = post[i, nz - 2]

    def drain(z, carry):
        pltpu.make_async_copy(obuf.at[:, z], o_pops.at[:, z], sem_out.at[z]).wait()
        return carry

    lax.fori_loop(1, nz - 1, drain, 0)


def outer_kernel(
    W, pops, flags, faces, near, fz1, fz2, zr1, zr2, half, o_pops, obuf, halo, sem_out
):
    nz, ny, nx = flags.shape
    wi = lax.axis_index("wide")
    even_z = wi % 2 == 0
    for side, leave, edges, there in (
        (0, leave_zp, (15, 18), wi > 0),
        (1, leave_zm, (17, 16), wi < W - 1),
    ):
        f_odd, f_even = (fz2, fz1) if side else (fz1, fz2)
        c_odd, c_even = (zr2, zr1) if side else (zr1, zr2)
        gone = jnp.broadcast_to(jnp.logical_not(there), (8, 128))
        for b in range(ny // 8):
            rows = slice(8 * b, 8 * b + 8)
            flag = pick(even_z, c_even[rows, :], c_odd[rows, :])
            shut = ((flag > 0.5) & (flag < 1.5)) | gone
            for k in range(5):
                at = slice(ny * k + 8 * b, ny * k + 8 * b + 8)
                v = pick(even_z, f_even[at, :], f_odd[at, :])
                halo[side, k, 8 + 8 * b : 16 + 8 * b, :] = pick(shut, CLOSED, v)
        at = slice(5 * ny, 5 * ny + 8)
        v = pick(even_z, f_even[at, :], f_odd[at, :])
        for y_side, i in enumerate(edges):
            flag = v[2 + y_side : 3 + y_side]
            shut = ((flag > 0.5) & (flag < 1.5)) | gone[0:1]
            yrow = 8 + ny if y_side else 7
            k = leave.index(i)
            edge = pick(shut, CLOSED, v[y_side : y_side + 1])
            halo[side, k, yrow : yrow + 1, :] = edge
    copies = []
    for side, z, leave in ((0, 0, leave_zp), (1, nz - 1, leave_zm)):

        def source(i, cz, rows, side=side, leave=leave):
            if cz == 0:
                return faces[i, side, rows, :]
            if i in leave:
                return halo[side, leave.index(i), rows, :]
            return near[i, side, rows, :]

        def put(i, rows, v, side=side):
            obuf[i, side, rows, :] = v

        pass_plane(z, pops, flags, lambda i, rows: faces[i, side, rows, :], source, put)
        copies.append(pltpu.make_async_copy(obuf.at[:, side], o_pops.at[:, z], sem_out.at[side]))
        copies[-1].start()
    for c in copies:
        c.wait()


def pair_first(size):
    return [(i, i ^ 1) for i in range(size)]


def pair_second(size, groups):
    found = []
    for g in range(groups):
        for i in range(size):
            j = i + 1 if i % 2 else i - 1
            if 0 <= j < size:
                found.append((g * size + i, g * size + j))
            elif g ^ 1 < groups:
                found.append((g * size + i, (g ^ 1) * size + i))
    return found


def solution(mesh):
    G, W, N = mesh.shape["groups"], mesh.shape["wide"], mesh.shape["narrow"]

    def per_device(populations, flags, potential, conductivity, coil_phase, phase_table, magnetic):
        f32 = jnp.float32
        nz, ny, nx = flags.shape
        kz, ky, kx = potential.shape
        zrows = ny + 2 * ky
        yrows = y_sections(nz)[2]
        frows = 5 * ny + 8
        params = pltpu.CompilerParams(vmem_limit_bytes=VMEM_LIMIT)
        shape = jax.ShapeDtypeStruct

        def in_hbm(*xs):
            return [pltpu.with_memory_space_constraint(x, pltpu.HBM) for x in xs]

        c1, c2, own = pl.pallas_call(
            pack_coarse,
            name="pack_coarse",
            out_shape=(
                shape((zrows, nx), f32),
                shape((zrows, nx), f32),
                shape((GROUPS, 16, nx), f32),
            ),
            in_specs=[hbm_spec] * 6,
            out_specs=[vmem_spec] * 3,
            scratch_shapes=[
                pltpu.VMEM((2, ny, nx), jnp.int32),
                pltpu.VMEM((2, zrows, nx), f32),
                pltpu.VMEM(potential.shape, f32),
                pltpu.VMEM(conductivity.shape, f32),
                pltpu.VMEM(coil_phase.shape, jnp.int32),
                pltpu.VMEM(magnetic.shape, f32),
                pltpu.SMEM(phase_table.shape, f32),
                pltpu.SemaphoreType.DMA((7,)),
            ],
            compiler_params=params,
        )(*in_hbm(flags, potential, conductivity, coil_phase, magnetic, phase_table))
        zr1 = lax.ppermute(c1, "wide", pair_first(W))
        zr2 = lax.ppermute(c2, ("groups", "wide"), pair_second(W, G))
        fine = pl.pallas_call(
            pack_y_faces,
            name="pack_y_faces",
            out_shape=shape((2, FACE * nz, nx), f32),
            in_specs=[hbm_spec] * 2 + [any_spec],
            out_specs=vmem_spec,
            scratch_shapes=[
                pltpu.VMEM((2, 19, nz, 8, nx), f32),
                pltpu.VMEM((2, nz, 8, nx), jnp.int32),
                pltpu.SemaphoreType.DMA((4,)),
            ],
            compiler_params=params,
        )(*in_hbm(populations, flags), own)
        y1, y2 = pl.pallas_call(
            lambda *refs: pack_rows(ny, ky, nz, *refs),
            name="pack_rows",
            out_shape=(shape((yrows, nx), f32), shape((yrows, nx), f32)),
            in_specs=[vmem_spec] * 4,
            out_specs=[vmem_spec] * 2,
            scratch_shapes=[pltpu.VMEM((2, yrows, nx), f32)],
            compiler_params=params,
        )(zr1, zr2, own, fine)
        yr1 = lax.ppermute(y1, "narrow", pair_first(N))
        yr2 = lax.ppermute(y2, ("groups", "narrow"), pair_second(N, G))
        pops_near = pltpu.with_memory_space_constraint(populations, pltpu.VMEM)
        flags_near = pltpu.with_memory_space_constraint(flags, pltpu.VMEM)
        pot_out, lorentz, f1, f2, faces, yh, force = pl.pallas_call(
            lambda *refs: face_kernel(W, N, *refs),
            name="faces",
            out_shape=(
                shape(potential.shape, f32),
                shape(magnetic.shape, f32),
                shape((frows, nx), f32),
                shape((frows, nx), f32),
                shape((19, 2, ny + 16, nx), f32),
                shape((2, 5, 16, nx), f32),
                shape((kz, 3, ny, nx), f32),
            ),
            in_specs=[vmem_spec] * 2 + [any_spec] + [vmem_spec] * 5,
            out_specs=[vmem_spec] * 7,
            scratch_shapes=[
                pltpu.VMEM((GROUPS + 4, 24, nx), f32),
                pltpu.VMEM((kz, 3, 24, nx), f32),
                pltpu.VMEM((2, frows, nx), f32),
                pltpu.SMEM(phase_table.shape, f32),
                pltpu.SemaphoreType.DMA,
            ],
            compiler_params=params,
        )(pops_near, flags_near, phase_table, yr1, yr2, zr1, zr2, own)
        fz1 = lax.ppermute(f1, "wide", pair_first(W))
        fz2 = lax.ppermute(f2, ("groups", "wide"), pair_second(W, G))
        half, near = pl.pallas_call(
            inner_kernel,
            name="inner",
            out_shape=(shape(populations.shape, f32), shape((19, 2, ny + 16, nx), f32)),
            in_specs=[vmem_spec] * 5,
            out_specs=[hbm_spec, vmem_spec],
            scratch_shapes=[
                pltpu.VMEM(populations.shape, f32),
                pltpu.VMEM((19, nz, ny + 16, nx), f32),
                pltpu.SemaphoreType.DMA((nz,)),
            ],
            compiler_params=params,
            cost_estimate=INNER_COST,
        )(pops_near, flags_near, faces, yh, force)
        passed = pl.pallas_call(
            lambda *refs: outer_kernel(W, *refs),
            name="outer",
            out_shape=shape(populations.shape, f32),
            in_specs=[vmem_spec] * 8 + [hbm_spec],
            out_specs=hbm_spec,
            input_output_aliases={8: 0},
            scratch_shapes=[
                pltpu.VMEM((19, 2, ny, nx), f32),
                pltpu.VMEM((2, 5, ny + 16, nx), f32),
                pltpu.SemaphoreType.DMA((2,)),
            ],
            compiler_params=params,
        )(pops_near, flags_near, faces, near, fz1, fz2, zr1, zr2, half)
        return passed, pot_out, lorentz

    in_specs = (
        P(None, ("groups", "wide"), "narrow", None),
        P(("groups", "wide"), "narrow", None),
        P(("groups", "wide"), "narrow", None),
        P(("groups", "wide"), "narrow", None),
        P(("groups", "wide"), "narrow", None),
        P(),
        P(None, ("groups", "wide"), "narrow", None),
    )
    out_specs = (
        P(None, ("groups", "wide"), "narrow", None),
        P(("groups", "wide"), "narrow", None),
        P(None, ("groups", "wide"), "narrow", None),
    )
    return jax.shard_map(
        per_device, mesh=mesh, in_specs=in_specs, out_specs=out_specs, check_vma=False
    )
```

time: 26.2 us -> 23.7 us (0.905)
  the two profiles are of different devices: /device:TPU:8 before, /device:TPU:0 now
where the time goes in v3:
time: 23.7 us; the launch traced here: 23.5 us
  Pallas kernels  10.2 us (43%)
  starting transfers between devices  8.98 us (38%)
  waiting for transfers between devices  3.63 us (15%)
  between operations  0.73 us (3%)
    pallas_call x1, Pallas kernels, per_device(): pl.pallas_call(inner_kernel, name='inner', out_shape=(shape(populations.s...  4.31 us
    ppermute x1, starting transfers between devices, per_device(): zr1 = lax.ppermute(c1, 'wide', pair_first(W))  3.09 us
    ppermute x1, waiting for transfers between devices, per_device(): yr2 = lax.ppermute(y2, ('groups', 'narrow'), pair_second(N, G))  2.87 us
    pallas_call x1, Pallas kernels, per_device(): pl.pallas_call(lambda *refs: face_kernel(W, N, *refs), name='faces', out_...  1.84 us
    pallas_call x1, Pallas kernels, per_device(): pl.pallas_call(pack_y_faces, name='pack_y_faces', out_shape=shape((2, FAC...  1.67 us
    ppermute x1, starting transfers between devices, per_device(): yr2 = lax.ppermute(y2, ('groups', 'narrow'), pair_second(N, G))  1.58 us
    ppermute x1, starting transfers between devices, per_device(): zr2 = lax.ppermute(c2, ('groups', 'wide'), pair_second(W, G))  1.52 us
    ppermute x1, starting transfers between devices, per_device(): fz2 = lax.ppermute(f2, ('groups', 'wide'), pair_second(W, G))  1.52 us
  transfers between devices with their start and end apart: 6, of which 2 were waited for; matrix products, arithmetic and copies ran while one was open for 0% of the time, Pallas kernels for 25%

profile of v3, /device:TPU:0, one launch (start us, length us, event | category | flops | bytes accessed | tf_op | source)
XLA Modules:
  0.0 23.5 jit_solution(11425331609231033051)
XLA Ops:
  0.6 0.0 copy-start.1
  0.6 0.0 copy-start.2
  0.7 0.0 copy-start
  0.7 1.2 %pack_coarse.1 = (f32[72,128]{1,0:T(8,128)S(1)}, f32[72,128]{1,0:T(8,128)S(1)}, f32[7,16,128]{2,1,0:T(8,128)S(1)}) custom-call(s32[12,48,128]{2,1,0:T(8,128)} %refs_1_.3, f32[3,12,32]{2,1,0:T(8,128)} %pot_hbm.1, f32[3,12,32]{2,1,0:T(8,128)} %cond_hbm.1, s32[3,12,32]{2,1,0:T(8,128)} %ph_hbm.1, f32[3,3,12,32]{3,2,1,0:T(8,128)} %mag_hbm.1, f32[3,4]{1,0:T(4,128)} %refs_2_.1), custom_call_target="tpu_custom_call" | custom-call | tf_op jit(solution)/shard_map/pack_coarse/pallas_call | solution.py:602
  1.9 3.1 %collective-permute-start = (f32[72,128]{1,0:T(8,128)S(1)}, f32[72,128]{1,0:T(8,128)S(1)}, u32[]{:S(2)}, u32[]{:S(2)}) collective-permute-start(f32[72,128]{1,0:T(8,128)S(1)} %get-tuple-element.17), channel_id=1, source_target_pairs={{0,4},{4,0},{8,12},{12,8},{1,5},{5,1},{9,13},{13,9},{2,6},{6,2},{1... | collective-permute-start | bytes 110600 | tf_op jit(solution)/shard_map/ppermute | solution.py:624
  5.0 1.5 %collective-permute-start.1 = (f32[72,128]{1,0:T(8,128)S(1)}, f32[72,128]{1,0:T(8,128)S(1)}, u32[]{:S(2)}, u32[]{:S(2)}) collective-permute-start(f32[72,128]{1,0:T(8,128)S(1)} %get-tuple-element.18), channel_id=1, source_target_pairs={{0,16},{4,8},{8,4},{12,28},{16,0},{20,24},{24,20},{28,12},{1,17},{... | collective-permute-start | bytes 110600 | tf_op jit(solution)/shard_map/ppermute | solution.py:625
  6.5 1.7 %pack_y_faces.1.refs_3_ = f32[2,120,128]{2,1,0:T(8,128)S(1)} custom-call(f32[19,12,48,128]{3,2,1,0:T(8,128)} %refs_0_.3, s32[12,48,128]{2,1,0:T(8,128)} %refs_1_.3, f32[7,16,128]{2,1,0:T(8,128)S(1)} %get-tuple-element.19.after.refs_2_.refs_7_), custom_call_target="tpu_custom_call" | custom-call | tf_op jit(solution)/shard_map/pack_y_faces/pallas_call | solution.py:626
  8.2 0.0 collective-permute-done.refs_0_.refs_5_.refs_6_
  8.2 0.7 %collective-permute-done.1.refs_1_.refs_6_.refs_7_ = f32[72,128]{1,0:T(8,128)S(1)} collective-permute-done((f32[72,128]{1,0:T(8,128)S(1)}, f32[72,128]{1,0:T(8,128)S(1)}, u32[]{:S(2)}, u32[]{:S(2)}) %collective-permute-start.1) | collective-permute-done | bytes 36896 | tf_op jit(solution)/shard_map/ppermute | solution.py:625
  9.0 0.1 collective-permute-start.2
  9.0 1.6 %collective-permute-start.3 = (f32[152,128]{1,0:T(8,128)S(1)}, f32[152,128]{1,0:T(8,128)S(1)}, u32[]{:S(2)}, u32[]{:S(2)}) collective-permute-start(f32[152,128]{1,0:T(8,128)S(1)} %get-tuple-element.21), channel_id=1, source_target_pairs={{0,16},{1,2},{2,1},{3,19},{16,0},{17,18},{18,17},{19,3},{4,20},{5,... | collective-permute-start | bytes 233480 | tf_op jit(solution)/shard_map/ppermute | solution.py:649
  10.6 0.0 collective-permute-done.2.refs_3_
  10.6 2.9 %collective-permute-done.3.refs_4_ = f32[152,128]{1,0:T(8,128)S(1)} collective-permute-done((f32[152,128]{1,0:T(8,128)S(1)}, f32[152,128]{1,0:T(8,128)S(1)}, u32[]{:S(2)}, u32[]{:S(2)}) %collective-permute-start.3) | collective-permute-done | bytes 77856 | tf_op jit(solution)/shard_map/ppermute | solution.py:649
  13.5 0.0 copy-done.1
  13.5 0.0 copy-done.2
  13.5 0.0 copy-done
  13.5 1.8 %faces.1 = (f32[3,12,32]{2,1,0:T(8,128)}, f32[3,3,12,32]{3,2,1,0:T(8,128)}, f32[248,128]{1,0:T(8,128)S(1)}, f32[248,128]{1,0:T(8,128)S(1)}, f32[19,2,64,128]{3,2...) custom-call(f32[19,12,48,128]{3,2,1,0:T(8,128)S(1)} %copy-done, ...), custom_call_target="tpu_custom_call" | custom-call | tf_op jit(solution)/shard_map/faces/pallas_call | solution.py:652
  15.3 1.2 %collective-permute-start.4 = (f32[248,128]{1,0:T(8,128)S(1)}, f32[248,128]{1,0:T(8,128)S(1)}, u32[]{:S(2)}, u32[]{:S(2)}) collective-permute-start(f32[248,128]{1,0:T(8,128)S(1)} %get-tuple-element.26), channel_id=1, source_target_pairs={{0,4},{4,0},{8,12},{12,8},{1,5},{5,1},{9,13},{13,9},{2,6},{6,2},{1... | collective-permute-start | bytes 380936 | tf_op jit(solution)/shard_map/ppermute | solution.py:675
  16.5 1.5 %collective-permute-start.5 = (f32[248,128]{1,0:T(8,128)S(1)}, f32[248,128]{1,0:T(8,128)S(1)}, u32[]{:S(2)}, u32[]{:S(2)}) collective-permute-start(f32[248,128]{1,0:T(8,128)S(1)} %get-tuple-element.27), channel_id=1, source_target_pairs={{0,16},{4,8},{8,4},{12,28},{16,0},{20,24},{24,20},{28,12},{1,17},{... | collective-permute-start | bytes 380936 | tf_op jit(solution)/shard_map/ppermute | solution.py:676
  18.1 4.3 %inner.1 = (f32[19,12,48,128]{3,2,1,0:T(8,128)}, f32[19,2,64,128]{3,2,1,0:T(8,128)S(1)}) custom-call(f32[19,12,48,128]{3,2,1,0:T(8,128)S(1)} %copy-done, s32[12,48,128]{2,1,0:T(8,128)S(1)} %copy-done.1, f32[19,2,64,128]{3,2,1,0:T(8,128)S(1)} %get-tuple-element.22.faces.refs_2_, f32[2,5,16,128]{3,2,1,0:T(8,128)S(1)} %get-tuple-element.23.yh, ...), custom_call_target="tpu_custom_call" | custom-call | flops 20000000000 | bytes 12000000 | tf_op jit(solution)/shard_map/inner/pallas_call | solution.py:677
  22.4 0.0 collective-permute-done.4.refs_4_
  22.4 0.0 collective-permute-done.5.refs_5_
  22.4 1.1 %outer.1 = f32[19,12,48,128]{3,2,1,0:T(8,128)} custom-call(f32[19,12,48,128]{3,2,1,0:T(8,128)S(1)} %copy-done, s32[12,48,128]{2,1,0:T(8,128)S(1)} %copy-done.1, f32[19,2,64,128]{3,2,1,0:T(8,128)S(1)} %get-tuple-element.22.faces.refs_2_, f32[19,2,64,128]{3,2,1,0:T(8,128)S(1)} %get-tuple-element.25.refs_3_, ...), custom_call_target="tpu_custom_call", output_to_operand_aliasing={{}: (8, {})} | custom-call | tf_op jit(solution)/shard_map/outer/pallas_call | solution.py:691
  (1 shorter events, 0.0 us)
Async XLA Ops:
  0.6 12.9 %copy-start.1 = (s32[12,48,128]{2,1,0:T(8,128)S(1)}, s32[12,48,128]{2,1,0:T(8,128)}, u32[]{:S(2)}) copy-start(s32[12,48,128]{2,1,0:T(8,128)} %refs_1_.3) | copy-start | bytes 884740
  0.6 12.9 %copy-start.2 = (f32[3,4]{1,0:T(4,128)S(1)}, f32[3,4]{1,0:T(4,128)}, u32[]{:S(2)}) copy-start(f32[3,4]{1,0:T(4,128)} %refs_2_.1) | copy-start | bytes 148
  0.7 12.8 %copy-start = (f32[19,12,48,128]{3,2,1,0:T(8,128)S(1)}, f32[19,12,48,128]{3,2,1,0:T(8,128)}, u32[]{:S(2)}) copy-start(f32[19,12,48,128]{3,2,1,0:T(8,128)} %refs_0_.3) | copy-start | bytes 16809988
  1.9 6.3 %collective-permute-start = (f32[72,128]{1,0:T(8,128)S(1)}, f32[72,128]{1,0:T(8,128)S(1)}, u32[]{:S(2)}, u32[]{:S(2)}) collective-permute-start(f32[72,128]{1,0:T(8,128)S(1)} %get-tuple-element.17), channel_id=1, source_target_pairs={{0,4},{4,0},{8,12},{12,8},{1,5},{5,1},{9,13},{13,9},{2,6},{6,2},{1... | collective-permute-start | bytes 110600 | tf_op jit(solution)/shard_map/ppermute | solution.py:624
  5.0 4.0 %collective-permute-start.1 = (f32[72,128]{1,0:T(8,128)S(1)}, f32[72,128]{1,0:T(8,128)S(1)}, u32[]{:S(2)}, u32[]{:S(2)}) collective-permute-start(f32[72,128]{1,0:T(8,128)S(1)} %get-tuple-element.18), channel_id=1, source_target_pairs={{0,16},{4,8},{8,4},{12,28},{16,0},{20,24},{24,20},{28,12},{1,17},{... | collective-permute-start | bytes 110600 | tf_op jit(solution)/shard_map/ppermute | solution.py:625
  9.0 1.7 %collective-permute-start.2 = (f32[152,128]{1,0:T(8,128)S(1)}, f32[152,128]{1,0:T(8,128)S(1)}, u32[]{:S(2)}, u32[]{:S(2)}) collective-permute-start(f32[152,128]{1,0:T(8,128)S(1)} %get-tuple-element.20), channel_id=1, source_target_pairs={{0,1},{1,0},{2,3},{3,2},{4,5},{5,4},{6,7},{7,6},{8,9},{9,8},{10,11... | collective-permute-start | bytes 233480 | tf_op jit(solution)/shard_map/ppermute | solution.py:648
  9.0 4.5 %collective-permute-start.3 = (f32[152,128]{1,0:T(8,128)S(1)}, f32[152,128]{1,0:T(8,128)S(1)}, u32[]{:S(2)}, u32[]{:S(2)}) collective-permute-start(f32[152,128]{1,0:T(8,128)S(1)} %get-tuple-element.21), channel_id=1, source_target_pairs={{0,16},{1,2},{2,1},{3,19},{16,0},{17,18},{18,17},{19,3},{4,20},{5,... | collective-permute-start | bytes 233480 | tf_op jit(solution)/shard_map/ppermute | solution.py:649
  15.3 7.0 %collective-permute-start.4 = (f32[248,128]{1,0:T(8,128)S(1)}, f32[248,128]{1,0:T(8,128)S(1)}, u32[]{:S(2)}, u32[]{:S(2)}) collective-permute-start(f32[248,128]{1,0:T(8,128)S(1)} %get-tuple-element.26), channel_id=1, source_target_pairs={{0,4},{4,0},{8,12},{12,8},{1,5},{5,1},{9,13},{13,9},{2,6},{6,2},{1... | collective-permute-start | bytes 380936 | tf_op jit(solution)/shard_map/ppermute | solution.py:675
  16.5 5.8 %collective-permute-start.5 = (f32[248,128]{1,0:T(8,128)S(1)}, f32[248,128]{1,0:T(8,128)S(1)}, u32[]{:S(2)}, u32[]{:S(2)}) collective-permute-start(f32[248,128]{1,0:T(8,128)S(1)} %get-tuple-element.27), channel_id=1, source_target_pairs={{0,16},{4,8},{8,4},{12,28},{16,0},{20,24},{24,20},{28,12},{1,17},{... | collective-permute-start | bytes 380936 | tf_op jit(solution)/shard_map/ppermute | solution.py:676

commit v4 on v3

--- a/solution.py
+++ b/solution.py
@@ -32,6 +32,7 @@
 force_scale = 0.02
 inlet_speed = 0.05
 force_factor = 1.0 - 0.5 / relax_time
+PUSH = 6.0 * force_factor / 36.0
 
 leave_yp = [3, 7, 10, 15, 17]
 leave_ym = [4, 8, 9, 16, 18]
@@ -39,8 +40,8 @@
 leave_zm = [6, 12, 13, 16, 17]
 
 FACE = 10
-GROUPS = 7
-POT, SRC, COND, PH, MX, MY, MZ = range(GROUPS)
+GROUPS = 9
+POT, SRC, COND, MX, MY, MZ, AX, AY, AZ = range(GROUPS)
 RIM = 4
 CLOSED = -1e30
 OPEN_ABOVE = -1e29
@@ -50,6 +51,10 @@
 any_spec = pl.BlockSpec(memory_space=pl.ANY)
 hbm_spec = pl.BlockSpec(memory_space=pltpu.HBM)
 vmem_spec = pl.BlockSpec(memory_space=pltpu.VMEM)
+
+
+def pick(cond, a, b):
+    return jnp.where(cond, a, b)
 
 
 def moments(f):
@@ -64,20 +69,19 @@
     return rho, mx, my, mz
 
 
-def coefficients(rho, mom, force, fluid, inlet):
-    inv = 1.0 / rho
-    u = [(m + 0.5 * f) * inv for m, f in zip(mom, force)]
-    u = [jnp.where(inlet, c, v) for c, v in zip((0.0, 0.0, -inlet_speed), u)]
-    r = jnp.where(fluid, rho * (1.0 / (36.0 * relax_time)), 1.0 / 36.0)
-    f = [jnp.where(fluid, v * (force_factor / 36.0), 0.0) for v in force]
-    sq = u[0] * u[0] + u[1] * u[1] + u[2] * u[2]
-    uf = u[0] * f[0] + u[1] * f[1] + u[2] * f[2]
-    base = r * (1.0 - 1.5 * sq) - 3.0 * uf
-    ru = [r * v for v in u]
-    g = [4.5 * a + 9.0 * b for a, b in zip(ru, f)]
-    h = [3.0 * (a + b) for a, b in zip(ru, f)]
-    keep = jnp.where(fluid, 1.0 - 1.0 / relax_time, 0.0)
-    return keep, base, u, g, h
+def coefficients(rho, mom, half, push, fluid, inlet, shut):
+    inv = 1.5 / rho
+    still = inlet | shut
+    b = [pick(still, 0.0, (m + f) * inv) for m, f in zip(mom[:2], half[:2])]
+    b.append(pick(still, pick(inlet, -1.5 * inlet_speed, 0.0), (mom[2] + half[2]) * inv))
+    r = pick(fluid, rho * (1.0 / (36.0 * relax_time)), pick(shut, CLOSED, 1.0 / 36.0))
+    p = [pick(fluid, v, 0.0) for v in push]
+    r2 = r + r
+    h = [r2 * v + w for v, w in zip(b, p)]
+    e = [v + w for v, w in zip(h, p)]
+    base = r - (b[0] * e[0] + b[1] * e[1] + b[2] * e[2]) * (1.0 / 3.0)
+    keep = pick(fluid, 1.0 - 1.0 / relax_time, 0.0)
+    return keep, base, b, e, h
 
 
 def along(c, v):
@@ -93,12 +97,12 @@
 
 
 def post_pair(i, co):
-    keep, base, u, g, h = co
+    _, base, b, e, h = co
     c = lattice_dirs[i]
-    sym = base + along(c, u) * along(c, g)
+    sym = base + along(c, b) * along(c, e)
     anti = along(c, h)
     if sum(abs(s) for s in c) == 1:
-        return 2.0 * sym, 2.0 * anti
+        return sym + sym, anti + anti
     return sym, anti
 
 
@@ -111,16 +115,15 @@
     return keep * f + (sym - anti)
 
 
-def pick(cond, a, b):
-    return jnp.where(cond, a, b)
-
-
-def beyond_face(values, leave, force, there):
+def beyond_face(values, leave, half, there):
     flag = values[9]
-    co = coefficients(values[5], values[6:9], force, flag < 0.5, (flag > 1.5) & (flag < 2.5))
     shut = (flag > 0.5) & (flag < 1.5)
     shut = shut | jnp.logical_not(there)
-    return [(i, pick(shut, CLOSED, post_one(i, values[k], co))) for k, i in leave]
+    fluid = (flag < 0.5) & there
+    inlet = (flag > 1.5) & (flag < 2.5) & there
+    push = [v * PUSH for v in half]
+    co = coefficients(values[5], values[6:9], half, push, fluid, inlet, shut)
+    return [(i, post_one(i, values[k], co)) for k, i in leave]
 
 
 def lanes_to(x, shift):
@@ -130,14 +133,13 @@
 
 def y_sections(nz):
     found, at = [], FACE * nz
-    for rows in [RIM, RIM, 1, 1, 1, 1, 1] + [RIM] * 4:
+    for rows in [RIM] * 2 + [1] * (GROUPS - 2) + [RIM] * 4:
         found.append((at, rows))
         at += rows
     return found, at, at + -at % 8
 
 
 def pack_coarse(
-    flags,
     pot_hbm,
     cond_hbm,
     ph_hbm,
@@ -146,8 +148,6 @@
     o_c1,
     o_c2,
     o_g,
-    fbuf,
-    zsc,
     pot,
     cond,
     ph,
@@ -155,77 +155,64 @@
     tab,
     sems,
 ):
-    nz, ny = flags.shape[0], flags.shape[1]
     kz, ky, kx = pot.shape
     coarse = [
-        pltpu.make_async_copy(a, b, sems.at[2 + k])
+        pltpu.make_async_copy(a, b, sems.at[k])
         for k, (a, b) in enumerate(
             ((tab_hbm, tab), (ph_hbm, ph), (cond_hbm, cond), (pot_hbm, pot), (mag_hbm, mag))
         )
     ]
-    copies = [
-        pltpu.make_async_copy(flags.at[plane], fbuf.at[k], sems.at[k])
-        for k, plane in enumerate((0, nz - 1))
-    ]
-    for c in coarse + copies:
+    for c in coarse:
         c.start()
     for c in coarse:
         c.wait()
     phase = ph[...]
     conductivity = cond[...]
-    source = conductivity * jnp.where(
-        phase == 0, tab[0, 0], jnp.where(phase == 1, tab[1, 0], tab[2, 0])
-    )
-    fields = [pot[...], source, conductivity, phase.astype(jnp.float32), mag[0], mag[1], mag[2]]
+    column = [
+        pick(phase == 0, tab[0, k], pick(phase == 1, tab[1, k], tab[2, k])) for k in range(4)
+    ]
+    fields = [pot[...], conductivity * column[0], conductivity, mag[0], mag[1], mag[2]]
+    fields += column[1:]
     blank = jnp.zeros((ky, 128 - kz * kx), jnp.float32)
     for g, field in enumerate(fields):
         row = jnp.concatenate([field[l] for l in range(kz)] + [blank], axis=1)
         o_g[g, 0:ky, :] = row
         if g <= SRC:
-            for side in range(2):
-                zsc[side, ny + ky * g : ny + ky * g + ky, :] = row
-    for c in copies:
-        c.wait()
-    for side in range(2):
-        zsc[side, 0:ny, :] = fbuf[side].astype(jnp.float32)
-    up_z = 1 - lax.axis_index("wide") % 2
-    o_c1[...] = zsc[up_z]
-    o_c2[...] = zsc[1 - up_z]
-
-
-def pack_y_faces(pops, flags, after, o_y, ybuf, fybuf, sems):
+            o_c1[ky * g : ky * g + ky, :] = row
+            o_c2[ky * g : ky * g + ky, :] = row
+
+
+def pack_y_faces(pops, flags, after, o_y, ybuf, fbuf, sems):
     nz, ny = pops.shape[1], pops.shape[2]
     copies = []
-    for side, row in ((0, 0), (1, ny - 8)):
-        rows = pl.ds(row, 8)
-        copies.append(pltpu.make_async_copy(pops.at[:, :, rows, :], ybuf.at[side], sems.at[side]))
-        copies.append(pltpu.make_async_copy(flags.at[:, rows, :], fybuf.at[side], sems.at[2 + side]))
+    for side, row in ((0, 0), (1, ny - 1)):
+        copies.append(pltpu.make_async_copy(pops.at[:, :, row, :], ybuf.at[side], sems.at[side]))
+        copies.append(pltpu.make_async_copy(flags.at[:, row, :], fbuf.at[side], sems.at[2 + side]))
     for c in copies:
         c.start()
     for c in copies:
         c.wait()
-    for side, leave, row in ((0, leave_ym, 0), (1, leave_yp, 7)):
-        for z in range(nz):
-            f = [ybuf[side, i, z] for i in range(19)]
-            values = [f[i] for i in leave] + list(moments(f))
-            values.append(fybuf[side, z].astype(jnp.float32))
-            for k, v in enumerate(values):
-                o_y[side, k * nz + z : k * nz + z + 1, :] = v[row : row + 1]
-
-
-def coarse_blocks(ny, ky, low, high, own):
+    for side, leave in ((0, leave_ym), (1, leave_yp)):
+        f = [ybuf[side, i] for i in range(19)]
+        values = [f[i] for i in leave] + list(moments(f))
+        values.append(fbuf[side].astype(jnp.float32))
+        for k, v in enumerate(values):
+            o_y[side, k * nz : k * nz + nz, :] = v
+
+
+def coarse_blocks(ky, low, high, own):
     blocks = [own[g, 0:ky, :] for g in range(GROUPS)]
     for side in (low, high):
-        blocks += [side[ny + ky * g : ny + ky * g + ky] for g in (POT, SRC)]
+        blocks += [side[ky * g : ky * g + ky] for g in (POT, SRC)]
     return blocks
 
 
-def pack_rows(ny, ky, nz, zr1, zr2, own, fine, o_y1, o_y2, ysc):
+def pack_rows(ky, nz, zr1, zr2, own, fine, o_y1, o_y2, ysc):
     even = lax.axis_index("wide") % 2 == 0
     low = pick(even, zr2[...], zr1[...])
     high = pick(even, zr1[...], zr2[...])
     sections, used, total = y_sections(nz)
-    blocks = coarse_blocks(ny, ky, low, high, own)
+    blocks = coarse_blocks(ky, low, high, own)
     for side in range(2):
         ysc[side, 0 : FACE * nz, :] = fine[side]
         for (at, rows), v in zip(sections, blocks):
@@ -245,16 +232,18 @@
         out = slice(8 + 8 * b, 16 + 8 * b)
         f = [pops[i, z, rows, :] for i in range(19)]
         flag = flags[z, rows, :]
-        force = [fu[l, a, rows, :] for a in range(3)]
+        half = [fu[l, a, rows, :] for a in range(3)]
+        push = [fu[l, 3 + a, rows, :] for a in range(3)]
         rho, mom_x, mom_y, mom_z = moments(f)
-        wall = flag == 1
-        co = coefficients(rho, (mom_x, mom_y, mom_z), force, flag == 0, flag == 2)
+        co = coefficients(
+            rho, (mom_x, mom_y, mom_z), half, push, flag == 0, flag == 2, flag == 1
+        )
         keep = co[0]
-        post[0, to, out, :] = pick(wall, CLOSED, keep * f[0] + 12.0 * co[1])
+        post[0, to, out, :] = keep * f[0] + 12.0 * co[1]
         for i, j in pairs:
             sym, anti = post_pair(i, co)
-            post[i, to, out, :] = pick(wall, CLOSED, keep * f[i] + (sym + anti))
-            post[j, to, out, :] = pick(wall, CLOSED, keep * f[j] + (sym - anti))
+            post[i, to, out, :] = keep * f[i] + (sym + anti)
+            post[j, to, out, :] = keep * f[j] + (sym - anti)
 
 
 def pass_plane(z, pops, flags, here, source, put):
@@ -287,7 +276,6 @@
     N,
     pops,
     flags,
-    tab_hbm,
     yr1,
     yr2,
     zr1,
@@ -303,14 +291,10 @@
     ext,
     fc,
     zsc,
-    tab,
-    sem_tab,
 ):
     nz, ny, nx = flags.shape
     kz, ky, kx = o_pot.shape
     wi, ni = lax.axis_index("wide"), lax.axis_index("narrow")
-    tcopy = pltpu.make_async_copy(tab_hbm, tab, sem_tab)
-    tcopy.start()
     even_z = wi % 2 == 0
     even_y = ni % 2 == 0
     has_low_y, has_high_y = ni > 0, ni < N - 1
@@ -320,7 +304,7 @@
     y_lo = pick(even_y, yr2[...], yr1[...])
     y_hi = pick(even_y, yr1[...], yr2[...])
     sections = y_sections(nz)[0]
-    blocks = coarse_blocks(ny, ky, z_lo, z_hi, own)
+    blocks = coarse_blocks(ky, z_lo, z_hi, own)
     blank = jnp.zeros((RIM, 128), jnp.float32)
     for k, ((at, rows), v) in enumerate(zip(sections, blocks)):
         if rows < RIM:
@@ -386,18 +370,13 @@
     field = sweep(field, zero, zero)
     field = sweep(field, zero, zero)
 
-    tcopy.wait()
     v = field[1]
     grad = (
         (next_x(v) - prev_x(v)) * 0.5,
         (next_y(v) - prev_y(v)) * 0.5,
         (next_z(v, field[2]) - prev_z(v, field[0])) * 0.5,
     )
-    phase = ext[PH]
-    cur = []
-    for a in range(3):
-        applied = pick(phase < 0.5, tab[0, 1 + a], pick(phase < 1.5, tab[1, 1 + a], tab[2, 1 + a]))
-        cur.append(ext[COND] * (applied - grad[a]))
+    cur = [ext[COND] * (ext[AX + a] - grad[a]) for a in range(3)]
     lorentz = [
         cur[1] * ext[MZ] - cur[2] * ext[MY],
         cur[2] * ext[MX] - cur[0] * ext[MZ],
@@ -421,7 +400,7 @@
             preferred_element_type=jnp.float32,
         )
 
-    stack = jnp.concatenate([v * force_scale for v in lorentz], axis=0)
+    stack = jnp.concatenate([v * (0.5 * force_scale) for v in lorentz], axis=0)
     wide = [widened(stack, l) for l in range(kz)]
     sub = lax.broadcasted_iota(jnp.int32, (8, 128), 0)
     for l in range(kz):
@@ -432,7 +411,9 @@
             for b in range(ny // 8):
                 first = jnp.broadcast_to(fc[l, a, pl.ds(RIM + 2 * b, 1), :], (8, 128))
                 second = jnp.broadcast_to(fc[l, a, pl.ds(RIM + 2 * b + 1, 1), :], (8, 128))
-                fu[l, a, 8 * b : 8 * b + 8, :] = pick(sub < 4, first, second)
+                half = pick(sub < 4, first, second)
+                fu[l, a, 8 * b : 8 * b + 8, :] = half
+                fu[l, 3 + a, 8 * b : 8 * b + 8, :] = half * PUSH
 
     zrow = lax.broadcasted_iota(jnp.int32, (nz, 128), 0)
     for low, leave, frow, at, there in (
@@ -467,13 +448,22 @@
             row = 9 * nz + z
             zsc[side, at + 2 + y_side : at + 3 + y_side, :] = rows[row : row + 1]
         zsc[side, at + 4 : at + 8, :] = jnp.zeros((4, 128), jnp.float32)
+        zsc[side, at + 8 : at + 8 + ny, :] = flags[z].astype(jnp.float32)
     up_z = 1 - wi % 2
     o_f1[...] = zsc[up_z]
     o_f2[...] = zsc[1 - up_z]
 
 
-def inner_kernel(pops, flags, faces, yh, fu, o_pops, o_near, obuf, post, sem_out):
+def inner_kernel(
+    pops, flags, faces, yh, fu, pot, lor, o_pops, o_near, o_pot, o_lor, obuf, post, sem_out
+):
     nz, ny, nx = flags.shape
+    results = [
+        pltpu.make_async_copy(pot, o_pot, sem_out.at[0]),
+        pltpu.make_async_copy(lor, o_lor, sem_out.at[nz - 1]),
+    ]
+    for c in results:
+        c.start()
     for i in range(19):
         post[i, 0] = faces[i, 0]
         post[i, nz - 1] = faces[i, 1]
@@ -515,10 +505,12 @@
         return carry
 
     lax.fori_loop(1, nz - 1, drain, 0)
+    for c in results:
+        c.wait()
 
 
 def outer_kernel(
-    W, pops, flags, faces, near, fz1, fz2, zr1, zr2, half, o_pops, obuf, halo, sem_out
+    W, pops, flags, faces, near, fz1, fz2, half, o_pops, obuf, halo, sem_out
 ):
     nz, ny, nx = flags.shape
     wi = lax.axis_index("wide")
@@ -528,11 +520,10 @@
         (1, leave_zm, (17, 16), wi < W - 1),
     ):
         f_odd, f_even = (fz2, fz1) if side else (fz1, fz2)
-        c_odd, c_even = (zr2, zr1) if side else (zr1, zr2)
         gone = jnp.broadcast_to(jnp.logical_not(there), (8, 128))
         for b in range(ny // 8):
-            rows = slice(8 * b, 8 * b + 8)
-            flag = pick(even_z, c_even[rows, :], c_odd[rows, :])
+            at = slice(5 * ny + 8 + 8 * b, 5 * ny + 16 + 8 * b)
+            flag = pick(even_z, f_even[at, :], f_odd[at, :])
             shut = ((flag > 0.5) & (flag < 1.5)) | gone
             for k in range(5):
                 at = slice(ny * k + 8 * b, ny * k + 8 * b + 8)
@@ -590,37 +581,36 @@
         f32 = jnp.float32
         nz, ny, nx = flags.shape
         kz, ky, kx = potential.shape
-        zrows = ny + 2 * ky
         yrows = y_sections(nz)[2]
-        frows = 5 * ny + 8
+        frows = 6 * ny + 8
         params = pltpu.CompilerParams(vmem_limit_bytes=VMEM_LIMIT)
         shape = jax.ShapeDtypeStruct
 
         def in_hbm(*xs):
             return [pltpu.with_memory_space_constraint(x, pltpu.HBM) for x in xs]
 
+        pops_near = pltpu.with_memory_space_constraint(populations, pltpu.VMEM)
+        flags_near = pltpu.with_memory_space_constraint(flags, pltpu.VMEM)
         c1, c2, own = pl.pallas_call(
             pack_coarse,
             name="pack_coarse",
             out_shape=(
-                shape((zrows, nx), f32),
-                shape((zrows, nx), f32),
+                shape((2 * ky, nx), f32),
+                shape((2 * ky, nx), f32),
                 shape((GROUPS, 16, nx), f32),
             ),
-            in_specs=[hbm_spec] * 6,
+            in_specs=[hbm_spec] * 5,
             out_specs=[vmem_spec] * 3,
             scratch_shapes=[
-                pltpu.VMEM((2, ny, nx), jnp.int32),
-                pltpu.VMEM((2, zrows, nx), f32),
                 pltpu.VMEM(potential.shape, f32),
                 pltpu.VMEM(conductivity.shape, f32),
                 pltpu.VMEM(coil_phase.shape, jnp.int32),
                 pltpu.VMEM(magnetic.shape, f32),
                 pltpu.SMEM(phase_table.shape, f32),
-                pltpu.SemaphoreType.DMA((7,)),
+                pltpu.SemaphoreType.DMA((5,)),
             ],
             compiler_params=params,
-        )(*in_hbm(flags, potential, conductivity, coil_phase, magnetic, phase_table))
+        )(*in_hbm(potential, conductivity, coil_phase, magnetic, phase_table))
         zr1 = lax.ppermute(c1, "wide", pair_first(W))
         zr2 = lax.ppermute(c2, ("groups", "wide"), pair_second(W, G))
         fine = pl.pallas_call(
@@ -630,14 +620,14 @@
             in_specs=[hbm_spec] * 2 + [any_spec],
             out_specs=vmem_spec,
             scratch_shapes=[
-                pltpu.VMEM((2, 19, nz, 8, nx), f32),
-                pltpu.VMEM((2, nz, 8, nx), jnp.int32),
+                pltpu.VMEM((2, 19, nz, nx), f32),
+                pltpu.VMEM((2, nz, nx), jnp.int32),
                 pltpu.SemaphoreType.DMA((4,)),
             ],
             compiler_params=params,
         )(*in_hbm(populations, flags), own)
         y1, y2 = pl.pallas_call(
-            lambda *refs: pack_rows(ny, ky, nz, *refs),
+            lambda *refs: pack_rows(ky, nz, *refs),
             name="pack_rows",
             out_shape=(shape((yrows, nx), f32), shape((yrows, nx), f32)),
             in_specs=[vmem_spec] * 4,
@@ -647,9 +637,7 @@
         )(zr1, zr2, own, fine)
         yr1 = lax.ppermute(y1, "narrow", pair_first(N))
         yr2 = lax.ppermute(y2, ("groups", "narrow"), pair_second(N, G))
-        pops_near = pltpu.with_memory_space_constraint(populations, pltpu.VMEM)
-        flags_near = pltpu.with_memory_space_constraint(flags, pltpu.VMEM)
-        pot_out, lorentz, f1, f2, faces, yh, force = pl.pallas_call(
+        pot_out, lorentz, f1, f2, faces, yh, half = pl.pallas_call(
             lambda *refs: face_kernel(W, N, *refs),
             name="faces",
             out_shape=(
@@ -659,27 +647,33 @@
                 shape((frows, nx), f32),
                 shape((19, 2, ny + 16, nx), f32),
                 shape((2, 5, 16, nx), f32),
-                shape((kz, 3, ny, nx), f32),
+                shape((kz, 6, ny, nx), f32),
             ),
-            in_specs=[vmem_spec] * 2 + [any_spec] + [vmem_spec] * 5,
+            in_specs=[vmem_spec] * 7,
             out_specs=[vmem_spec] * 7,
             scratch_shapes=[
                 pltpu.VMEM((GROUPS + 4, 24, nx), f32),
                 pltpu.VMEM((kz, 3, 24, nx), f32),
                 pltpu.VMEM((2, frows, nx), f32),
-                pltpu.SMEM(phase_table.shape, f32),
-                pltpu.SemaphoreType.DMA,
             ],
             compiler_params=params,
-        )(pops_near, flags_near, phase_table, yr1, yr2, zr1, zr2, own)
+        )(pops_near, flags_near, yr1, yr2, zr1, zr2, own)
         fz1 = lax.ppermute(f1, "wide", pair_first(W))
         fz2 = lax.ppermute(f2, ("groups", "wide"), pair_second(W, G))
-        half, near = pl.pallas_call(
+        pot_near, lorentz_near = [
+            pltpu.with_memory_space_constraint(x, pltpu.VMEM) for x in (pot_out, lorentz)
+        ]
+        inside, near, pot_out, lorentz = pl.pallas_call(
             inner_kernel,
             name="inner",
-            out_shape=(shape(populations.shape, f32), shape((19, 2, ny + 16, nx), f32)),
-            in_specs=[vmem_spec] * 5,
-            out_specs=[hbm_spec, vmem_spec],
+            out_shape=(
+                shape(populations.shape, f32),
+                shape((19, 2, ny + 16, nx), f32),
+                shape(potential.shape, f32),
+                shape(magnetic.shape, f32),
+            ),
+            in_specs=[vmem_spec] * 7,
+            out_specs=[hbm_spec, vmem_spec, hbm_spec, hbm_spec],
             scratch_shapes=[
                 pltpu.VMEM(populations.shape, f32),
                 pltpu.VMEM((19, nz, ny + 16, nx), f32),
@@ -687,21 +681,21 @@
             ],
             compiler_params=params,
             cost_estimate=INNER_COST,
-        )(pops_near, flags_near, faces, yh, force)
+        )(pops_near, flags_near, faces, yh, half, pot_near, lorentz_near)
         passed = pl.pallas_call(
             lambda *refs: outer_kernel(W, *refs),
             name="outer",
             out_shape=shape(populations.shape, f32),
-            in_specs=[vmem_spec] * 8 + [hbm_spec],
+            in_specs=[vmem_spec] * 6 + [hbm_spec],
             out_specs=hbm_spec,
-            input_output_aliases={8: 0},
+            input_output_aliases={6: 0},
             scratch_shapes=[
                 pltpu.VMEM((19, 2, ny, nx), f32),
                 pltpu.VMEM((2, 5, ny + 16, nx), f32),
                 pltpu.SemaphoreType.DMA((2,)),
             ],
             compiler_params=params,
-        )(pops_near, flags_near, faces, near, fz1, fz2, zr1, zr2, half)
+        )(pops_near, flags_near, faces, near, fz1, fz2, inside)
         return passed, pot_out, lorentz
 
     in_specs = (

time: 23.7 us -> 22.3 us (0.941)
  Pallas kernels: 10.2 us -> 8.33 us
  waiting for transfers between devices: 3.63 us -> 4.16 us
    pallas_call x1, Pallas kernels: 1.84 us -> 1 us  [per_device(): pl.pallas_call(lambda *refs: face_kernel(W, N, *refs), name='faces', out_...]
    pallas_call x1, Pallas kernels: 1.67 us -> 1.08 us  [per_device(): pl.pallas_call(pack_y_faces, name='pack_y_faces', out_shape=shape((2, FAC...]
    pallas_call x1, Pallas kernels: 4.31 us -> 3.94 us  [per_device(): pl.pallas_call(inner_kernel, name='inner', out_shape=(shape(populations.s...]
    ppermute x1, waiting for transfers between devices: 0.75 us -> 1.08 us  [per_device(): zr2 = lax.ppermute(c2, ('groups', 'wide'), pair_second(W, G))]
  transfers between devices with their start and end apart: 6 -> 6, of which waited for: 2 -> 3; matrix products, arithmetic and copies ran while one was open for 0% -> 0% of each run, Pallas kernels for 25% -> 23%
where the time goes in v4:
time: 22.3 us; the launch traced here: 22.2 us
  starting transfers between devices  8.98 us (40%)
  Pallas kernels  8.33 us (37%)
  waiting for transfers between devices  4.16 us (19%)
  between operations  0.71 us (3%)
    pallas_call x1, Pallas kernels, per_device(): pl.pallas_call(inner_kernel, name='inner', out_shape=(shape(populations.s...  3.94 us
    ppermute x1, starting transfers between devices, per_device(): zr1 = lax.ppermute(c1, 'wide', pair_first(W))  3.09 us
    ppermute x1, waiting for transfers between devices, per_device(): yr2 = lax.ppermute(y2, ('groups', 'narrow'), pair_second(N, G))  2.87 us
    ppermute x1, starting transfers between devices, per_device(): yr2 = lax.ppermute(y2, ('groups', 'narrow'), pair_second(N, G))  1.58 us
    ppermute x1, starting transfers between devices, per_device(): zr2 = lax.ppermute(c2, ('groups', 'wide'), pair_second(W, G))  1.52 us
    ppermute x1, starting transfers between devices, per_device(): fz2 = lax.ppermute(f2, ('groups', 'wide'), pair_second(W, G))  1.52 us
    ppermute x1, starting transfers between devices, per_device(): fz1 = lax.ppermute(f1, 'wide', pair_first(W))  1.2 us
    pallas_call x1, Pallas kernels, per_device(): pl.pallas_call(pack_coarse, name='pack_coarse', out_shape=(shape((2 * ky,...  1.16 us
  transfers between devices with their start and end apart: 6, of which 3 were waited for; matrix products, arithmetic and copies ran while one was open for 0% of the time, Pallas kernels for 23%

profile of v4, /device:TPU:0, one launch (start us, length us, event | category | flops | bytes accessed | tf_op | source)
XLA Modules:
  0.0 22.2 jit_solution(9477206709318132804)
XLA Ops:
  0.6 0.0 copy-start.1
  0.6 0.0 copy-start
  0.7 1.2 %pack_coarse.1 = (f32[24,128]{1,0:T(8,128)S(1)}, f32[24,128]{1,0:T(8,128)S(1)}, f32[9,16,128]{2,1,0:T(8,128)S(1)}) custom-call(f32[3,12,32]{2,1,0:T(8,128)} %pot_hbm.1, f32[3,12,32]{2,1,0:T(8,128)} %cond_hbm.1, s32[3,12,32]{2,1,0:T(8,128)} %ph_hbm.1, f32[3,3,12,32]{3,2,1,0:T(8,128)} %mag_hbm.1, f32[3,4]{1,0:T(4,128)} %tab_hbm.1), custom_call_target="tpu_custom_call" | custom-call | tf_op jit(solution)/shard_map/pack_coarse/pallas_call | solution.py:594
  1.8 3.1 %collective-permute-start = (f32[24,128]{1,0:T(8,128)S(1)}, f32[24,128]{1,0:T(8,128)S(1)}, u32[]{:S(2)}, u32[]{:S(2)}) collective-permute-start(f32[24,128]{1,0:T(8,128)S(1)} %get-tuple-element.19), channel_id=1, source_target_pairs={{0,4},{4,0},{8,12},{12,8},{1,5},{5,1},{9,13},{13,9},{2,6},{6,2},{1... | collective-permute-start | bytes 36872 | tf_op jit(solution)/shard_map/ppermute | solution.py:614
  4.9 1.5 %collective-permute-start.1 = (f32[24,128]{1,0:T(8,128)S(1)}, f32[24,128]{1,0:T(8,128)S(1)}, u32[]{:S(2)}, u32[]{:S(2)}) collective-permute-start(f32[24,128]{1,0:T(8,128)S(1)} %get-tuple-element.20), channel_id=1, source_target_pairs={{0,16},{4,8},{8,4},{12,28},{16,0},{20,24},{24,20},{28,12},{1,17},{... | collective-permute-start | bytes 36872 | tf_op jit(solution)/shard_map/ppermute | solution.py:615
  6.4 1.1 %pack_y_faces.1.refs_3_ = f32[2,120,128]{2,1,0:T(8,128)S(1)} custom-call(f32[19,12,48,128]{3,2,1,0:T(8,128)} %refs_0_.3, s32[12,48,128]{2,1,0:T(8,128)} %refs_1_.3, f32[9,16,128]{2,1,0:T(8,128)S(1)} %get-tuple-element.21.after.refs_2_.refs_6_), custom_call_target="tpu_custom_call" | custom-call | tf_op jit(solution)/shard_map/pack_y_faces/pallas_call | solution.py:616
  7.5 0.0 collective-permute-done.refs_0_.refs_4_
  7.5 1.1 %collective-permute-done.1.refs_1_.refs_5_ = f32[24,128]{1,0:T(8,128)S(1)} collective-permute-done((f32[24,128]{1,0:T(8,128)S(1)}, f32[24,128]{1,0:T(8,128)S(1)}, u32[]{:S(2)}, u32[]{:S(2)}) %collective-permute-start.1) | collective-permute-done | bytes 12320 | tf_op jit(solution)/shard_map/ppermute | solution.py:615
  8.7 0.1 collective-permute-start.2
  8.7 1.6 %collective-permute-start.3 = (f32[152,128]{1,0:T(8,128)S(1)}, f32[152,128]{1,0:T(8,128)S(1)}, u32[]{:S(2)}, u32[]{:S(2)}) collective-permute-start(f32[152,128]{1,0:T(8,128)S(1)} %get-tuple-element.23), channel_id=1, source_target_pairs={{0,16},{1,2},{2,1},{3,19},{16,0},{17,18},{18,17},{19,3},{4,20},{5,... | collective-permute-start | bytes 233480 | tf_op jit(solution)/shard_map/ppermute | solution.py:639
  10.3 0.0 collective-permute-done.2.refs_2_
  10.3 2.9 %collective-permute-done.3.refs_3_ = f32[152,128]{1,0:T(8,128)S(1)} collective-permute-done((f32[152,128]{1,0:T(8,128)S(1)}, f32[152,128]{1,0:T(8,128)S(1)}, u32[]{:S(2)}, u32[]{:S(2)}) %collective-permute-start.3) | collective-permute-done | bytes 77856 | tf_op jit(solution)/shard_map/ppermute | solution.py:639
  13.2 0.0 copy-done.1
  13.2 0.0 copy-done
  13.2 1.0 %faces.1 = (f32[3,12,32]{2,1,0:T(8,128)S(1)}, f32[3,3,12,32]{3,2,1,0:T(8,128)S(1)}, f32[296,128]{1,0:T(8,128)S(1)}, f32[296,128]{1,0:T(8,128)S(1)}, f32[19,2,64,...) custom-call(f32[19,12,48,128]{3,2,1,0:T(8,128)S(1)} %copy-done, ...), custom_call_target="tpu_custom_call" | custom-call | tf_op jit(solution)/shard_map/faces/pallas_call | solution.py:640
  14.2 1.2 %collective-permute-start.4 = (f32[296,128]{1,0:T(8,128)S(1)}, f32[296,128]{1,0:T(8,128)S(1)}, u32[]{:S(2)}, u32[]{:S(2)}) collective-permute-start(f32[296,128]{1,0:T(8,128)S(1)} %get-tuple-element.30), channel_id=1, source_target_pairs={{0,4},{4,0},{8,12},{12,8},{1,5},{5,1},{9,13},{13,9},{2,6},{6,2},{1... | collective-permute-start | bytes 454664 | tf_op jit(solution)/shard_map/ppermute | solution.py:661
  15.4 1.5 %collective-permute-start.5 = (f32[296,128]{1,0:T(8,128)S(1)}, f32[296,128]{1,0:T(8,128)S(1)}, u32[]{:S(2)}, u32[]{:S(2)}) collective-permute-start(f32[296,128]{1,0:T(8,128)S(1)} %get-tuple-element.31), channel_id=1, source_target_pairs={{0,16},{4,8},{8,4},{12,28},{16,0},{20,24},{24,20},{28,12},{1,17},{... | collective-permute-start | bytes 454664 | tf_op jit(solution)/shard_map/ppermute | solution.py:662
  16.9 3.9 %inner.1 = (f32[19,12,48,128]{3,2,1,0:T(8,128)}, f32[19,2,64,128]{3,2,1,0:T(8,128)S(1)}, f32[3,12,32]{2,1,0:T(8,128)}, f32[3,3,12,32]{3,2,1,0:T(8,128)}) custom-call(f32[19,12,48,128]{3,2,1,0:T(8,128)S(1)} %copy-done, s32[12,48,128]{2,1,0:T(8,128)S(1)} %copy-done.1, f32[19,2,64,128]{3,2,1,0:T(8,128)S(1)} %get-tuple-element.24.faces.refs_2_, ...), custom_call_target="tpu_custom_call" | custom-call | flops 20000000000 | bytes 12000000 | tf_op jit(solution)/shard_map/inner/pallas_call | solution.py:666
  20.9 0.0 collective-permute-done.4.refs_4_
  20.9 0.2 collective-permute-done.5.refs_5_
  21.1 1.1 %outer.1 = f32[19,12,48,128]{3,2,1,0:T(8,128)} custom-call(f32[19,12,48,128]{3,2,1,0:T(8,128)S(1)} %copy-done, s32[12,48,128]{2,1,0:T(8,128)S(1)} %copy-done.1, f32[19,2,64,128]{3,2,1,0:T(8,128)S(1)} %get-tuple-element.24.faces.refs_2_, f32[19,2,64,128]{3,2,1,0:T(8,128)S(1)} %get-tuple-element.29.refs_3_, ...), custom_call_target="tpu_custom_call", output_to_operand_aliasing={{}: (6, {})} | custom-call | tf_op jit(solution)/shard_map/outer/pallas_call | solution.py:685
  (1 shorter events, 0.0 us)
Async XLA Ops:
  0.6 12.6 %copy-start.1 = (s32[12,48,128]{2,1,0:T(8,128)S(1)}, s32[12,48,128]{2,1,0:T(8,128)}, u32[]{:S(2)}) copy-start(s32[12,48,128]{2,1,0:T(8,128)} %refs_1_.3) | copy-start | bytes 884740
  0.6 12.6 %copy-start = (f32[19,12,48,128]{3,2,1,0:T(8,128)S(1)}, f32[19,12,48,128]{3,2,1,0:T(8,128)}, u32[]{:S(2)}) copy-start(f32[19,12,48,128]{3,2,1,0:T(8,128)} %refs_0_.3) | copy-start | bytes 16809988
  1.8 5.7 %collective-permute-start = (f32[24,128]{1,0:T(8,128)S(1)}, f32[24,128]{1,0:T(8,128)S(1)}, u32[]{:S(2)}, u32[]{:S(2)}) collective-permute-start(f32[24,128]{1,0:T(8,128)S(1)} %get-tuple-element.19), channel_id=1, source_target_pairs={{0,4},{4,0},{8,12},{12,8},{1,5},{5,1},{9,13},{13,9},{2,6},{6,2},{1... | collective-permute-start | bytes 36872 | tf_op jit(solution)/shard_map/ppermute | solution.py:614
  4.9 3.7 %collective-permute-start.1 = (f32[24,128]{1,0:T(8,128)S(1)}, f32[24,128]{1,0:T(8,128)S(1)}, u32[]{:S(2)}, u32[]{:S(2)}) collective-permute-start(f32[24,128]{1,0:T(8,128)S(1)} %get-tuple-element.20), channel_id=1, source_target_pairs={{0,16},{4,8},{8,4},{12,28},{16,0},{20,24},{24,20},{28,12},{1,17},{... | collective-permute-start | bytes 36872 | tf_op jit(solution)/shard_map/ppermute | solution.py:615
  8.7 1.7 %collective-permute-start.2 = (f32[152,128]{1,0:T(8,128)S(1)}, f32[152,128]{1,0:T(8,128)S(1)}, u32[]{:S(2)}, u32[]{:S(2)}) collective-permute-start(f32[152,128]{1,0:T(8,128)S(1)} %get-tuple-element.22), channel_id=1, source_target_pairs={{0,1},{1,0},{2,3},{3,2},{4,5},{5,4},{6,7},{7,6},{8,9},{9,8},{10,11... | collective-permute-start | bytes 233480 | tf_op jit(solution)/shard_map/ppermute | solution.py:638
  8.7 4.5 %collective-permute-start.3 = (f32[152,128]{1,0:T(8,128)S(1)}, f32[152,128]{1,0:T(8,128)S(1)}, u32[]{:S(2)}, u32[]{:S(2)}) collective-permute-start(f32[152,128]{1,0:T(8,128)S(1)} %get-tuple-element.23), channel_id=1, source_target_pairs={{0,16},{1,2},{2,1},{3,19},{16,0},{17,18},{18,17},{19,3},{4,20},{5,... | collective-permute-start | bytes 233480 | tf_op jit(solution)/shard_map/ppermute | solution.py:639
  14.2 6.7 %collective-permute-start.4 = (f32[296,128]{1,0:T(8,128)S(1)}, f32[296,128]{1,0:T(8,128)S(1)}, u32[]{:S(2)}, u32[]{:S(2)}) collective-permute-start(f32[296,128]{1,0:T(8,128)S(1)} %get-tuple-element.30), channel_id=1, source_target_pairs={{0,4},{4,0},{8,12},{12,8},{1,5},{5,1},{9,13},{13,9},{2,6},{6,2},{1... | collective-permute-start | bytes 454664 | tf_op jit(solution)/shard_map/ppermute | solution.py:661
  15.4 5.7 %collective-permute-start.5 = (f32[296,128]{1,0:T(8,128)S(1)}, f32[296,128]{1,0:T(8,128)S(1)}, u32[]{:S(2)}, u32[]{:S(2)}) collective-permute-start(f32[296,128]{1,0:T(8,128)S(1)} %get-tuple-element.31), channel_id=1, source_target_pairs={{0,16},{4,8},{8,4},{12,28},{16,0},{20,24},{24,20},{28,12},{1,17},{... | collective-permute-start | bytes 454664 | tf_op jit(solution)/shard_map/ppermute | solution.py:662

commit v5 on v4

--- a/solution.py
+++ b/solution.py
@@ -46,6 +46,7 @@
 CLOSED = -1e30
 OPEN_ABOVE = -1e29
 INNER_COST = pl.CostEstimate(flops=20000000000, bytes_accessed=12000000, transcendentals=0)
+TAIL = 2
 VMEM_LIMIT = 24 * 1024 * 1024
 
 any_spec = pl.BlockSpec(memory_space=pl.ANY)
@@ -69,8 +70,7 @@
     return rho, mx, my, mz
 
 
-def coefficients(rho, mom, half, push, fluid, inlet, shut):
-    inv = 1.5 / rho
+def coefficients(rho, inv, mom, half, push, fluid, inlet, shut):
     still = inlet | shut
     b = [pick(still, 0.0, (m + f) * inv) for m, f in zip(mom[:2], half[:2])]
     b.append(pick(still, pick(inlet, -1.5 * inlet_speed, 0.0), (mom[2] + half[2]) * inv))
@@ -122,7 +122,7 @@
     fluid = (flag < 0.5) & there
     inlet = (flag > 1.5) & (flag < 2.5) & there
     push = [v * PUSH for v in half]
-    co = coefficients(values[5], values[6:9], half, push, fluid, inlet, shut)
+    co = coefficients(values[5], 1.5 / values[5], values[6:9], half, push, fluid, inlet, shut)
     return [(i, post_one(i, values[k], co)) for k, i in leave]
 
 
@@ -140,6 +140,7 @@
 
 
 def pack_coarse(
+    flags,
     pot_hbm,
     cond_hbm,
     ph_hbm,
@@ -148,6 +149,7 @@
     o_c1,
     o_c2,
     o_g,
+    fbuf,
     pot,
     cond,
     ph,
@@ -162,7 +164,13 @@
             ((tab_hbm, tab), (ph_hbm, ph), (cond_hbm, cond), (pot_hbm, pot), (mag_hbm, mag))
         )
     ]
-    for c in coarse:
+    nz, ny = flags.shape[0], flags.shape[1]
+    up_z = 1 - lax.axis_index("wide") % 2
+    copies = [
+        pltpu.make_async_copy(flags.at[up_z * (nz - 1)], fbuf.at[0], sems.at[5]),
+        pltpu.make_async_copy(flags.at[(1 - up_z) * (nz - 1)], fbuf.at[1], sems.at[6]),
+    ]
+    for c in coarse + copies:
         c.start()
     for c in coarse:
         c.wait()
@@ -180,6 +188,9 @@
         if g <= SRC:
             o_c1[ky * g : ky * g + ky, :] = row
             o_c2[ky * g : ky * g + ky, :] = row
+    for k, (c, o) in enumerate(zip(copies, (o_c1, o_c2))):
+        c.wait()
+        o[2 * ky : 2 * ky + ny, :] = fbuf[k].astype(jnp.float32)
 
 
 def pack_y_faces(pops, flags, after, o_y, ybuf, fbuf, sems):
@@ -200,6 +211,20 @@
             o_y[side, k * nz : k * nz + nz, :] = v
 
 
+def sum_cells(pops, after, mom):
+    nz, ny = pops.shape[1], pops.shape[2]
+
+    def plane(z, carry):
+        for b in range(ny // 8):
+            rows = slice(8 * b, 8 * b + 8)
+            rho, *momenta = moments([pops[i, z, rows, :] for i in range(19)])
+            for k, v in enumerate([rho, 1.5 / rho] + momenta):
+                mom[k, z, rows, :] = v
+        return carry
+
+    lax.fori_loop(0, nz, plane, 0)
+
+
 def coarse_blocks(ky, low, high, own):
     blocks = [own[g, 0:ky, :] for g in range(GROUPS)]
     for side in (low, high):
@@ -224,7 +249,7 @@
     o_y2[...] = ysc[1 - up_y]
 
 
-def collide_plane(z, to, pops, flags, fu, post):
+def collide_plane(z, to, pops, flags, mom, fu, post):
     ny = flags.shape[1]
     l = z // 4
     for b in range(ny // 8):
@@ -234,10 +259,8 @@
         flag = flags[z, rows, :]
         half = [fu[l, a, rows, :] for a in range(3)]
         push = [fu[l, 3 + a, rows, :] for a in range(3)]
-        rho, mom_x, mom_y, mom_z = moments(f)
-        co = coefficients(
-            rho, (mom_x, mom_y, mom_z), half, push, flag == 0, flag == 2, flag == 1
-        )
+        rho, inv, *momenta = [mom[k, z, rows, :] for k in range(5)]
+        co = coefficients(rho, inv, momenta, half, push, flag == 0, flag == 2, flag == 1)
         keep = co[0]
         post[0, to, out, :] = keep * f[0] + 12.0 * co[1]
         for i, j in pairs:
@@ -246,7 +269,7 @@
             post[j, to, out, :] = keep * f[j] + (sym - anti)
 
 
-def pass_plane(z, pops, flags, here, source, put):
+def pass_plane(z, which, pops, flags, here, source, put):
     ny, nx = flags.shape[1:]
     lane8 = lax.broadcasted_iota(jnp.int32, (8, 128), 1)
     not_first = lane8 > 0
@@ -255,7 +278,7 @@
         rows = slice(8 * b, 8 * b + 8)
         out = slice(8 + 8 * b, 16 + 8 * b)
         wall = flags[z, rows, :] == 1
-        for i in range(19):
+        for i in which:
             cx, cy, cz = lattice_dirs[i]
             own = here(opposite_dir[i], out)
             if i > 0:
@@ -276,6 +299,7 @@
     N,
     pops,
     flags,
+    mom,
     yr1,
     yr2,
     zr1,
@@ -435,8 +459,8 @@
             for to, z in enumerate((0, nz - 1)):
                 post[i, to, at : at + 1, :] = v[z : z + 1]
 
-    collide_plane(0, 0, pops, flags, fu, post)
-    collide_plane(nz - 1, 1, pops, flags, fu, post)
+    collide_plane(0, 0, pops, flags, mom, fu, post)
+    collide_plane(nz - 1, 1, pops, flags, mom, fu, post)
     for side, leave, edges in ((0, leave_zm, (17, 16)), (1, leave_zp, (15, 18))):
         for k, i in enumerate(leave):
             zsc[side, ny * k : ny * k + ny, :] = post[i, side, 8 : 8 + ny, :]
@@ -448,82 +472,138 @@
             row = 9 * nz + z
             zsc[side, at + 2 + y_side : at + 3 + y_side, :] = rows[row : row + 1]
         zsc[side, at + 4 : at + 8, :] = jnp.zeros((4, 128), jnp.float32)
-        zsc[side, at + 8 : at + 8 + ny, :] = flags[z].astype(jnp.float32)
     up_z = 1 - wi % 2
     o_f1[...] = zsc[up_z]
     o_f2[...] = zsc[1 - up_z]
 
 
+def runs(which):
+    found = []
+    for i in which:
+        if found and found[-1][0] + found[-1][1] == i:
+            found[-1] = (found[-1][0], found[-1][1] + 1)
+        else:
+            found.append((i, 1))
+    return found
+
+
+staying_low = [i for i in range(19) if i not in leave_zp]
+staying_high = [i for i in range(19) if i not in leave_zm]
+
+
 def inner_kernel(
-    pops, flags, faces, yh, fu, pot, lor, o_pops, o_near, o_pot, o_lor, obuf, post, sem_out
+    pops,
+    flags,
+    mom,
+    faces,
+    yh,
+    fu,
+    pot,
+    lor,
+    o_pops,
+    o_tail,
+    o_pot,
+    o_lor,
+    obuf,
+    post,
+    sem_out,
+    sem_edge,
+    sem_coarse,
 ):
     nz, ny, nx = flags.shape
     results = [
-        pltpu.make_async_copy(pot, o_pot, sem_out.at[0]),
-        pltpu.make_async_copy(lor, o_lor, sem_out.at[nz - 1]),
+        pltpu.make_async_copy(pot, o_pot, sem_coarse.at[0]),
+        pltpu.make_async_copy(lor, o_lor, sem_coarse.at[1]),
     ]
     for c in results:
         c.start()
-    for i in range(19):
-        post[i, 0] = faces[i, 0]
-        post[i, nz - 1] = faces[i, 1]
     for side, leave, at in ((0, leave_yp, 7), (1, leave_ym, 8 + ny)):
         for k, i in enumerate(leave):
             rows = yh[side, k]
             for z in range(1, nz - 1):
                 post[i, z, at : at + 1, :] = rows[z : z + 1]
 
-    def passing(z):
+    def read(i, z, rows):
+        if isinstance(z, int) and z in (0, nz - 1):
+            return faces[i, 0 if z == 0 else 1, rows, :]
+        return post[i, z, rows, :]
+
+    def passing(z, which, into, at):
         def put(i, rows, v):
-            obuf[i, z, rows, :] = v
+            into[i, at, rows, :] = v
 
         pass_plane(
             z,
+            which,
             pops,
             flags,
-            lambda i, rows: post[i, z, rows, :],
-            lambda i, cz, rows: post[i, z - cz, rows, :],
+            lambda i, rows: read(i, z, rows),
+            lambda i, cz, rows: read(i, z - cz, rows),
             put,
         )
+
+    def edge(z, which, sem):
+        passing(z, which, obuf, z)
+        for k, (first, length) in enumerate(runs(which)):
+            part = pl.ds(first, length)
+            c = pltpu.make_async_copy(obuf.at[part, z], o_pops.at[part, z], sem_edge.at[sem, k])
+            c.start()
+            results.append(c)
+
+    def out(z):
+        passing(z, range(19), obuf, z)
         pltpu.make_async_copy(obuf.at[:, z], o_pops.at[:, z], sem_out.at[z]).start()
 
-    collide_plane(1, 1, pops, flags, fu, post)
+    collide_plane(1, 1, pops, flags, mom, fu, post)
+    edge(0, staying_low, 0)
+    collide_plane(nz - 2, nz - 2, pops, flags, mom, fu, post)
+    edge(nz - 1, staying_high, 1)
+    collide_plane(2, 2, pops, flags, mom, fu, post)
+    out(1)
+    last = nz - 1 - TAIL
 
     def plane(z, carry):
-        collide_plane(z + 1, z + 1, pops, flags, fu, post)
-        passing(z)
+        collide_plane(z + 1, z + 1, pops, flags, mom, fu, post)
+        out(z)
         return carry
 
-    lax.fori_loop(1, nz - 2, plane, 0)
-    passing(nz - 2)
-    for i in range(19):
-        o_near[i, 0] = post[i, 1]
-        o_near[i, 1] = post[i, nz - 2]
+    lax.fori_loop(2, last, plane, 0)
+    for z in range(last + 1, nz - 2):
+        collide_plane(z, z, pops, flags, mom, fu, post)
+    for k in range(TAIL):
+        passing(last + k, range(19), o_tail, k)
 
     def drain(z, carry):
         pltpu.make_async_copy(obuf.at[:, z], o_pops.at[:, z], sem_out.at[z]).wait()
         return carry
 
-    lax.fori_loop(1, nz - 1, drain, 0)
+    lax.fori_loop(1, last, drain, 0)
     for c in results:
         c.wait()
 
 
 def outer_kernel(
-    W, pops, flags, faces, near, fz1, fz2, half, o_pops, obuf, halo, sem_out
+    W, ky, pops, flags, faces, tail, fz1, fz2, zr1, zr2, half, o_pops, obuf, halo, sems, sem_tail
 ):
     nz, ny, nx = flags.shape
     wi = lax.axis_index("wide")
     even_z = wi % 2 == 0
+    copies = [
+        pltpu.make_async_copy(tail.at[:, k], o_pops.at[:, nz - 1 - TAIL + k], sem_tail.at[k])
+        for k in range(TAIL)
+    ]
+    for c in copies:
+        c.start()
     for side, leave, edges, there in (
         (0, leave_zp, (15, 18), wi > 0),
         (1, leave_zm, (17, 16), wi < W - 1),
     ):
         f_odd, f_even = (fz2, fz1) if side else (fz1, fz2)
+        c_odd, c_even = (zr2, zr1) if side else (zr1, zr2)
         gone = jnp.broadcast_to(jnp.logical_not(there), (8, 128))
         for b in range(ny // 8):
-            at = slice(5 * ny + 8 + 8 * b, 5 * ny + 16 + 8 * b)
-            flag = pick(even_z, f_even[at, :], f_odd[at, :])
+            at = slice(2 * ky + 8 * b, 2 * ky + 8 * b + 8)
+            flag = pick(even_z, c_even[at, :], c_odd[at, :])
             shut = ((flag > 0.5) & (flag < 1.5)) | gone
             for k in range(5):
                 at = slice(ny * k + 8 * b, ny * k + 8 * b + 8)
@@ -538,22 +618,22 @@
             k = leave.index(i)
             edge = pick(shut, CLOSED, v[y_side : y_side + 1])
             halo[side, k, yrow : yrow + 1, :] = edge
-    copies = []
     for side, z, leave in ((0, 0, leave_zp), (1, nz - 1, leave_zm)):
 
         def source(i, cz, rows, side=side, leave=leave):
-            if cz == 0:
-                return faces[i, side, rows, :]
-            if i in leave:
-                return halo[side, leave.index(i), rows, :]
-            return near[i, side, rows, :]
+            return halo[side, leave.index(i), rows, :]
 
         def put(i, rows, v, side=side):
-            obuf[i, side, rows, :] = v
-
-        pass_plane(z, pops, flags, lambda i, rows: faces[i, side, rows, :], source, put)
-        copies.append(pltpu.make_async_copy(obuf.at[:, side], o_pops.at[:, z], sem_out.at[side]))
-        copies[-1].start()
+            obuf[side, i, rows, :] = v
+
+        pass_plane(
+            z, leave, pops, flags, lambda i, rows: faces[i, side, rows, :], source, put
+        )
+        for k, (first, length) in enumerate(runs(leave)):
+            part = pl.ds(first, length)
+            c = pltpu.make_async_copy(obuf.at[side, part], o_pops.at[part, z], sems.at[side, k])
+            c.start()
+            copies.append(c)
     for c in copies:
         c.wait()
 
@@ -582,7 +662,7 @@
         nz, ny, nx = flags.shape
         kz, ky, kx = potential.shape
         yrows = y_sections(nz)[2]
-        frows = 6 * ny + 8
+        frows = 5 * ny + 8
         params = pltpu.CompilerParams(vmem_limit_bytes=VMEM_LIMIT)
         shape = jax.ShapeDtypeStruct
 
@@ -595,22 +675,23 @@
             pack_coarse,
             name="pack_coarse",
             out_shape=(
-                shape((2 * ky, nx), f32),
-                shape((2 * ky, nx), f32),
+                shape((2 * ky + ny, nx), f32),
+                shape((2 * ky + ny, nx), f32),
                 shape((GROUPS, 16, nx), f32),
             ),
-            in_specs=[hbm_spec] * 5,
+            in_specs=[hbm_spec] * 6,
             out_specs=[vmem_spec] * 3,
             scratch_shapes=[
+                pltpu.VMEM((2, ny, nx), jnp.int32),
                 pltpu.VMEM(potential.shape, f32),
                 pltpu.VMEM(conductivity.shape, f32),
                 pltpu.VMEM(coil_phase.shape, jnp.int32),
                 pltpu.VMEM(magnetic.shape, f32),
                 pltpu.SMEM(phase_table.shape, f32),
-                pltpu.SemaphoreType.DMA((5,)),
+                pltpu.SemaphoreType.DMA((7,)),
             ],
             compiler_params=params,
-        )(*in_hbm(potential, conductivity, coil_phase, magnetic, phase_table))
+        )(*in_hbm(flags, potential, conductivity, coil_phase, magnetic, phase_table))
         zr1 = lax.ppermute(c1, "wide", pair_first(W))
         zr2 = lax.ppermute(c2, ("groups", "wide"), pair_second(W, G))
         fine = pl.pallas_call(
@@ -637,6 +718,14 @@
         )(zr1, zr2, own, fine)
         yr1 = lax.ppermute(y1, "narrow", pair_first(N))
         yr2 = lax.ppermute(y2, ("groups", "narrow"), pair_second(N, G))
+        mom = pl.pallas_call(
+            sum_cells,
+            name="sum_cells",
+            out_shape=shape((5, nz, ny, nx), f32),
+            in_specs=[vmem_spec, any_spec],
+            out_specs=vmem_spec,
+            compiler_params=params,
+        )(pops_near, y1)
         pot_out, lorentz, f1, f2, faces, yh, half = pl.pallas_call(
             lambda *refs: face_kernel(W, N, *refs),
             name="faces",
@@ -649,7 +738,7 @@
                 shape((2, 5, 16, nx), f32),
                 shape((kz, 6, ny, nx), f32),
             ),
-            in_specs=[vmem_spec] * 7,
+            in_specs=[vmem_spec] * 8,
             out_specs=[vmem_spec] * 7,
             scratch_shapes=[
                 pltpu.VMEM((GROUPS + 4, 24, nx), f32),
@@ -657,45 +746,48 @@
                 pltpu.VMEM((2, frows, nx), f32),
             ],
             compiler_params=params,
-        )(pops_near, flags_near, yr1, yr2, zr1, zr2, own)
+        )(pops_near, flags_near, mom, yr1, yr2, zr1, zr2, own)
         fz1 = lax.ppermute(f1, "wide", pair_first(W))
         fz2 = lax.ppermute(f2, ("groups", "wide"), pair_second(W, G))
         pot_near, lorentz_near = [
             pltpu.with_memory_space_constraint(x, pltpu.VMEM) for x in (pot_out, lorentz)
         ]
-        inside, near, pot_out, lorentz = pl.pallas_call(
+        inside, tail, pot_out, lorentz = pl.pallas_call(
             inner_kernel,
             name="inner",
             out_shape=(
                 shape(populations.shape, f32),
-                shape((19, 2, ny + 16, nx), f32),
+                shape((19, TAIL, ny, nx), f32),
                 shape(potential.shape, f32),
                 shape(magnetic.shape, f32),
             ),
-            in_specs=[vmem_spec] * 7,
+            in_specs=[vmem_spec] * 8,
             out_specs=[hbm_spec, vmem_spec, hbm_spec, hbm_spec],
             scratch_shapes=[
                 pltpu.VMEM(populations.shape, f32),
                 pltpu.VMEM((19, nz, ny + 16, nx), f32),
                 pltpu.SemaphoreType.DMA((nz,)),
+                pltpu.SemaphoreType.DMA((2, 4)),
+                pltpu.SemaphoreType.DMA((2,)),
             ],
             compiler_params=params,
             cost_estimate=INNER_COST,
-        )(pops_near, flags_near, faces, yh, half, pot_near, lorentz_near)
+        )(pops_near, flags_near, mom, faces, yh, half, pot_near, lorentz_near)
         passed = pl.pallas_call(
-            lambda *refs: outer_kernel(W, *refs),
+            lambda *refs: outer_kernel(W, ky, *refs),
             name="outer",
             out_shape=shape(populations.shape, f32),
-            in_specs=[vmem_spec] * 6 + [hbm_spec],
+            in_specs=[vmem_spec] * 8 + [hbm_spec],
             out_specs=hbm_spec,
-            input_output_aliases={6: 0},
+            input_output_aliases={8: 0},
             scratch_shapes=[
-                pltpu.VMEM((19, 2, ny, nx), f32),
+                pltpu.VMEM((2, 19, ny, nx), f32),
                 pltpu.VMEM((2, 5, ny + 16, nx), f32),
-                pltpu.SemaphoreType.DMA((2,)),
+                pltpu.SemaphoreType.DMA((2, 4)),
+                pltpu.SemaphoreType.DMA((TAIL,)),
             ],
             compiler_params=params,
-        )(pops_near, flags_near, faces, near, fz1, fz2, inside)
+        )(pops_near, flags_near, faces, tail, fz1, fz2, zr1, zr2, inside)
         return passed, pot_out, lorentz
 
     in_specs = (

time: 22.3 us -> 21.8 us (0.978)
  waiting for transfers between devices: 4.16 us -> 3.55 us
    ppermute x1, waiting for transfers between devices: 2.87 us -> 2.24 us  [per_device(): yr2 = lax.ppermute(y2, ('groups', 'narrow'), pair_second(N, G))]
    pallas_call x2 -> x3, Pallas kernels: 2.28 us -> 2.84 us  [the longest x1 1.19 us: per_device(): pl.pallas_call(pack_coarse, name='pack_coarse', out_shape=(shape((2 * ky...]
    pallas_call x1, Pallas kernels: 3.94 us -> 3.43 us  [per_device(): pl.pallas_call(inner_kernel, name='inner', out_shape=(shape(populations.s...]
  transfers between devices with their start and end apart: 6 -> 6, of which waited for: 3 -> 2; matrix products, arithmetic and copies ran while one was open for 0% -> 0% of each run, Pallas kernels for 23% -> 24%
where the time goes in v5:
time: 21.8 us; the launch traced here: 21.6 us
  starting transfers between devices  8.99 us (41%)
  Pallas kernels  8.39 us (38%)
  waiting for transfers between devices  3.55 us (16%)
  between operations  0.71 us (3%)
    pallas_call x1, Pallas kernels, per_device(): pl.pallas_call(inner_kernel, name='inner', out_shape=(shape(populations.s...  3.43 us
    ppermute x1, starting transfers between devices, per_device(): zr1 = lax.ppermute(c1, 'wide', pair_first(W))  3.09 us
    ppermute x1, waiting for transfers between devices, per_device(): yr2 = lax.ppermute(y2, ('groups', 'narrow'), pair_second(N, G))  2.24 us
    ppermute x1, starting transfers between devices, per_device(): yr2 = lax.ppermute(y2, ('groups', 'narrow'), pair_second(N, G))  1.58 us
    ppermute x1, starting transfers between devices, per_device(): zr2 = lax.ppermute(c2, ('groups', 'wide'), pair_second(W, G))  1.52 us
    ppermute x1, starting transfers between devices, per_device(): fz2 = lax.ppermute(f2, ('groups', 'wide'), pair_second(W, G))  1.52 us
    ppermute x1, waiting for transfers between devices, per_device(): zr2 = lax.ppermute(c2, ('groups', 'wide'), pair_second(W, G))  1.29 us
    pallas_call x1, Pallas kernels, per_device(): pl.pallas_call(pack_coarse, name='pack_coarse', out_shape=(shape((2 * ky...  1.19 us
  transfers between devices with their start and end apart: 6, of which 2 were waited for; matrix products, arithmetic and copies ran while one was open for 0% of the time, Pallas kernels for 24%

profile of v5, /device:TPU:0, one launch (start us, length us, event | category | flops | bytes accessed | tf_op | source)
XLA Modules:
  0.0 21.6 jit_solution(2787170228460048284)
XLA Ops:
  0.6 0.0 copy-start
  0.6 1.2 %pack_coarse.1 = (f32[72,128]{1,0:T(8,128)S(1)}, f32[72,128]{1,0:T(8,128)S(1)}, f32[9,16,128]{2,1,0:T(8,128)S(1)}) custom-call(s32[12,48,128]{2,1,0:T(8,128)} %refs_1_.3, f32[3,12,32]{2,1,0:T(8,128)} %pot_hbm.1, f32[3,12,32]{2,1,0:T(8,128)} %cond_hbm.1, s32[3,12,32]{2,1,0:T(8,128)} %ph_hbm.1, f32[3,3,12,32]{3,2,1,0:T(8,128)} %mag_hbm.1, f32[3,4]{1,0:T(4,128)} %tab_hbm.1), custom_call_target="tpu_custom_call" | custom-call | tf_op jit(solution)/shard_map/pack_coarse/pallas_call | solution.py:674
  1.8 3.1 %collective-permute-start = (f32[72,128]{1,0:T(8,128)S(1)}, f32[72,128]{1,0:T(8,128)S(1)}, u32[]{:S(2)}, u32[]{:S(2)}) collective-permute-start(f32[72,128]{1,0:T(8,128)S(1)} %get-tuple-element.19), channel_id=1, source_target_pairs={{0,4},{4,0},{8,12},{12,8},{1,5},{5,1},{9,13},{13,9},{2,6},{6,2},{1... | collective-permute-start | bytes 110600 | tf_op jit(solution)/shard_map/ppermute | solution.py:695
  4.9 1.5 %collective-permute-start.1 = (f32[72,128]{1,0:T(8,128)S(1)}, f32[72,128]{1,0:T(8,128)S(1)}, u32[]{:S(2)}, u32[]{:S(2)}) collective-permute-start(f32[72,128]{1,0:T(8,128)S(1)} %get-tuple-element.20), channel_id=1, source_target_pairs={{0,16},{4,8},{8,4},{12,28},{16,0},{20,24},{24,20},{28,12},{1,17},{... | collective-permute-start | bytes 110600 | tf_op jit(solution)/shard_map/ppermute | solution.py:696
  6.5 0.0 copy-start.1
  6.5 1.1 %pack_y_faces.1.refs_3_ = f32[2,120,128]{2,1,0:T(8,128)S(1)} custom-call(f32[19,12,48,128]{3,2,1,0:T(8,128)} %refs_0_.3, s32[12,48,128]{2,1,0:T(8,128)} %refs_1_.3, f32[9,16,128]{2,1,0:T(8,128)S(1)} %get-tuple-element.21.after.refs_2_.refs_7_), custom_call_target="tpu_custom_call" | custom-call | tf_op jit(solution)/shard_map/pack_y_faces/pallas_call | solution.py:697
  7.6 0.0 collective-permute-done.refs_0_.refs_5_.refs_6_
  7.6 1.3 %collective-permute-done.1.refs_1_.refs_6_.refs_7_ = f32[72,128]{1,0:T(8,128)S(1)} collective-permute-done((f32[72,128]{1,0:T(8,128)S(1)}, f32[72,128]{1,0:T(8,128)S(1)}, u32[]{:S(2)}, u32[]{:S(2)}) %collective-permute-start.1) | collective-permute-done | bytes 36896 | tf_op jit(solution)/shard_map/ppermute | solution.py:696
  8.9 1.6 %collective-permute-start.3 = (f32[152,128]{1,0:T(8,128)S(1)}, f32[152,128]{1,0:T(8,128)S(1)}, u32[]{:S(2)}, u32[]{:S(2)}) collective-permute-start(f32[152,128]{1,0:T(8,128)S(1)} %get-tuple-element.23), channel_id=1, source_target_pairs={{0,16},{1,2},{2,1},{3,19},{16,0},{17,18},{18,17},{19,3},{4,20},{5,... | collective-permute-start | bytes 233480 | tf_op jit(solution)/shard_map/ppermute | solution.py:720
  10.5 0.1 collective-permute-start.2
  10.6 0.0 copy-done
  10.6 0.5 %sum_cells.1.refs_2_.mom = f32[5,12,48,128]{3,2,1,0:T(8,128)S(1)} custom-call(f32[19,12,48,128]{3,2,1,0:T(8,128)S(1)} %copy-done, f32[152,128]{1,0:T(8,128)S(1)} %get-tuple-element.22.after), custom_call_target="tpu_custom_call" | custom-call | tf_op jit(solution)/shard_map/sum_cells/pallas_call | solution.py:721
  11.1 2.2 %collective-permute-done.3.refs_4_ = f32[152,128]{1,0:T(8,128)S(1)} collective-permute-done((f32[152,128]{1,0:T(8,128)S(1)}, f32[152,128]{1,0:T(8,128)S(1)}, u32[]{:S(2)}, u32[]{:S(2)}) %collective-permute-start.3) | collective-permute-done | bytes 77856 | tf_op jit(solution)/shard_map/ppermute | solution.py:720
  13.4 0.0 collective-permute-done.2.refs_3_
  13.4 0.0 copy-done.1
  13.4 1.0 %faces.1 = (f32[3,12,32]{2,1,0:T(8,128)S(1)}, f32[3,3,12,32]{3,2,1,0:T(8,128)S(1)}, f32[248,128]{1,0:T(8,128)S(1)}, f32[248,128]{1,0:T(8,128)S(1)}, f32[19,2,64,...) custom-call(f32[19,12,48,128]{3,2,1,0:T(8,128)S(1)} %copy-done, ...), custom_call_target="tpu_custom_call" | custom-call | tf_op jit(solution)/shard_map/faces/pallas_call | solution.py:729
  14.4 1.2 %collective-permute-start.4 = (f32[248,128]{1,0:T(8,128)S(1)}, f32[248,128]{1,0:T(8,128)S(1)}, u32[]{:S(2)}, u32[]{:S(2)}) collective-permute-start(f32[248,128]{1,0:T(8,128)S(1)} %get-tuple-element.30), channel_id=1, source_target_pairs={{0,4},{4,0},{8,12},{12,8},{1,5},{5,1},{9,13},{13,9},{2,6},{6,2},{1... | collective-permute-start | bytes 380936 | tf_op jit(solution)/shard_map/ppermute | solution.py:750
  15.5 1.5 %collective-permute-start.5 = (f32[248,128]{1,0:T(8,128)S(1)}, f32[248,128]{1,0:T(8,128)S(1)}, u32[]{:S(2)}, u32[]{:S(2)}) collective-permute-start(f32[248,128]{1,0:T(8,128)S(1)} %get-tuple-element.31), channel_id=1, source_target_pairs={{0,16},{4,8},{8,4},{12,28},{16,0},{20,24},{24,20},{28,12},{1,17},{... | collective-permute-start | bytes 380936 | tf_op jit(solution)/shard_map/ppermute | solution.py:751
  17.1 3.4 %inner.1 = (f32[19,12,48,128]{3,2,1,0:T(8,128)}, f32[19,2,48,128]{3,2,1,0:T(8,128)S(1)}, f32[3,12,32]{2,1,0:T(8,128)}, f32[3,3,12,32]{3,2,1,0:T(8,128)}) custom-call(f32[19,12,48,128]{3,2,1,0:T(8,128)S(1)} %copy-done, s32[12,48,128]{2,1,0:T(8,128)S(1)} %copy-done.1, f32[5,12,48,128]{3,2,1,0:T(8,128)S(1)} %sum_cells.1.refs_2_.mom, ...), custom_call_target="tpu_custom_call" | custom-call | flops 20000000000 | bytes 12000000 | tf_op jit(solution)/shard_map/inner/pallas_call | solution.py:755
  20.5 0.0 collective-permute-done.4.refs_4_
  20.5 0.0 collective-permute-done.5.refs_5_
  20.5 1.1 %outer.1 = f32[19,12,48,128]{3,2,1,0:T(8,128)} custom-call(f32[19,12,48,128]{3,2,1,0:T(8,128)S(1)} %copy-done, s32[12,48,128]{2,1,0:T(8,128)S(1)} %copy-done.1, f32[19,2,64,128]{3,2,1,0:T(8,128)S(1)} %get-tuple-element.24.faces.refs_2_, f32[19,2,48,128]{3,2,1,0:T(8,128)S(1)} %get-tuple-element.29.refs_3_, ...), custom_call_target="tpu_custom_call", output_to_operand_aliasing={{}: (8, {})} | custom-call | tf_op jit(solution)/shard_map/outer/pallas_call | solution.py:776
  (1 shorter events, 0.0 us)
Async XLA Ops:
  0.6 10.0 %copy-start = (f32[19,12,48,128]{3,2,1,0:T(8,128)S(1)}, f32[19,12,48,128]{3,2,1,0:T(8,128)}, u32[]{:S(2)}) copy-start(f32[19,12,48,128]{3,2,1,0:T(8,128)} %refs_0_.3) | copy-start | bytes 16809988
  1.8 5.7 %collective-permute-start = (f32[72,128]{1,0:T(8,128)S(1)}, f32[72,128]{1,0:T(8,128)S(1)}, u32[]{:S(2)}, u32[]{:S(2)}) collective-permute-start(f32[72,128]{1,0:T(8,128)S(1)} %get-tuple-element.19), channel_id=1, source_target_pairs={{0,4},{4,0},{8,12},{12,8},{1,5},{5,1},{9,13},{13,9},{2,6},{6,2},{1... | collective-permute-start | bytes 110600 | tf_op jit(solution)/shard_map/ppermute | solution.py:695
  4.9 4.0 %collective-permute-start.1 = (f32[72,128]{1,0:T(8,128)S(1)}, f32[72,128]{1,0:T(8,128)S(1)}, u32[]{:S(2)}, u32[]{:S(2)}) collective-permute-start(f32[72,128]{1,0:T(8,128)S(1)} %get-tuple-element.20), channel_id=1, source_target_pairs={{0,16},{4,8},{8,4},{12,28},{16,0},{20,24},{24,20},{28,12},{1,17},{... | collective-permute-start | bytes 110600 | tf_op jit(solution)/shard_map/ppermute | solution.py:696
  6.5 6.9 %copy-start.1 = (s32[12,48,128]{2,1,0:T(8,128)S(1)}, s32[12,48,128]{2,1,0:T(8,128)}, u32[]{:S(2)}) copy-start(s32[12,48,128]{2,1,0:T(8,128)} %refs_1_.3) | copy-start | bytes 884740
  8.9 4.5 %collective-permute-start.3 = (f32[152,128]{1,0:T(8,128)S(1)}, f32[152,128]{1,0:T(8,128)S(1)}, u32[]{:S(2)}, u32[]{:S(2)}) collective-permute-start(f32[152,128]{1,0:T(8,128)S(1)} %get-tuple-element.23), channel_id=1, source_target_pairs={{0,16},{1,2},{2,1},{3,19},{16,0},{17,18},{18,17},{19,3},{4,20},{5,... | collective-permute-start | bytes 233480 | tf_op jit(solution)/shard_map/ppermute | solution.py:720
  10.5 2.9 %collective-permute-start.2 = (f32[152,128]{1,0:T(8,128)S(1)}, f32[152,128]{1,0:T(8,128)S(1)}, u32[]{:S(2)}, u32[]{:S(2)}) collective-permute-start(f32[152,128]{1,0:T(8,128)S(1)} %get-tuple-element.22.after), channel_id=1, source_target_pairs={{0,1},{1,0},{2,3},{3,2},{4,5},{5,4},{6,7},{7,6},{8,9},{9,8},{10,11... | collective-permute-start | bytes 233480 | tf_op jit(solution)/shard_map/ppermute | solution.py:719
  14.4 6.2 %collective-permute-start.4 = (f32[248,128]{1,0:T(8,128)S(1)}, f32[248,128]{1,0:T(8,128)S(1)}, u32[]{:S(2)}, u32[]{:S(2)}) collective-permute-start(f32[248,128]{1,0:T(8,128)S(1)} %get-tuple-element.30), channel_id=1, source_target_pairs={{0,4},{4,0},{8,12},{12,8},{1,5},{5,1},{9,13},{13,9},{2,6},{6,2},{1... | collective-permute-start | bytes 380936 | tf_op jit(solution)/shard_map/ppermute | solution.py:750
  15.5 5.0 %collective-permute-start.5 = (f32[248,128]{1,0:T(8,128)S(1)}, f32[248,128]{1,0:T(8,128)S(1)}, u32[]{:S(2)}, u32[]{:S(2)}) collective-permute-start(f32[248,128]{1,0:T(8,128)S(1)} %get-tuple-element.31), channel_id=1, source_target_pairs={{0,16},{4,8},{8,4},{12,28},{16,0},{20,24},{24,20},{28,12},{1,17},{... | collective-permute-start | bytes 380936 | tf_op jit(solution)/shard_map/ppermute | solution.py:751

commit v6 on v5

--- a/solution.py
+++ b/solution.py
@@ -642,15 +642,18 @@
     return [(i, i ^ 1) for i in range(size)]
 
 
-def pair_second(size, groups):
+def pair_second(size, other, major):
+    def at(i, k):
+        return k * size + i if major else i * other + k
+
     found = []
-    for g in range(groups):
+    for k in range(other):
         for i in range(size):
             j = i + 1 if i % 2 else i - 1
             if 0 <= j < size:
-                found.append((g * size + i, g * size + j))
-            elif g ^ 1 < groups:
-                found.append((g * size + i, (g ^ 1) * size + i))
+                found.append((at(i, k), at(j, k)))
+            elif k ^ 1 < other:
+                found.append((at(i, k), at(i, k ^ 1)))
     return found
 
 
@@ -693,7 +696,7 @@
             compiler_params=params,
         )(*in_hbm(flags, potential, conductivity, coil_phase, magnetic, phase_table))
         zr1 = lax.ppermute(c1, "wide", pair_first(W))
-        zr2 = lax.ppermute(c2, ("groups", "wide"), pair_second(W, G))
+        zr2 = lax.ppermute(c2, ("wide", "narrow"), pair_second(W, N, False))
         fine = pl.pallas_call(
             pack_y_faces,
             name="pack_y_faces",
@@ -717,7 +720,7 @@
             compiler_params=params,
         )(zr1, zr2, own, fine)
         yr1 = lax.ppermute(y1, "narrow", pair_first(N))
-        yr2 = lax.ppermute(y2, ("groups", "narrow"), pair_second(N, G))
+        yr2 = lax.ppermute(y2, ("groups", "narrow"), pair_second(N, G, True))
         mom = pl.pallas_call(
             sum_cells,
             name="sum_cells",
@@ -748,7 +751,7 @@
             compiler_params=params,
         )(pops_near, flags_near, mom, yr1, yr2, zr1, zr2, own)
         fz1 = lax.ppermute(f1, "wide", pair_first(W))
-        fz2 = lax.ppermute(f2, ("groups", "wide"), pair_second(W, G))
+        fz2 = lax.ppermute(f2, ("wide", "narrow"), pair_second(W, N, False))
         pot_near, lorentz_near = [
             pltpu.with_memory_space_constraint(x, pltpu.VMEM) for x in (pot_out, lorentz)
         ]

time: 21.8 us -> 20.3 us (0.931)
  waiting for transfers between devices: 3.55 us -> 2.61 us
  starting transfers between devices: 8.99 us -> 8.41 us
    ppermute x3, starting transfers between devices: 4.62 us -> 2.03 us  [the longest x1 2.03 us: per_device(): yr2 = lax.ppermute(y2, ('groups', 'narrow'), pair_second(N, G, True))]
    ppermute x1, starting transfers between devices: 1.19 us -> 3.2 us  [per_device(): fz1 = lax.ppermute(f1, 'wide', pair_first(W))]
    ppermute x3, waiting for transfers between devices: 3.54 us -> 1.8 us  [the longest x1 1.8 us: per_device(): yr2 = lax.ppermute(y2, ('groups', 'narrow'), pair_second(N, G, True))]
    ppermute x1, waiting for transfers between devices: 0.01 us -> 0.8 us  [per_device(): zr1 = lax.ppermute(c1, 'wide', pair_first(W))]
  transfers between devices with their start and end apart: 6 -> 6, of which waited for: 2 -> 2; matrix products, arithmetic and copies ran while one was open for 0% -> 0% of each run, Pallas kernels for 24% -> 25%
where the time goes in v6:
time: 20.3 us; the launch traced here: 20.1 us
  starting transfers between devices  8.41 us (41%)
  Pallas kernels  8.39 us (41%)
  waiting for transfers between devices  2.61 us (13%)
  between operations  0.7 us (3%)
    pallas_call x1, Pallas kernels, per_device(): pl.pallas_call(inner_kernel, name='inner', out_shape=(shape(populations.s...  3.43 us
    ppermute x1, starting transfers between devices, per_device(): fz1 = lax.ppermute(f1, 'wide', pair_first(W))  3.2 us
    ppermute x1, starting transfers between devices, per_device(): zr1 = lax.ppermute(c1, 'wide', pair_first(W))  3.09 us
    ppermute x1, starting transfers between devices, per_device(): yr2 = lax.ppermute(y2, ('groups', 'narrow'), pair_second(N, G, True))  2.03 us
    ppermute x1, waiting for transfers between devices, per_device(): yr2 = lax.ppermute(y2, ('groups', 'narrow'), pair_second(N, G, True))  1.8 us
    pallas_call x1, Pallas kernels, per_device(): pl.pallas_call(pack_coarse, name='pack_coarse', out_shape=(shape((2 * ky...  1.19 us
    pallas_call x1, Pallas kernels, per_device(): pl.pallas_call(pack_y_faces, name='pack_y_faces', out_shape=shape((2, FAC...  1.12 us
    pallas_call x1, Pallas kernels, per_device(): pl.pallas_call(lambda *refs: outer_kernel(W, ky, *refs), name='outer', ou...  1.12 us
  transfers between devices with their start and end apart: 6, of which 2 were waited for; matrix products, arithmetic and copies ran while one was open for 0% of the time, Pallas kernels for 25%

profile of v6, /device:TPU:0, one launch (start us, length us, event | category | flops | bytes accessed | tf_op | source)
XLA Modules:
  0.0 20.1 jit_solution(10192628973294055149)
XLA Ops:
  0.6 0.0 copy-start
  0.6 1.2 %pack_coarse.1 = (f32[72,128]{1,0:T(8,128)S(1)}, f32[72,128]{1,0:T(8,128)S(1)}, f32[9,16,128]{2,1,0:T(8,128)S(1)}) custom-call(s32[12,48,128]{2,1,0:T(8,128)} %refs_1_.3, f32[3,12,32]{2,1,0:T(8,128)} %pot_hbm.1, f32[3,12,32]{2,1,0:T(8,128)} %cond_hbm.1, s32[3,12,32]{2,1,0:T(8,128)} %ph_hbm.1, f32[3,3,12,32]{3,2,1,0:T(8,128)} %mag_hbm.1, f32[3,4]{1,0:T(4,128)} %tab_hbm.1), custom_call_target="tpu_custom_call" | custom-call | tf_op jit(solution)/shard_map/pack_coarse/pallas_call | solution.py:677
  1.8 3.1 %collective-permute-start = (f32[72,128]{1,0:T(8,128)S(1)}, f32[72,128]{1,0:T(8,128)S(1)}, u32[]{:S(2)}, u32[]{:S(2)}) collective-permute-start(f32[72,128]{1,0:T(8,128)S(1)} %get-tuple-element.19), channel_id=1, source_target_pairs={{0,4},{4,0},{8,12},{12,8},{1,5},{5,1},{9,13},{13,9},{2,6},{6,2},{1... | collective-permute-start | bytes 110600 | tf_op jit(solution)/shard_map/ppermute | solution.py:698
  4.9 0.0 collective-permute-start.1
  4.9 0.0 copy-start.1
  4.9 1.1 %pack_y_faces.1.refs_3_ = f32[2,120,128]{2,1,0:T(8,128)S(1)} custom-call(f32[19,12,48,128]{3,2,1,0:T(8,128)} %refs_0_.3, s32[12,48,128]{2,1,0:T(8,128)} %refs_1_.3, f32[9,16,128]{2,1,0:T(8,128)S(1)} %get-tuple-element.21.after.refs_2_.refs_7_), custom_call_target="tpu_custom_call" | custom-call | tf_op jit(solution)/shard_map/pack_y_faces/pallas_call | solution.py:700
  6.1 0.8 %collective-permute-done.refs_0_.refs_5_.refs_6_ = f32[72,128]{1,0:T(8,128)S(1)} collective-permute-done((f32[72,128]{1,0:T(8,128)S(1)}, f32[72,128]{1,0:T(8,128)S(1)}, u32[]{:S(2)}, u32[]{:S(2)}) %collective-permute-start) | collective-permute-done | bytes 36896 | tf_op jit(solution)/shard_map/ppermute | solution.py:698
  6.9 0.0 collective-permute-done.1.refs_1_.refs_6_.refs_7_
  6.9 2.0 %collective-permute-start.3 = (f32[152,128]{1,0:T(8,128)S(1)}, f32[152,128]{1,0:T(8,128)S(1)}, u32[]{:S(2)}, u32[]{:S(2)}) collective-permute-start(f32[152,128]{1,0:T(8,128)S(1)} %get-tuple-element.23), channel_id=1, source_target_pairs={{0,16},{1,2},{2,1},{3,19},{16,0},{17,18},{18,17},{19,3},{4,20},{5,... | collective-permute-start | bytes 233480 | tf_op jit(solution)/shard_map/ppermute | solution.py:723
  8.9 0.1 collective-permute-start.2
  9.0 0.0 copy-done
  9.0 0.5 %sum_cells.1.refs_2_.mom = f32[5,12,48,128]{3,2,1,0:T(8,128)S(1)} custom-call(f32[19,12,48,128]{3,2,1,0:T(8,128)S(1)} %copy-done, f32[152,128]{1,0:T(8,128)S(1)} %get-tuple-element.22.after), custom_call_target="tpu_custom_call" | custom-call | tf_op jit(solution)/shard_map/sum_cells/pallas_call | solution.py:724
  9.6 1.8 %collective-permute-done.3.refs_4_ = f32[152,128]{1,0:T(8,128)S(1)} collective-permute-done((f32[152,128]{1,0:T(8,128)S(1)}, f32[152,128]{1,0:T(8,128)S(1)}, u32[]{:S(2)}, u32[]{:S(2)}) %collective-permute-start.3) | collective-permute-done | bytes 77856 | tf_op jit(solution)/shard_map/ppermute | solution.py:723
  11.4 0.0 collective-permute-done.2.refs_3_
  11.4 0.0 copy-done.1
  11.4 1.0 %faces.1 = (f32[3,12,32]{2,1,0:T(8,128)S(1)}, f32[3,3,12,32]{3,2,1,0:T(8,128)S(1)}, f32[248,128]{1,0:T(8,128)S(1)}, f32[248,128]{1,0:T(8,128)S(1)}, f32[19,2,64,...) custom-call(f32[19,12,48,128]{3,2,1,0:T(8,128)S(1)} %copy-done, ...), custom_call_target="tpu_custom_call" | custom-call | tf_op jit(solution)/shard_map/faces/pallas_call | solution.py:732
  12.3 3.2 %collective-permute-start.4 = (f32[248,128]{1,0:T(8,128)S(1)}, f32[248,128]{1,0:T(8,128)S(1)}, u32[]{:S(2)}, u32[]{:S(2)}) collective-permute-start(f32[248,128]{1,0:T(8,128)S(1)} %get-tuple-element.30), channel_id=1, source_target_pairs={{0,4},{4,0},{8,12},{12,8},{1,5},{5,1},{9,13},{13,9},{2,6},{6,2},{1... | collective-permute-start | bytes 380936 | tf_op jit(solution)/shard_map/ppermute | solution.py:753
  15.5 0.0 collective-permute-start.5
  15.5 3.4 %inner.1 = (f32[19,12,48,128]{3,2,1,0:T(8,128)}, f32[19,2,48,128]{3,2,1,0:T(8,128)S(1)}, f32[3,12,32]{2,1,0:T(8,128)}, f32[3,3,12,32]{3,2,1,0:T(8,128)}) custom-call(f32[19,12,48,128]{3,2,1,0:T(8,128)S(1)} %copy-done, s32[12,48,128]{2,1,0:T(8,128)S(1)} %copy-done.1, f32[5,12,48,128]{3,2,1,0:T(8,128)S(1)} %sum_cells.1.refs_2_.mom, ...), custom_call_target="tpu_custom_call" | custom-call | flops 20000000000 | bytes 12000000 | tf_op jit(solution)/shard_map/inner/pallas_call | solution.py:758
  19.0 0.0 collective-permute-done.4.refs_4_
  19.0 0.0 collective-permute-done.5.refs_5_
  19.0 1.1 %outer.1 = f32[19,12,48,128]{3,2,1,0:T(8,128)} custom-call(f32[19,12,48,128]{3,2,1,0:T(8,128)S(1)} %copy-done, s32[12,48,128]{2,1,0:T(8,128)S(1)} %copy-done.1, f32[19,2,64,128]{3,2,1,0:T(8,128)S(1)} %get-tuple-element.24.faces.refs_2_, f32[19,2,48,128]{3,2,1,0:T(8,128)S(1)} %get-tuple-element.29.refs_3_, ...), custom_call_target="tpu_custom_call", output_to_operand_aliasing={{}: (8, {})} | custom-call | tf_op jit(solution)/shard_map/outer/pallas_call | solution.py:779
  (1 shorter events, 0.0 us)
Async XLA Ops:
  0.6 8.4 %copy-start = (f32[19,12,48,128]{3,2,1,0:T(8,128)S(1)}, f32[19,12,48,128]{3,2,1,0:T(8,128)}, u32[]{:S(2)}) copy-start(f32[19,12,48,128]{3,2,1,0:T(8,128)} %refs_0_.3) | copy-start | bytes 16809988
  1.8 5.0 %collective-permute-start = (f32[72,128]{1,0:T(8,128)S(1)}, f32[72,128]{1,0:T(8,128)S(1)}, u32[]{:S(2)}, u32[]{:S(2)}) collective-permute-start(f32[72,128]{1,0:T(8,128)S(1)} %get-tuple-element.19), channel_id=1, source_target_pairs={{0,4},{4,0},{8,12},{12,8},{1,5},{5,1},{9,13},{13,9},{2,6},{6,2},{1... | collective-permute-start | bytes 110600 | tf_op jit(solution)/shard_map/ppermute | solution.py:698
  4.9 1.9 %collective-permute-start.1 = (f32[72,128]{1,0:T(8,128)S(1)}, f32[72,128]{1,0:T(8,128)S(1)}, u32[]{:S(2)}, u32[]{:S(2)}) collective-permute-start(f32[72,128]{1,0:T(8,128)S(1)} %get-tuple-element.20), channel_id=1, source_target_pairs={{0,1},{4,8},{8,4},{12,13},{1,0},{5,9},{9,5},{13,12},{2,3},{6,10},{... | collective-permute-start | bytes 110600 | tf_op jit(solution)/shard_map/ppermute | solution.py:699
  4.9 6.4 %copy-start.1 = (s32[12,48,128]{2,1,0:T(8,128)S(1)}, s32[12,48,128]{2,1,0:T(8,128)}, u32[]{:S(2)}) copy-start(s32[12,48,128]{2,1,0:T(8,128)} %refs_1_.3) | copy-start | bytes 884740
  6.9 4.5 %collective-permute-start.3 = (f32[152,128]{1,0:T(8,128)S(1)}, f32[152,128]{1,0:T(8,128)S(1)}, u32[]{:S(2)}, u32[]{:S(2)}) collective-permute-start(f32[152,128]{1,0:T(8,128)S(1)} %get-tuple-element.23), channel_id=1, source_target_pairs={{0,16},{1,2},{2,1},{3,19},{16,0},{17,18},{18,17},{19,3},{4,20},{5,... | collective-permute-start | bytes 233480 | tf_op jit(solution)/shard_map/ppermute | solution.py:723
  8.9 2.4 %collective-permute-start.2 = (f32[152,128]{1,0:T(8,128)S(1)}, f32[152,128]{1,0:T(8,128)S(1)}, u32[]{:S(2)}, u32[]{:S(2)}) collective-permute-start(f32[152,128]{1,0:T(8,128)S(1)} %get-tuple-element.22.after), channel_id=1, source_target_pairs={{0,1},{1,0},{2,3},{3,2},{4,5},{5,4},{6,7},{7,6},{8,9},{9,8},{10,11... | collective-permute-start | bytes 233480 | tf_op jit(solution)/shard_map/ppermute | solution.py:722
  12.3 6.6 %collective-permute-start.4 = (f32[248,128]{1,0:T(8,128)S(1)}, f32[248,128]{1,0:T(8,128)S(1)}, u32[]{:S(2)}, u32[]{:S(2)}) collective-permute-start(f32[248,128]{1,0:T(8,128)S(1)} %get-tuple-element.30), channel_id=1, source_target_pairs={{0,4},{4,0},{8,12},{12,8},{1,5},{5,1},{9,13},{13,9},{2,6},{6,2},{1... | collective-permute-start | bytes 380936 | tf_op jit(solution)/shard_map/ppermute | solution.py:753
  15.5 3.5 %collective-permute-start.5 = (f32[248,128]{1,0:T(8,128)S(1)}, f32[248,128]{1,0:T(8,128)S(1)}, u32[]{:S(2)}, u32[]{:S(2)}) collective-permute-start(f32[248,128]{1,0:T(8,128)S(1)} %get-tuple-element.31), channel_id=1, source_target_pairs={{0,1},{4,8},{8,4},{12,13},{1,0},{5,9},{9,5},{13,12},{2,3},{6,10},{... | collective-permute-start | bytes 380936 | tf_op jit(solution)/shard_map/ppermute | solution.py:754
